TPU v7x, 256 devices: a whole 4x4x8 slice. The times are simulated.
256 devices in a mesh: blk: 64 (over x, z_lo, y), rep: 4 (over z_hi, core).
Axes of the slice: x: 4, y: 4, z: 8 (z_hi: 2, z_lo: 4; z = z_hi * 4 + z_lo), core: 2. Of those that a mesh axis runs over, the one named last changes fastest.
Arguments:
- node_feats: float32 [32768, 256], P('blk'), may hold values from -6 to 6
- operator_tiles: float32 [256, 16, 128, 128], P('blk', 'rep'), may hold values from -0.125 to 0.125
- tile_cols: int32 [256, 16], P('blk', 'rep'), may hold values from 0 to 255, as said below
- weight: float32 [256, 256], replicated, may hold values from -0.375 to 0.375
- layer_bias: float32 [256], replicated, may hold values from -3 to 3
- cotangent: float32 [32768, 256], P(('blk', 'rep')), may hold values from -6 to 6
Outputs:
- layer_out: float32 [32768, 256], P(('blk', 'rep'))
- grad_feats: float32 [32768, 256], P(('blk', 'rep'))
- grad_weight: float32 [256, 256], replicated
- grad_bias: float32 [256], replicated
Inputs may be any that keep to these rules, and one draw needn't show every extreme that they name: `tile_cols`: owner of block j is j // 4, among 64 owners on a closed cycle. Slots r * 4 to (r + 1) * 4 - 1 of row block i name blocks whose owner lies at cycle distance (owner of i minus owner of the column, modulo the number of owners) from r * 16 to (r + 1) * 16 - 1. Slot 0 of row block i names block i itself. Entries may repeat within a row block.
All inputs are finite; a program needn't handle non-finite values.
Results may differ from a plain program's by a relative error of at most 0.0003.
Values sent between devices are 32-bit elements; how exact they have to be, the bound alone decides.
No kernel may reach another device: no remote copies, remote signals or barrier semaphores. Data moves between devices by JAX's collectives and lax.ppermute only.
A program may use at most 64 MiB of HBM per device.

v0:
```python
import math

import jax
import jax.numpy as jnp
from jax import lax
from jax.sharding import PartitionSpec as P

TOP_PRECISION = lax.Precision.HIGHEST


def shifted_2(value, axis, steps):
    count = lax.axis_size(axis)
    pairs = [(source, (source + steps) % count) for source in range(count)]
    return lax.ppermute(value, axis, pairs)


def body(node_feats, operator_tiles, tile_cols, weight, layer_bias, cotangent):
    cycle_size = lax.axis_size("blk")
    rep_size = lax.axis_size("rep")
    window = cycle_size // rep_size
    position = lax.axis_index("blk")
    replica = lax.axis_index("rep")
    offset = replica * window
    blocks, slot_count, tile_size, _ = operator_tiles.shape
    width = node_feats.shape[1]
    row_count = blocks * tile_size
    owners = tile_cols // blocks
    within = tile_cols % blocks
    distance = jnp.mod(position - owners, cycle_size) - offset
    columns = jnp.arange(blocks, dtype=jnp.int32)
    sections = jnp.arange(window, dtype=jnp.int32)
    chosen = (
        (distance[:, :, None, None] == sections[None, None, :, None])
        & (within[:, :, None, None] == columns[None, None, None, :])
    ).astype(jnp.float32)

    def reshape_to_blocks(rows):
        return rows.reshape(blocks, tile_size, width)

    def store(stacked, section_no, current):
        return lax.dynamic_update_index_in_dim(stacked, reshape_to_blocks(current), section_no, 0)

    aligned = node_feats
    for bit_pos in range(rep_size.bit_length() - 1):
        shifted = shifted_2(aligned, "blk", window << bit_pos)
        aligned = jnp.where((replica >> bit_pos) % 2 == 1, shifted, aligned)
    empty = jnp.zeros((window, blocks, tile_size, width), jnp.float32)

    def advance(section_no, loop_state):
        current, stacked = loop_state
        current = shifted_2(current, "blk", 1)
        return (current, store(stacked, section_no, current))

    _, received = lax.fori_loop(1, window, advance, (aligned, store(empty, 0, aligned)))
    selected_tiles = jnp.einsum("iksc,scbd->ikbd", chosen, received, precision=TOP_PRECISION)
    partial_aggregate = jnp.einsum(
        "uzrj,uzje->ure", operator_tiles, selected_tiles, precision=TOP_PRECISION
    ).reshape(row_count, width)
    aggregated = lax.psum_scatter(partial_aggregate, "rep", scatter_dimension=0, tiled=True)
    pre_act = jnp.dot(aggregated, weight, precision=TOP_PRECISION) + layer_bias
    negative = jnp.minimum(pre_act, 0.0)
    layer_out = jnp.where(pre_act > 0, pre_act, jnp.expm1(negative))
    grad_pre = cotangent * jnp.where(pre_act > 0, 1.0, jnp.exp(negative))
    grad_scale = 1.0 / math.sqrt(row_count * cycle_size)
    grad_weight = (
        jnp.einsum("rd,re->de", aggregated, grad_pre, precision=TOP_PRECISION) * grad_scale
    )
    grad_bias = jnp.sum(grad_pre, axis=0) * grad_scale
    grad_weight, grad_bias = lax.psum((grad_weight, grad_bias), ("blk", "rep"))
    grad_hidden = jnp.einsum("re,de->rd", grad_pre, weight, precision=TOP_PRECISION)
    hidden_gradient = lax.all_gather(grad_hidden, "rep", axis=0, tiled=True)
    slot_terms = jnp.einsum(
        "xszt,xzc->xstc",
        operator_tiles,
        reshape_to_blocks(hidden_gradient),
        precision=TOP_PRECISION,
    )
    sorted_terms = jnp.einsum("iksc,ikbd->scbd", chosen, slot_terms, precision=TOP_PRECISION)

    def adjoint_term(section_no):
        return lax.dynamic_index_in_dim(sorted_terms, section_no, 0, keepdims=False).reshape(
            row_count, width
        )

    def retreat(counter, running):
        moved = shifted_2(running, "blk", -1)
        return moved + adjoint_term(window - 1 - counter)

    adjoint = lax.fori_loop(1, window, retreat, adjoint_term(window - 1))
    for bit_pos in range(rep_size.bit_length() - 1):
        returned = shifted_2(adjoint, "blk", -(window << bit_pos))
        adjoint = jnp.where((replica >> bit_pos) % 2 == 1, returned, adjoint)
    grad_feats = lax.psum_scatter(adjoint, "rep", scatter_dimension=0, tiled=True)
    return (layer_out, grad_feats, grad_weight, grad_bias)


def solution(mesh):
    return jax.shard_map(
        body,
        mesh=mesh,
        in_specs=(
            P("blk", None),
            P("blk", "rep", None, None),
            P("blk", "rep"),
            P(),
            P(),
            P(("blk", "rep"), None),
        ),
        out_specs=(P(("blk", "rep"), None), P(("blk", "rep"), None), P(), P()),
        check_vma=False,
    )
```

profile of v0, /device:TPU:1, one launch (start us, length us, event | category | flops | bytes accessed | tf_op | source)
XLA Modules:
  0.0 966.0 jit_solution(15077650085938543299)
XLA Ops:
  9.3 10.8 %collective-permute-done.2 = f32[512,256]{1,0:T(8,128)S(1)} collective-permute-done((f32[512,256]{1,0:T(8,128)}, f32[512,256]{1,0:T(8,128)S(1)}, u32[]{:S(2)}, u32[]{:S(2)}) %collective-permute-start.2) | collective-permute-done | bytes 524320 | tf_op jit(solution)/shard_map/ppermute | solution.py:14
  24.8 7.8 collective-permute-done.3
  37.0 259.1 %while.30 = (s32[]{:T(128)}, f32[512,256]{1,0:T(8,128)S(1)}, f32[16,4,128,256]{3,2,1,0:T(8,128)}, s32[]{:T(128)}, s32[]{:T(128)}, /*index=5*/s32[]{:T(128)}) while((s32[]{:T(128)}, f32[512,256]{1,0:T(8,128)S(1)}, f32[16,4,128,256]{3,2,1,0:T(8,128)}, s32[]{:T(128)}, s32[]{:T(128)}, /*index=5*/s32[]{:T(128)}) %tuple.67), condition=%wide.region_1.2_spmd, body=%wide.region_0.1_spmd.sunk | while | flops 5 | bytes 4194459 | solution.py:54
  40.4 15.2 %collective-permute-done = f32[512,256]{1,0:T(8,128)S(1)} collective-permute-done((f32[512,256]{1,0:T(8,128)S(1)}, f32[512,256]{1,0:T(8,128)S(1)}, u32[]{:S(2)}, u32[]{:S(2)}) %collective-permute-start) | collective-permute-done | bytes 524320 | tf_op jit(solution)/shard_map/while/body/eval_jaxpr/ppermute | solution.py:14
  56.6 15.3 %collective-permute-done = f32[512,256]{1,0:T(8,128)S(1)} collective-permute-done((f32[512,256]{1,0:T(8,128)S(1)}, f32[512,256]{1,0:T(8,128)S(1)}, u32[]{:S(2)}, u32[]{:S(2)}) %collective-permute-start) | collective-permute-done | bytes 524320 | tf_op jit(solution)/shard_map/while/body/eval_jaxpr/ppermute | solution.py:14
  72.9 14.3 %collective-permute-done = f32[512,256]{1,0:T(8,128)S(1)} collective-permute-done((f32[512,256]{1,0:T(8,128)S(1)}, f32[512,256]{1,0:T(8,128)S(1)}, u32[]{:S(2)}, u32[]{:S(2)}) %collective-permute-start) | collective-permute-done | bytes 524320 | tf_op jit(solution)/shard_map/while/body/eval_jaxpr/ppermute | solution.py:14
  88.2 14.0 %collective-permute-done = f32[512,256]{1,0:T(8,128)S(1)} collective-permute-done((f32[512,256]{1,0:T(8,128)S(1)}, f32[512,256]{1,0:T(8,128)S(1)}, u32[]{:S(2)}, u32[]{:S(2)}) %collective-permute-start) | collective-permute-done | bytes 524320 | tf_op jit(solution)/shard_map/while/body/eval_jaxpr/ppermute | solution.py:14
  103.2 14.0 %collective-permute-done = f32[512,256]{1,0:T(8,128)S(1)} collective-permute-done((f32[512,256]{1,0:T(8,128)S(1)}, f32[512,256]{1,0:T(8,128)S(1)}, u32[]{:S(2)}, u32[]{:S(2)}) %collective-permute-start) | collective-permute-done | bytes 524320 | tf_op jit(solution)/shard_map/while/body/eval_jaxpr/ppermute | solution.py:14
  118.3 14.0 %collective-permute-done = f32[512,256]{1,0:T(8,128)S(1)} collective-permute-done((f32[512,256]{1,0:T(8,128)S(1)}, f32[512,256]{1,0:T(8,128)S(1)}, u32[]{:S(2)}, u32[]{:S(2)}) %collective-permute-start) | collective-permute-done | bytes 524320 | tf_op jit(solution)/shard_map/while/body/eval_jaxpr/ppermute | solution.py:14
  133.3 14.0 %collective-permute-done = f32[512,256]{1,0:T(8,128)S(1)} collective-permute-done((f32[512,256]{1,0:T(8,128)S(1)}, f32[512,256]{1,0:T(8,128)S(1)}, u32[]{:S(2)}, u32[]{:S(2)}) %collective-permute-start) | collective-permute-done | bytes 524320 | tf_op jit(solution)/shard_map/while/body/eval_jaxpr/ppermute | solution.py:14
  148.3 14.5 %collective-permute-done = f32[512,256]{1,0:T(8,128)S(1)} collective-permute-done((f32[512,256]{1,0:T(8,128)S(1)}, f32[512,256]{1,0:T(8,128)S(1)}, u32[]{:S(2)}, u32[]{:S(2)}) %collective-permute-start) | collective-permute-done | bytes 524320 | tf_op jit(solution)/shard_map/while/body/eval_jaxpr/ppermute | solution.py:14
  163.8 15.6 %collective-permute-done = f32[512,256]{1,0:T(8,128)S(1)} collective-permute-done((f32[512,256]{1,0:T(8,128)S(1)}, f32[512,256]{1,0:T(8,128)S(1)}, u32[]{:S(2)}, u32[]{:S(2)}) %collective-permute-start) | collective-permute-done | bytes 524320 | tf_op jit(solution)/shard_map/while/body/eval_jaxpr/ppermute | solution.py:14
  180.4 16.7 %collective-permute-done = f32[512,256]{1,0:T(8,128)S(1)} collective-permute-done((f32[512,256]{1,0:T(8,128)S(1)}, f32[512,256]{1,0:T(8,128)S(1)}, u32[]{:S(2)}, u32[]{:S(2)}) %collective-permute-start) | collective-permute-done | bytes 524320 | tf_op jit(solution)/shard_map/while/body/eval_jaxpr/ppermute | solution.py:14
  198.1 17.7 %collective-permute-done = f32[512,256]{1,0:T(8,128)S(1)} collective-permute-done((f32[512,256]{1,0:T(8,128)S(1)}, f32[512,256]{1,0:T(8,128)S(1)}, u32[]{:S(2)}, u32[]{:S(2)}) %collective-permute-start) | collective-permute-done | bytes 524320 | tf_op jit(solution)/shard_map/while/body/eval_jaxpr/ppermute | solution.py:14
  216.9 18.9 %collective-permute-done = f32[512,256]{1,0:T(8,128)S(1)} collective-permute-done((f32[512,256]{1,0:T(8,128)S(1)}, f32[512,256]{1,0:T(8,128)S(1)}, u32[]{:S(2)}, u32[]{:S(2)}) %collective-permute-start) | collective-permute-done | bytes 524320 | tf_op jit(solution)/shard_map/while/body/eval_jaxpr/ppermute | solution.py:14
  236.7 19.7 %collective-permute-done = f32[512,256]{1,0:T(8,128)S(1)} collective-permute-done((f32[512,256]{1,0:T(8,128)S(1)}, f32[512,256]{1,0:T(8,128)S(1)}, u32[]{:S(2)}, u32[]{:S(2)}) %collective-permute-start) | collective-permute-done | bytes 524320 | tf_op jit(solution)/shard_map/while/body/eval_jaxpr/ppermute | solution.py:14
  257.4 18.8 %collective-permute-done = f32[512,256]{1,0:T(8,128)S(1)} collective-permute-done((f32[512,256]{1,0:T(8,128)S(1)}, f32[512,256]{1,0:T(8,128)S(1)}, u32[]{:S(2)}, u32[]{:S(2)}) %collective-permute-start) | collective-permute-done | bytes 524320 | tf_op jit(solution)/shard_map/while/body/eval_jaxpr/ppermute | solution.py:14
  277.1 17.8 %collective-permute-done = f32[512,256]{1,0:T(8,128)S(1)} collective-permute-done((f32[512,256]{1,0:T(8,128)S(1)}, f32[512,256]{1,0:T(8,128)S(1)}, u32[]{:S(2)}, u32[]{:S(2)}) %collective-permute-start) | collective-permute-done | bytes 524320 | tf_op jit(solution)/shard_map/while/body/eval_jaxpr/ppermute | solution.py:14
  296.1 13.0 %fusion = f32[4,4,128,256,1]{3,1,4,2,0:T(4,128)S(1)} fusion(f32[16,4,128,256,1]{3,2,1,0,4:T(8,128)} %bitcast.48, pred[4,4,4]{1,0,2:T(4,128)(4,1)S(1)} %iota_compare_fusion, pred[4,4,16]{2,1,0:T(4,128)(4,1)S(1)} %iota_compare_fusion.1), kind=kOutput, calls=%fused_computation.3 | convolution fusion | flops 402654208 | bytes 10486080 | tf_op jit(solution)/shard_map/iksc,scbd->ikbd/dot_general | solution.py:55
  311.9 55.4 %reduce-scatter.3.cloned.1.call-done = f32[128,256]{1,0:T(8,128)} async-done(((f32[512,256]{1,0:T(8,128)}), f32[128,256]{1,0:T(8,128)}) %reduce-scatter.3.cloned.1.call-update) | async-done | bytes 131088 | tf_op jit(solution)/shard_map/reduce_scatter | solution.py:59
  369.5 13.7 %all_gather.3 = f32[512,256]{1,0:T(8,128)S(1)} all-gather(f32[128,256]{1,0:T(8,128)S(1)} %fusion.16), channel_id=1, replica_groups=mesh['blk'=64,'rep'=4] {'rep'}, dimensions={0}, use_global_device_ids=true | all-gather | bytes 655360 | tf_op jit(solution)/shard_map/all_gather | solution.py:71
  387.1 5.9 convolution_bitcast_fusion
  396.3 242.4 %while.31 = (s32[]{:T(128)}, f32[512,256]{1,0:T(8,128)S(1)}, f32[16,4,128,256]{3,0,2,1:T(8,128)}, s32[]{:T(128)}, s32[]{:T(128)}, /*index=5*/s32[]{:T(128)}, s32[]{:T(128)}) while((s32[]{:T(128)}, f32[512,256]{1,0:T(8,128)S(1)}, f32[16,4,128,256]{3,0,2,1:T(8,128)}, s32[]{:T(128)}, s32[]{:T(128)}, /*index=5*/s32[]{:T(128)}, s32[]{:T(128)}) %tuple.81), condition=%wide.region_4.5_spmd, body=%wide.region_3.4_spmd.sunk | while | flops 131078 | bytes 5767335 | solution.py:89
  402.6 8.6 collective-permute-done.1
  411.3 8.3 collective-permute-start.1
  422.2 7.7 collective-permute-done.1
  429.9 8.3 collective-permute-start.1
  440.8 6.7 collective-permute-done.1
  447.7 8.3 collective-permute-start.1
  464.5 8.3 collective-permute-start.1
  480.3 8.3 collective-permute-start.1
  495.3 8.3 collective-permute-start.1
  509.8 8.0 collective-permute-start.1
  524.0 8.0 collective-permute-start.1
  538.2 8.0 collective-permute-start.1
  552.4 8.0 collective-permute-start.1
  567.5 8.0 collective-permute-start.1
  583.7 8.0 collective-permute-start.1
  594.3 6.6 collective-permute-done.1
  600.9 8.0 collective-permute-start.1
  611.5 7.6 collective-permute-done.1
  619.3 8.0 collective-permute-start.1
  629.9 8.7 collective-permute-done.1
  638.8 8.3 collective-permute-done.4
  648.5 8.3 collective-permute-done.5
  657.7 94.6 %psum.15 = f32[256]{0:T(256)} all-reduce(f32[256]{0:T(256)S(1)} %broadcast_multiply_fusion), channel_id=1, replica_groups=mesh['blk'=64,'rep'=4] {'blk','rep'}, use_global_device_ids=true, to_apply=%region_8.9 | all-reduce | flops 256 | bytes 2048 | tf_op jit(solution)/shard_map/psum | solution.py:69
  752.3 162.6 %all-reduce.3.cloned.1.call-done = f32[256,256]{1,0:T(8,128)} async-done(((f32[256,256]{1,0:T(8,128)}), f32[256,256]{1,0:T(8,128)}) %all-reduce.3.cloned.1.call-update) | async-done | bytes 262160 | tf_op jit(solution)/shard_map/psum | solution.py:69
  914.9 42.9 %reduce-scatter.5.cloned.1.call-done = f32[128,256]{1,0:T(8,128)} async-done(((f32[512,256]{1,0:T(8,128)}), f32[128,256]{1,0:T(8,128)}) %reduce-scatter.5.cloned.1.call-update) | async-done | bytes 131088 | tf_op jit(solution)/shard_map/reduce_scatter | solution.py:93
  (140 shorter events, 127.4 us)
Async XLA Ops:
  7.2 301.9 %copy-start = (f32[4,4,128,128]{3,2,1,0:T(8,128)S(1)}, f32[4,4,128,128]{3,2,1,0:T(8,128)}, u32[]{:S(2)}) copy-start(f32[4,4,128,128]{3,2,1,0:T(8,128)} %param.11) | copy-start | bytes 3145732
  7.2 360.1 %reduce-scatter.3.cloned.1.call-start = ((), (), s32[]{:S(2)}) async-start(), calls=%async_computation.2 | async-start | bytes 655360 | tf_op jit(solution)/shard_map/reduce_scatter | solution.py:59
  7.2 12.9 %collective-permute-start.2 = (f32[512,256]{1,0:T(8,128)}, f32[512,256]{1,0:T(8,128)S(1)}, u32[]{:S(2)}, u32[]{:S(2)}) collective-permute-start(f32[512,256]{1,0:T(8,128)} %param.10), channel_id=1, source_target_pairs={{0,64},{4,68},{8,72},{12,76},{16,80},{20,84},{24,88},{28,92},{32,9... | collective-permute-start | bytes 1572872 | tf_op jit(solution)/shard_map/ppermute | solution.py:14
  20.2 12.4 %collective-permute-start.3 = (f32[512,256]{1,0:T(8,128)S(1)}, f32[512,256]{1,0:T(8,128)S(1)}, u32[]{:S(2)}, u32[]{:S(2)}) collective-permute-start(f32[512,256]{1,0:T(8,128)S(1)} %broadcast_select_fusion.1), channel_id=1, source_target_pairs={{0,128},{4,132},{8,136},{12,140},{16,144},{20,148},{24,152},{28,15... | collective-permute-start | bytes 1572872 | tf_op jit(solution)/shard_map/ppermute | solution.py:14
  37.0 18.7 %collective-permute-start = (f32[512,256]{1,0:T(8,128)S(1)}, f32[512,256]{1,0:T(8,128)S(1)}, u32[]{:S(2)}, u32[]{:S(2)}) collective-permute-start(f32[512,256]{1,0:T(8,128)S(1)} %get-tuple-element.223), channel_id=1, source_target_pairs={{0,4},{4,8},{8,12},{12,16},{16,20},{20,24},{24,28},{28,32},{32,36}... | collective-permute-start | bytes 1572872 | tf_op jit(solution)/shard_map/while/body/eval_jaxpr/ppermute | solution.py:14
  56.5 15.4 %collective-permute-start = (f32[512,256]{1,0:T(8,128)S(1)}, f32[512,256]{1,0:T(8,128)S(1)}, u32[]{:S(2)}, u32[]{:S(2)}) collective-permute-start(f32[512,256]{1,0:T(8,128)S(1)} %get-tuple-element.223), channel_id=1, source_target_pairs={{0,4},{4,8},{8,12},{12,16},{16,20},{20,24},{24,28},{28,32},{32,36}... | collective-permute-start | bytes 1572872 | tf_op jit(solution)/shard_map/while/body/eval_jaxpr/ppermute | solution.py:14
  72.8 14.4 %collective-permute-start = (f32[512,256]{1,0:T(8,128)S(1)}, f32[512,256]{1,0:T(8,128)S(1)}, u32[]{:S(2)}, u32[]{:S(2)}) collective-permute-start(f32[512,256]{1,0:T(8,128)S(1)} %get-tuple-element.223), channel_id=1, source_target_pairs={{0,4},{4,8},{8,12},{12,16},{16,20},{20,24},{24,28},{28,32},{32,36}... | collective-permute-start | bytes 1572872 | tf_op jit(solution)/shard_map/while/body/eval_jaxpr/ppermute | solution.py:14
  88.1 14.1 %collective-permute-start = (f32[512,256]{1,0:T(8,128)S(1)}, f32[512,256]{1,0:T(8,128)S(1)}, u32[]{:S(2)}, u32[]{:S(2)}) collective-permute-start(f32[512,256]{1,0:T(8,128)S(1)} %get-tuple-element.223), channel_id=1, source_target_pairs={{0,4},{4,8},{8,12},{12,16},{16,20},{20,24},{24,28},{28,32},{32,36}... | collective-permute-start | bytes 1572872 | tf_op jit(solution)/shard_map/while/body/eval_jaxpr/ppermute | solution.py:14
  103.2 14.1 %collective-permute-start = (f32[512,256]{1,0:T(8,128)S(1)}, f32[512,256]{1,0:T(8,128)S(1)}, u32[]{:S(2)}, u32[]{:S(2)}) collective-permute-start(f32[512,256]{1,0:T(8,128)S(1)} %get-tuple-element.223), channel_id=1, source_target_pairs={{0,4},{4,8},{8,12},{12,16},{16,20},{20,24},{24,28},{28,32},{32,36}... | collective-permute-start | bytes 1572872 | tf_op jit(solution)/shard_map/while/body/eval_jaxpr/ppermute | solution.py:14
  118.2 14.1 %collective-permute-start = (f32[512,256]{1,0:T(8,128)S(1)}, f32[512,256]{1,0:T(8,128)S(1)}, u32[]{:S(2)}, u32[]{:S(2)}) collective-permute-start(f32[512,256]{1,0:T(8,128)S(1)} %get-tuple-element.223), channel_id=1, source_target_pairs={{0,4},{4,8},{8,12},{12,16},{16,20},{20,24},{24,28},{28,32},{32,36}... | collective-permute-start | bytes 1572872 | tf_op jit(solution)/shard_map/while/body/eval_jaxpr/ppermute | solution.py:14
  133.2 14.1 %collective-permute-start = (f32[512,256]{1,0:T(8,128)S(1)}, f32[512,256]{1,0:T(8,128)S(1)}, u32[]{:S(2)}, u32[]{:S(2)}) collective-permute-start(f32[512,256]{1,0:T(8,128)S(1)} %get-tuple-element.223), channel_id=1, source_target_pairs={{0,4},{4,8},{8,12},{12,16},{16,20},{20,24},{24,28},{28,32},{32,36}... | collective-permute-start | bytes 1572872 | tf_op jit(solution)/shard_map/while/body/eval_jaxpr/ppermute | solution.py:14
  148.2 14.6 %collective-permute-start = (f32[512,256]{1,0:T(8,128)S(1)}, f32[512,256]{1,0:T(8,128)S(1)}, u32[]{:S(2)}, u32[]{:S(2)}) collective-permute-start(f32[512,256]{1,0:T(8,128)S(1)} %get-tuple-element.223), channel_id=1, source_target_pairs={{0,4},{4,8},{8,12},{12,16},{16,20},{20,24},{24,28},{28,32},{32,36}... | collective-permute-start | bytes 1572872 | tf_op jit(solution)/shard_map/while/body/eval_jaxpr/ppermute | solution.py:14
  163.7 15.7 %collective-permute-start = (f32[512,256]{1,0:T(8,128)S(1)}, f32[512,256]{1,0:T(8,128)S(1)}, u32[]{:S(2)}, u32[]{:S(2)}) collective-permute-start(f32[512,256]{1,0:T(8,128)S(1)} %get-tuple-element.223), channel_id=1, source_target_pairs={{0,4},{4,8},{8,12},{12,16},{16,20},{20,24},{24,28},{28,32},{32,36}... | collective-permute-start | bytes 1572872 | tf_op jit(solution)/shard_map/while/body/eval_jaxpr/ppermute | solution.py:14
  180.3 16.8 %collective-permute-start = (f32[512,256]{1,0:T(8,128)S(1)}, f32[512,256]{1,0:T(8,128)S(1)}, u32[]{:S(2)}, u32[]{:S(2)}) collective-permute-start(f32[512,256]{1,0:T(8,128)S(1)} %get-tuple-element.223), channel_id=1, source_target_pairs={{0,4},{4,8},{8,12},{12,16},{16,20},{20,24},{24,28},{28,32},{32,36}... | collective-permute-start | bytes 1572872 | tf_op jit(solution)/shard_map/while/body/eval_jaxpr/ppermute | solution.py:14
  198.1 17.8 %collective-permute-start = (f32[512,256]{1,0:T(8,128)S(1)}, f32[512,256]{1,0:T(8,128)S(1)}, u32[]{:S(2)}, u32[]{:S(2)}) collective-permute-start(f32[512,256]{1,0:T(8,128)S(1)} %get-tuple-element.223), channel_id=1, source_target_pairs={{0,4},{4,8},{8,12},{12,16},{16,20},{20,24},{24,28},{28,32},{32,36}... | collective-permute-start | bytes 1572872 | tf_op jit(solution)/shard_map/while/body/eval_jaxpr/ppermute | solution.py:14
  216.8 19.0 %collective-permute-start = (f32[512,256]{1,0:T(8,128)S(1)}, f32[512,256]{1,0:T(8,128)S(1)}, u32[]{:S(2)}, u32[]{:S(2)}) collective-permute-start(f32[512,256]{1,0:T(8,128)S(1)} %get-tuple-element.223), channel_id=1, source_target_pairs={{0,4},{4,8},{8,12},{12,16},{16,20},{20,24},{24,28},{28,32},{32,36}... | collective-permute-start | bytes 1572872 | tf_op jit(solution)/shard_map/while/body/eval_jaxpr/ppermute | solution.py:14
  236.6 19.7 %collective-permute-start = (f32[512,256]{1,0:T(8,128)S(1)}, f32[512,256]{1,0:T(8,128)S(1)}, u32[]{:S(2)}, u32[]{:S(2)}) collective-permute-start(f32[512,256]{1,0:T(8,128)S(1)} %get-tuple-element.223), channel_id=1, source_target_pairs={{0,4},{4,8},{8,12},{12,16},{16,20},{20,24},{24,28},{28,32},{32,36}... | collective-permute-start | bytes 1572872 | tf_op jit(solution)/shard_map/while/body/eval_jaxpr/ppermute | solution.py:14
  257.3 18.8 %collective-permute-start = (f32[512,256]{1,0:T(8,128)S(1)}, f32[512,256]{1,0:T(8,128)S(1)}, u32[]{:S(2)}, u32[]{:S(2)}) collective-permute-start(f32[512,256]{1,0:T(8,128)S(1)} %get-tuple-element.223), channel_id=1, source_target_pairs={{0,4},{4,8},{8,12},{12,16},{16,20},{20,24},{24,28},{28,32},{32,36}... | collective-permute-start | bytes 1572872 | tf_op jit(solution)/shard_map/while/body/eval_jaxpr/ppermute | solution.py:14
  277.0 17.9 %collective-permute-start = (f32[512,256]{1,0:T(8,128)S(1)}, f32[512,256]{1,0:T(8,128)S(1)}, u32[]{:S(2)}, u32[]{:S(2)}) collective-permute-start(f32[512,256]{1,0:T(8,128)S(1)} %get-tuple-element.223), channel_id=1, source_target_pairs={{0,4},{4,8},{8,12},{12,16},{16,20},{20,24},{24,28},{28,32},{32,36}... | collective-permute-start | bytes 1572872 | tf_op jit(solution)/shard_map/while/body/eval_jaxpr/ppermute | solution.py:14
  296.1 71.2 %copy-start.1 = (f32[128,256]{1,0:T(8,128)S(1)}, f32[128,256]{1,0:T(8,128)}, u32[]{:S(2)}) copy-start(f32[128,256]{1,0:T(8,128)} %param.15) | copy-start | bytes 393220
  296.1 71.2 %copy-start.3 = (f32[256,256]{1,0:T(8,128)S(1)}, f32[256,256]{1,0:T(8,128)}, u32[]{:S(2)}) copy-start(f32[256,256]{1,0:T(8,128)} %param.13) | copy-start | bytes 786436
  296.1 71.2 %copy-start.5 = (f32[256]{0:T(256)S(1)}, f32[256]{0:T(256)}, u32[]{:S(2)}) copy-start(f32[256]{0:T(256)} %param.14) | copy-start | bytes 3076
  311.6 603.3 %all-reduce.3.cloned.1.call-start = ((), (), s32[]{:S(2)}) async-start(), calls=%async_computation.4 | async-start | bytes 524288 | tf_op jit(solution)/shard_map/psum | solution.py:69
  393.1 3.2 copy-start.2
  396.3 250.9 %copy-start.4 = (f32[128,256]{1,0:T(8,128)S(1)}, f32[128,256]{1,0:T(8,128)}, u32[]{:S(2)}) copy-start(f32[128,256]{1,0:T(8,128)} %reduce-scatter.3.cloned.1.call-done) | copy-start | bytes 393220
  396.3 14.9 %collective-permute-start.1 = (f32[512,256]{1,0:T(8,128)S(1)}, f32[512,256]{1,0:T(8,128)S(1)}, u32[]{:S(2)}, u32[]{:S(2)}) collective-permute-start(f32[512,256]{1,0:T(8,128)S(1)} %get-tuple-element.242), channel_id=1, source_target_pairs={{0,252},{4,0},{8,4},{12,8},{16,12},{20,16},{24,20},{28,24},{32,28}... | collective-permute-start | bytes 1572872 | tf_op jit(solution)/shard_map/while/body/eval_jaxpr/ppermute | solution.py:14
  411.3 18.6 %collective-permute-start.1 = (f32[512,256]{1,0:T(8,128)S(1)}, f32[512,256]{1,0:T(8,128)S(1)}, u32[]{:S(2)}, u32[]{:S(2)}) collective-permute-start(f32[512,256]{1,0:T(8,128)S(1)} %get-tuple-element.242), channel_id=1, source_target_pairs={{0,252},{4,0},{8,4},{12,8},{16,12},{20,16},{24,20},{28,24},{32,28}... | collective-permute-start | bytes 1572872 | tf_op jit(solution)/shard_map/while/body/eval_jaxpr/ppermute | solution.py:14
  429.9 17.6 %collective-permute-start.1 = (f32[512,256]{1,0:T(8,128)S(1)}, f32[512,256]{1,0:T(8,128)S(1)}, u32[]{:S(2)}, u32[]{:S(2)}) collective-permute-start(f32[512,256]{1,0:T(8,128)S(1)} %get-tuple-element.242), channel_id=1, source_target_pairs={{0,252},{4,0},{8,4},{12,8},{16,12},{20,16},{24,20},{28,24},{32,28}... | collective-permute-start | bytes 1572872 | tf_op jit(solution)/shard_map/while/body/eval_jaxpr/ppermute | solution.py:14
  447.7 16.7 %collective-permute-start.1 = (f32[512,256]{1,0:T(8,128)S(1)}, f32[512,256]{1,0:T(8,128)S(1)}, u32[]{:S(2)}, u32[]{:S(2)}) collective-permute-start(f32[512,256]{1,0:T(8,128)S(1)} %get-tuple-element.242), channel_id=1, source_target_pairs={{0,252},{4,0},{8,4},{12,8},{16,12},{20,16},{24,20},{28,24},{32,28}... | collective-permute-start | bytes 1572872 | tf_op jit(solution)/shard_map/while/body/eval_jaxpr/ppermute | solution.py:14
  464.5 15.8 %collective-permute-start.1 = (f32[512,256]{1,0:T(8,128)S(1)}, f32[512,256]{1,0:T(8,128)S(1)}, u32[]{:S(2)}, u32[]{:S(2)}) collective-permute-start(f32[512,256]{1,0:T(8,128)S(1)} %get-tuple-element.242), channel_id=1, source_target_pairs={{0,252},{4,0},{8,4},{12,8},{16,12},{20,16},{24,20},{28,24},{32,28}... | collective-permute-start | bytes 1572872 | tf_op jit(solution)/shard_map/while/body/eval_jaxpr/ppermute | solution.py:14
  480.3 14.9 %collective-permute-start.1 = (f32[512,256]{1,0:T(8,128)S(1)}, f32[512,256]{1,0:T(8,128)S(1)}, u32[]{:S(2)}, u32[]{:S(2)}) collective-permute-start(f32[512,256]{1,0:T(8,128)S(1)} %get-tuple-element.242), channel_id=1, source_target_pairs={{0,252},{4,0},{8,4},{12,8},{16,12},{20,16},{24,20},{28,24},{32,28}... | collective-permute-start | bytes 1572872 | tf_op jit(solution)/shard_map/while/body/eval_jaxpr/ppermute | solution.py:14
  495.3 14.4 %collective-permute-start.1 = (f32[512,256]{1,0:T(8,128)S(1)}, f32[512,256]{1,0:T(8,128)S(1)}, u32[]{:S(2)}, u32[]{:S(2)}) collective-permute-start(f32[512,256]{1,0:T(8,128)S(1)} %get-tuple-element.242), channel_id=1, source_target_pairs={{0,252},{4,0},{8,4},{12,8},{16,12},{20,16},{24,20},{28,24},{32,28}... | collective-permute-start | bytes 1572872 | tf_op jit(solution)/shard_map/while/body/eval_jaxpr/ppermute | solution.py:14
  509.8 14.1 %collective-permute-start.1 = (f32[512,256]{1,0:T(8,128)S(1)}, f32[512,256]{1,0:T(8,128)S(1)}, u32[]{:S(2)}, u32[]{:S(2)}) collective-permute-start(f32[512,256]{1,0:T(8,128)S(1)} %get-tuple-element.242), channel_id=1, source_target_pairs={{0,252},{4,0},{8,4},{12,8},{16,12},{20,16},{24,20},{28,24},{32,28}... | collective-permute-start | bytes 1572872 | tf_op jit(solution)/shard_map/while/body/eval_jaxpr/ppermute | solution.py:14
  524.0 14.1 %collective-permute-start.1 = (f32[512,256]{1,0:T(8,128)S(1)}, f32[512,256]{1,0:T(8,128)S(1)}, u32[]{:S(2)}, u32[]{:S(2)}) collective-permute-start(f32[512,256]{1,0:T(8,128)S(1)} %get-tuple-element.242), channel_id=1, source_target_pairs={{0,252},{4,0},{8,4},{12,8},{16,12},{20,16},{24,20},{28,24},{32,28}... | collective-permute-start | bytes 1572872 | tf_op jit(solution)/shard_map/while/body/eval_jaxpr/ppermute | solution.py:14
  538.2 14.1 %collective-permute-start.1 = (f32[512,256]{1,0:T(8,128)S(1)}, f32[512,256]{1,0:T(8,128)S(1)}, u32[]{:S(2)}, u32[]{:S(2)}) collective-permute-start(f32[512,256]{1,0:T(8,128)S(1)} %get-tuple-element.242), channel_id=1, source_target_pairs={{0,252},{4,0},{8,4},{12,8},{16,12},{20,16},{24,20},{28,24},{32,28}... | collective-permute-start | bytes 1572872 | tf_op jit(solution)/shard_map/while/body/eval_jaxpr/ppermute | solution.py:14
  552.4 15.0 %collective-permute-start.1 = (f32[512,256]{1,0:T(8,128)S(1)}, f32[512,256]{1,0:T(8,128)S(1)}, u32[]{:S(2)}, u32[]{:S(2)}) collective-permute-start(f32[512,256]{1,0:T(8,128)S(1)} %get-tuple-element.242), channel_id=1, source_target_pairs={{0,252},{4,0},{8,4},{12,8},{16,12},{20,16},{24,20},{28,24},{32,28}... | collective-permute-start | bytes 1572872 | tf_op jit(solution)/shard_map/while/body/eval_jaxpr/ppermute | solution.py:14
  567.5 16.1 %collective-permute-start.1 = (f32[512,256]{1,0:T(8,128)S(1)}, f32[512,256]{1,0:T(8,128)S(1)}, u32[]{:S(2)}, u32[]{:S(2)}) collective-permute-start(f32[512,256]{1,0:T(8,128)S(1)} %get-tuple-element.242), channel_id=1, source_target_pairs={{0,252},{4,0},{8,4},{12,8},{16,12},{20,16},{24,20},{28,24},{32,28}... | collective-permute-start | bytes 1572872 | tf_op jit(solution)/shard_map/while/body/eval_jaxpr/ppermute | solution.py:14
  583.7 17.2 %collective-permute-start.1 = (f32[512,256]{1,0:T(8,128)S(1)}, f32[512,256]{1,0:T(8,128)S(1)}, u32[]{:S(2)}, u32[]{:S(2)}) collective-permute-start(f32[512,256]{1,0:T(8,128)S(1)} %get-tuple-element.242), channel_id=1, source_target_pairs={{0,252},{4,0},{8,4},{12,8},{16,12},{20,16},{24,20},{28,24},{32,28}... | collective-permute-start | bytes 1572872 | tf_op jit(solution)/shard_map/while/body/eval_jaxpr/ppermute | solution.py:14
  600.9 18.2 %collective-permute-start.1 = (f32[512,256]{1,0:T(8,128)S(1)}, f32[512,256]{1,0:T(8,128)S(1)}, u32[]{:S(2)}, u32[]{:S(2)}) collective-permute-start(f32[512,256]{1,0:T(8,128)S(1)} %get-tuple-element.242), channel_id=1, source_target_pairs={{0,252},{4,0},{8,4},{12,8},{16,12},{20,16},{24,20},{28,24},{32,28}... | collective-permute-start | bytes 1572872 | tf_op jit(solution)/shard_map/while/body/eval_jaxpr/ppermute | solution.py:14
  619.3 19.3 %collective-permute-start.1 = (f32[512,256]{1,0:T(8,128)S(1)}, f32[512,256]{1,0:T(8,128)S(1)}, u32[]{:S(2)}, u32[]{:S(2)}) collective-permute-start(f32[512,256]{1,0:T(8,128)S(1)} %get-tuple-element.242), channel_id=1, source_target_pairs={{0,252},{4,0},{8,4},{12,8},{16,12},{20,16},{24,20},{28,24},{32,28}... | collective-permute-start | bytes 1572872 | tf_op jit(solution)/shard_map/while/body/eval_jaxpr/ppermute | solution.py:14
  638.7 8.4 collective-permute-start.4
  647.1 9.6 collective-permute-start.5
  648.4 309.4 %reduce-scatter.5.cloned.1.call-start = ((), (), s32[]{:S(2)}) async-start(), calls=%async_computation.3 | async-start | bytes 655360 | tf_op jit(solution)/shard_map/reduce_scatter | solution.py:93
Sparse Core Ops, SparseCore 0:
  311.7 55.4 reduce-scatter.2
  648.5 266.3 all-reduce.2
  918.4 39.3 reduce-scatter.4
where the time goes:
time: 967 us; the launch traced here: 966 us
  waiting for transfers between devices  621 us (64%)
  starting transfers between devices  129 us (13%)
  blocking collectives  108 us (11%)
  local copies, waits for them, and re-layouts  63.2 us (7%)
  matrix products  26.6 us (3%)
  between operations  13.9 us (1%)
    ppermute x34, waiting for transfers between devices, shifted_2(): return lax.ppermute(value, axis, pairs)  361 us
    psum x1, waiting for transfers between devices, body(): grad_weight, grad_bias = lax.psum((grad_weight, grad_bias), ('blk', 'rep'))  163 us
    ppermute x34, starting transfers between devices, shifted_2(): return lax.ppermute(value, axis, pairs)  128 us
    psum x1, blocking collectives, body(): grad_weight, grad_bias = lax.psum((grad_weight, grad_bias), ('blk', 'rep'))  94.6 us
    reduce_scatter x1, waiting for transfers between devices, body(): lax.psum_scatter(partial_aggregate, 'rep', scatter_dimension=0, tiled=True)  55.4 us
    reduce_scatter x1, waiting for transfers between devices, body(): lax.psum_scatter(adjoint, 'rep', scatter_dimension=0, tiled=True)  42.9 us
    dynamic_slice x31, local copies, waits for them, and re-layouts, adjoint_term(): lax.dynamic_index_in_dim(sorted_terms, section_no, 0, keepdims=False)  39.3 us
  transfers between devices with their start and end apart: 37, of which 37 were waited for; matrix products, arithmetic and copies ran while one was open for 4% of the time, Pallas kernels for 0%

commit v1 on v0

v1 whole, which is shorter than its diff:
```python
import math

import jax
import jax.numpy as jnp
from jax import lax
from jax.experimental import pallas as pl
from jax.experimental.pallas import tpu as pltpu
from jax.sharding import Mesh
from jax.sharding import PartitionSpec as P

AXES = ("x", "zl", "y", "zh", "c")
PLANE = ("zl", "y")
TOP = lax.Precision.HIGHEST
F32 = jnp.float32
LIMIT = 48 * 1024 * 1024


def shift(value, axis, steps):
    count = lax.axis_size(axis)
    return lax.ppermute(value, axis, [(s, (s + steps) % count) for s in range(count)])


def plane_exchange(value):
    return lax.all_to_all(value, PLANE, 0, 0, tiled=True)


def vmem():
    return pl.BlockSpec(memory_space=pltpu.VMEM)


def smem():
    return pl.BlockSpec(memory_space=pltpu.SMEM)


def call(kernel, out_shape, specs, scratch=(), flops=0, moved=0):
    return pl.pallas_call(
        kernel,
        out_shape=out_shape,
        in_specs=specs,
        out_specs=jax.tree.map(lambda _: vmem(), out_shape),
        scratch_shapes=scratch,
        compiler_params=pltpu.CompilerParams(vmem_limit_bytes=LIMIT),
        cost_estimate=pl.CostEstimate(flops=flops, bytes_accessed=moved, transcendentals=0),
    )


def gather_kernel(index_ref, where_ref, near_ref, far_ref, out_ref):
    core = where_ref[0]

    def one(dest, carry):
        for slot in range(16):
            row = index_ref[dest * 16 + slot]
            out_ref[dest, 2 * slot + core] = near_ref[row]
            out_ref[dest, 2 * slot + 1 - core] = far_ref[row]
        return carry

    lax.fori_loop(0, 16, one, 0)


def scatter_kernel(index_ref, where_ref, got_ref, keep_ref, send_ref):
    core = where_ref[0]
    keep_ref[...] = jnp.zeros_like(keep_ref)
    send_ref[...] = jnp.zeros_like(send_ref)

    def one(source, carry):
        for slot in range(16):
            row = index_ref[source * 16 + slot]
            spot = row + 6 * (row // 64)
            keep_ref[spot] += got_ref[source, 2 * slot + core]
            send_ref[spot] += got_ref[source, 2 * slot + 1 - core]
        return carry

    lax.fori_loop(0, 16, one, 0)
    for part in range(6):
        total = jnp.sum(got_ref[:, 32 + part], axis=0)
        for plane in range(4):
            keep_ref[plane * 70 + 64 + part] = total
            send_ref[plane * 70 + 64 + part] = total


def dot(a, b):
    return lax.dot_general(
        a, b, (((1,), (0,)), ((), ())), precision=TOP, preferred_element_type=F32
    )


def dot_first(a, b):
    return lax.dot_general(
        a, b, (((0,), (0,)), ((), ())), precision=TOP, preferred_element_type=F32
    )


def dot_last(a, b):
    return lax.dot_general(
        a, b, (((1,), (1,)), ((), ())), precision=TOP, preferred_element_type=F32
    )


def forward_kernel(where_ref, own_ref, swapped_ref, got_ref, out_ref):
    half = where_ref[1]
    for block in range(2):
        total = [jnp.zeros((128, 128), F32), jnp.zeros((128, 128), F32)]
        for source in range(2):
            for k in range(4):
                slot = block * 8 + source * 4 + k
                tile = own_ref[2 * half + block, k] if source == 0 else swapped_ref[block, k]
                for h in range(2):
                    total[h] += dot(tile, got_ref[:, 2 * slot + h].reshape(128, 128))
        for h in range(2):
            out_ref[block, :, 128 * h : 128 * (h + 1)] = total[h]


def middle_kernel(
    scale,
    where_ref,
    own_ref,
    swapped_ref,
    mine_ref,
    other_ref,
    cot_ref,
    weight_ref,
    bias_ref,
    layer_ref,
    out_ref,
):
    core = where_ref[0]
    half = where_ref[1]
    for block in range(2):
        hidden = mine_ref[block] + other_ref[block]
        pre = dot(hidden, weight_ref[...]) + bias_ref[...]
        grow = jnp.exp(jnp.minimum(pre, 0.0))
        layer = jnp.where(pre > 0, pre, grow - 1.0)
        grad_pre = cot_ref[block] * jnp.where(pre > 0, 1.0, grow)
        grad_hidden = dot_last(grad_pre, weight_ref[...])

        @pl.when(core == block)
        def _():
            layer_ref[...] = layer
            grad_weight = dot_first(hidden, grad_pre) * scale
            grad_bias = jnp.sum(grad_pre, axis=0, keepdims=True) * scale
            for m in range(16):
                for part in range(4):
                    top, left = 16 * m + 8 * (part // 2), 128 * (part % 2)
                    out_ref[m, 32 + part] = grad_weight[top : top + 8, left : left + 128]
                for h in range(2):
                    out_ref[m, 36 + h] = jnp.broadcast_to(
                        grad_bias[:, 128 * h : 128 * (h + 1)], (8, 128)
                    )

        for source in range(2):
            for k in range(4):
                slot = block * 8 + source * 4 + k
                tile = own_ref[2 * half + block, k] if source == 0 else swapped_ref[block, k]
                term = dot_first(tile, grad_hidden)
                for h in range(2):
                    out_ref[:, 2 * slot + h] = term[:, 128 * h : 128 * (h + 1)].reshape(
                        16, 8, 128
                    )


def body(node_feats, operator_tiles, tile_cols, weight, layer_bias, cotangent):
    x = lax.axis_index("x")
    half = lax.axis_index("zh")
    core = lax.axis_index("c")
    where = jnp.stack([core, half]).astype(jnp.int32)
    scale = 1.0 / math.sqrt(32768)

    swapped = shift(lax.dynamic_slice_in_dim(operator_tiles, 2 * (1 - half), 2, 0), "zh", 1)
    cot_other = shift(cotangent, "c", 1)
    cots = jnp.where(
        core == 0, jnp.stack([cotangent, cot_other]), jnp.stack([cot_other, cotangent])
    )

    columns = lax.dynamic_slice_in_dim(node_feats, core * 128, 128, 1)
    chunks = columns.reshape(4, 16, 8, 128).transpose(1, 0, 2, 3)
    wanted = jnp.pad(tile_cols.astype(F32).reshape(1, 16), ((0, 7), (0, 112)))
    wanted = jnp.broadcast_to(wanted[None, None], (16, 1, 8, 128))
    arrived = plane_exchange(jnp.concatenate([chunks, wanted], axis=1))
    plane = arrived[:, :4].reshape(64, 8, 128)
    near = jnp.concatenate([plane] + [shift(plane, "x", d) for d in (1, 2, 3)], axis=0)
    far = shift(near, "c", 1)

    asked = arrived[:, 4, 0, :16]
    asked_other = shift(asked, "zh", 1)
    asked = jnp.stack([asked.reshape(16, 4, 4), asked_other.reshape(16, 4, 4)], axis=2)
    asked = lax.dynamic_slice_in_dim(asked, 2 * half, 2, 1).reshape(256).astype(jnp.int32)
    index = jnp.mod(x - asked // 64, 4) * 64 + asked % 64

    sent = call(
        gather_kernel,
        jax.ShapeDtypeStruct((16, 32, 8, 128), F32),
        [smem(), smem(), vmem(), vmem()],
        moved=4 << 20,
    )(index, where, near, far)
    got = plane_exchange(sent)
    mine = call(
        forward_kernel,
        jax.ShapeDtypeStruct((2, 128, 256), F32),
        [smem(), vmem(), vmem(), vmem()],
        flops=134217728 * 6,
        moved=4 << 20,
    )(where, operator_tiles, swapped, got)
    other = shift(mine, "c", 1)

    def middle(*refs):
        middle_kernel(scale, *refs)

    layer_out, terms = call(
        middle,
        (
            jax.ShapeDtypeStruct((128, 256), F32),
            jax.ShapeDtypeStruct((16, 38, 8, 128), F32),
        ),
        [smem()] + [vmem()] * 7,
        flops=234217728 * 6,
        moved=5 << 20,
    )(where, operator_tiles, swapped, mine, other, cots, weight, layer_bias.reshape(1, 256))
    back = plane_exchange(terms)
    keep, send = call(
        scatter_kernel,
        (
            jax.ShapeDtypeStruct((280, 8, 128), F32),
            jax.ShapeDtypeStruct((280, 8, 128), F32),
        ),
        [smem(), smem(), vmem()],
        moved=5 << 20,
    )(index, where, back)
    table = (keep + shift(send, "c", 1)).reshape(4, 70, 8, 128)
    total = table[0]
    for d in (1, 2, 3):
        total = total + shift(table[d], "x", -d)
    by_owner = total[:64].reshape(16, 4, 8, 128)
    staying = lax.dynamic_slice_in_dim(by_owner, 2 * half, 2, 1).reshape(32, 8, 128)
    leaving = lax.dynamic_slice_in_dim(by_owner, 2 * (1 - half), 2, 1).reshape(32, 8, 128)
    final = jnp.concatenate([staying, total[64:]], axis=0) + shift(
        jnp.concatenate([leaving, total[64:]], axis=0), "zh", 1
    )
    home = plane_exchange(
        jnp.concatenate(
            [
                final[:32].reshape(16, 2, 8, 128),
                jnp.broadcast_to(final[None, 32:36], (16, 4, 8, 128)),
            ],
            axis=1,
        )
    )
    grad_weight = (
        home[:, 2:].reshape(16, 2, 2, 8, 128).transpose(0, 1, 3, 2, 4).reshape(256, 256)
    )
    grad_bias = final[36:, 0].reshape(256)
    pair = home[:, :2].transpose(1, 0, 2, 3).reshape(2, 128, 128)
    own = lax.dynamic_index_in_dim(pair, core, 0, keepdims=False)
    given = shift(lax.dynamic_index_in_dim(pair, 1 - core, 0, keepdims=False), "c", 1)
    grad_feats = jnp.where(
        core == 0,
        jnp.concatenate([own, given], axis=1),
        jnp.concatenate([given, own], axis=1),
    )
    return layer_out, grad_feats, grad_weight, grad_bias


def solution(mesh):
    fine = Mesh(mesh.devices.reshape(4, 4, 4, 2, 2), AXES)
    blk, rep = ("x", "zl", "y"), ("zh", "c")
    return jax.shard_map(
        body,
        mesh=fine,
        in_specs=(
            P(blk, None),
            P(blk, rep, None, None),
            P(blk, rep),
            P(),
            P(),
            P(AXES, None),
        ),
        out_specs=(P(AXES, None), P(AXES, None), P(), P()),
        check_vma=False,
    )
```

time: 967 us -> 256 us (0.26)
  waiting for transfers between devices: 621 us -> 106 us
  starting transfers between devices: 129 us -> 40.5 us
  local copies, waits for them, and re-layouts: 63.2 us -> 6.68 us
  matrix products: 26.6 us -> 0 us
  blocking collectives: 108 us -> 86.1 us
  between operations: 13.9 us -> 0.9 us
  Pallas kernels: 0 us -> 12.1 us
    ppermute x34 -> x14, waiting for transfers between devices: 361 us -> 91.2 us  [shift(): lax.ppermute(value, axis, [(s, (s + steps) % count) for s in range(count)])]
    psum x1 -> x0, waiting for transfers between devices: 163 us -> none  [body(): grad_weight, grad_bias = lax.psum((grad_weight, grad_bias), ('blk', 'rep'))]
    ppermute x34 -> x14, starting transfers between devices: 128 us -> 28.4 us  [shift(): lax.ppermute(value, axis, [(s, (s + steps) % count) for s in range(count)])]
    reduce_scatter x2 -> x0, waiting for transfers between devices: 98.3 us -> none  [the longest x1 55.4 us: body(): lax.psum_scatter(partial_aggregate, 'rep', scatter_dimension=0, tiled=True)]
    psum x1 -> x0, blocking collectives: 94.6 us -> none  [body(): grad_weight, grad_bias = lax.psum((grad_weight, grad_bias), ('blk', 'rep'))]
    all_to_all x0 -> x2, blocking collectives: none -> 86.1 us  [plane_exchange(): return lax.all_to_all(value, PLANE, 0, 0, tiled=True)]
    dynamic_slice x31 -> x3, local copies, waits for them, and re-layouts: 39.3 us -> 1.18 us  [the longest x1 1.13 us: body(): lax.dynamic_slice_in_dim(operator_tiles, 2 * (1 - half), 2, 0)]
    dot_general x7 -> x0, matrix products: 26.6 us -> none  [the longest x1 13 us: body(): jnp.einsum('iksc,scbd->ikbd', chosen, received, precision=TOP_PRECISION)]
  transfers between devices with their start and end apart: 37 -> 16, of which waited for: 37 -> 12; matrix products, arithmetic and copies ran while one was open for 4% -> 1% of each run, Pallas kernels for 0% -> 0%
where the time goes in v1:
time: 256 us; the launch traced here: 255 us
  waiting for transfers between devices  106 us (41%)
  blocking collectives  86.1 us (34%)
  starting transfers between devices  40.5 us (16%)
  Pallas kernels  12.1 us (5%)
  local copies, waits for them, and re-layouts  6.68 us (3%)
  other arithmetic  2.62 us (1%)
    ppermute x14, waiting for transfers between devices, shift(): lax.ppermute(value, axis, [(s, (s + steps) % count) for s in range(count)])  91.2 us
    all_to_all x2, blocking collectives, plane_exchange(): return lax.all_to_all(value, PLANE, 0, 0, tiled=True)  86.1 us
    ppermute x14, starting transfers between devices, shift(): lax.ppermute(value, axis, [(s, (s + steps) % count) for s in range(count)])  28.4 us
    all_to_all x2, waiting for transfers between devices, plane_exchange(): return lax.all_to_all(value, PLANE, 0, 0, tiled=True)  15 us
    all_to_all x2, starting transfers between devices, plane_exchange(): return lax.all_to_all(value, PLANE, 0, 0, tiled=True)  12.1 us
  transfers between devices with their start and end apart: 16, of which 12 were waited for; matrix products, arithmetic and copies ran while one was open for 1% of the time, Pallas kernels for 0%

profile of v1, /device:TPU:1, one launch (start us, length us, event | category | flops | bytes accessed | tf_op | source)
XLA Modules:
  0.0 255.1 jit_solution(13145758699048044525)
XLA Ops:
  0.7 0.7 convert_element_type.11
  1.4 0.1 reshape.57
  1.5 0.2 copy-done
  1.8 19.6 %all_to_all.20 = f32[16,5,8,128]{3,2,1,0:T(8,128)S(1)} all-to-all(f32[16,5,8,128]{3,2,1,0:T(8,128)S(1)} %copy.16), channel_id=1, replica_groups=mesh['x'=4,'zl'=4,'y'=4,'zh'=2,'c'=2] {'zl','y'}, dimensions={0} | all-to-all | bytes 655360 | tf_op jit(solution)/shard_map/all_to_all | solution.py:24
  21.4 2.6 %collective-permute-start.4 = (f32[64,8,128]{2,1,0:T(8,128)S(1)}, f32[64,8,128]{2,1,0:T(8,128)S(1)}, u32[]{:S(2)}, u32[]{:S(2)}) collective-permute-start(f32[64,8,128]{2,1,0:T(8,128)S(1)} %bitcast.34), channel_id=1, source_target_pairs={{0,192},{64,0},{128,64},{192,128},{1,193},{65,1},{129,65},{193,129... | collective-permute-start | bytes 786440 | tf_op jit(solution)/shard_map/ppermute | solution.py:20
  24.0 0.5 collective-permute-start.3
  24.5 0.6 collective-permute-start.2
  25.1 4.1 %collective-permute-done.4 = f32[64,8,128]{2,1,0:T(8,128)S(1)} collective-permute-done((f32[64,8,128]{2,1,0:T(8,128)S(1)}, f32[64,8,128]{2,1,0:T(8,128)S(1)}, u32[]{:S(2)}, u32[]{:S(2)}) %collective-permute-start.4) | collective-permute-done | bytes 262176 | tf_op jit(solution)/shard_map/ppermute | solution.py:20
  29.2 1.6 collective-permute-done.3
  30.8 8.2 %collective-permute-done.2 = f32[64,8,128]{2,1,0:T(8,128)S(1)} collective-permute-done((f32[64,8,128]{2,1,0:T(8,128)S(1)}, f32[64,8,128]{2,1,0:T(8,128)S(1)}, u32[]{:S(2)}, u32[]{:S(2)}) %collective-permute-start.2) | collective-permute-done | bytes 262176 | tf_op jit(solution)/shard_map/ppermute | solution.py:20
  39.0 0.9 collective-permute-start.5
  40.1 4.2 %collective-permute-start.1 = (f32[16,16]{0,1:T(8,128)S(1)}, f32[16,16]{0,1:T(8,128)S(1)}, u32[]{:S(2)}, u32[]{:S(2)}) collective-permute-start(f32[16,16]{0,1:T(8,128)S(1)} %bitcast.44), channel_id=1, source_target_pairs={{0,2},{2,0},{1,3},{3,1},{4,6},{6,4},{5,7},{7,5},{8,10},{10,8},{9,1... | collective-permute-start | bytes 3080 | tf_op jit(solution)/shard_map/ppermute | solution.py:20
  44.4 2.1 collective-permute-done.1
  46.5 0.1 copy.18
  46.6 0.1 convert_element_type.13
  46.8 2.6 %shard_map.93 = f32[16,32,8,128]{3,2,1,0:T(8,128)} custom-call(s32[256]{0:T(256)S(1)} %fusion.6.index_ref, s32[2]{0:T(128)S(1)} %pad_add_fusion.where_ref.refs_0_, f32[256,8,128]{2,1,0:T(8,128)S(1)} %pad_maximum_fusion.near_ref, f32[256,8,128]{2,1,0:T(8,128)S(1)} %collective-permute-done.5.far_ref), custom_call_target="tpu_custom_call" | custom-call | bytes 4194304 | tf_op jit(solution)/shard_map/pallas_call | solution.py:189
  49.4 4.4 %all-to-all-start.1 = ((f32[16,32,8,128]{3,2,1,0:T(8,128)}), f32[16,32,8,128]{3,2,1,0:T(8,128)S(1)}, u32[]{:S(2)}, u32[]{:S(2)}) async-start(f32[16,32,8,128]{3,2,1,0:T(8,128)} %shard_map.93), calls=%async_computation.1 | async-start | bytes 4194304 | tf_op jit(solution)/shard_map/all_to_all | solution.py:24
  53.8 1.1 constant_dynamic-slice_fusion.3
  54.9 4.3 %collective-permute-start = (f32[2,4,128,128]{3,2,1,0:T(8,128)S(1)}, f32[2,4,128,128]{3,2,1,0:T(8,128)S(1)}, u32[]{:S(2)}, u32[]{:S(2)}) collective-permute-start(f32[2,4,128,128]{3,2,1,0:T(8,128)S(1)} %constant_dynamic-slice_fusion.3), channel_id=1, source_target_pairs={{0,2},{2,0},{1,3},{3,1},{4,6},{6,4},{5,7},{7,5},{8,10},{10,8},{9,1... | collective-permute-start | bytes 1572872 | tf_op jit(solution)/shard_map/ppermute | solution.py:20
  59.2 54.6 %collective-permute-done.swapped_ref.refs_2_ = f32[2,4,128,128]{3,2,1,0:T(8,128)S(1)} collective-permute-done((f32[2,4,128,128]{3,2,1,0:T(8,128)S(1)}, f32[2,4,128,128]{3,2,1,0:T(8,128)S(1)}, u32[]{:S(2)}, u32[]{:S(2)}) %collective-permute-start) | collective-permute-done | bytes 524320 | tf_op jit(solution)/shard_map/ppermute | solution.py:20
  113.8 3.9 %all-to-all-done.1.got_ref = f32[16,32,8,128]{3,2,1,0:T(8,128)S(1)} async-done(((f32[16,32,8,128]{3,2,1,0:T(8,128)}), f32[16,32,8,128]{3,2,1,0:T(8,128)S(1)}, u32[]{:S(2)}, u32[]{:S(2)}) %all-to-all-start.1) | async-done | bytes 2097184 | tf_op jit(solution)/shard_map/all_to_all | solution.py:24
  117.7 1.2 copy-done.1
  118.9 2.4 shard_map.94.refs_3_
  121.2 2.6 %collective-permute-start.6 = (f32[2,128,256]{2,1,0:T(8,128)S(1)}, f32[2,128,256]{2,1,0:T(8,128)S(1)}, u32[]{:S(2)}, u32[]{:S(2)}) collective-permute-start(f32[2,128,256]{2,1,0:T(8,128)S(1)} %shard_map.94.refs_3_), channel_id=1, source_target_pairs={{0,1},{1,0},{2,3},{3,2},{4,5},{5,4},{6,7},{7,6},{8,9},{9,8},{10,11... | collective-permute-start | bytes 786440 | tf_op jit(solution)/shard_map/ppermute | solution.py:20
  123.9 0.1 collective-permute-start.7
  124.0 1.2 collective-permute-done.7
  125.3 1.2 copy-done.2
  126.5 0.9 copy-done.3
  127.4 4.5 %shard_map.95 = (f32[128,256]{1,0:T(8,128)}, f32[16,38,8,128]{3,2,1,0:T(8,128)S(1)}) custom-call(s32[2]{0:T(128)S(1)} %pad_add_fusion.where_ref.refs_0_, f32[4,4,128,128]{3,2,1,0:T(8,128)S(1)} %copy-done.2, f32[2,4,128,128]{3,2,1,0:T(8,128)S(1)} %collective-permute-done.swapped_ref.refs_2_, f32[2,128,256]{2,1,0:T(8,128)S(1)} %shard_map.94.refs_3_, ...), custom_call_target="tpu_custom_call" | custom-call | flops 1405306368 | bytes 5242880 | tf_op jit(solution)/shard_map/pallas_call | solution.py:208
  131.9 66.5 %all_to_all.21.got_ref = f32[16,38,8,128]{3,2,1,0:T(8,128)S(1)} all-to-all(f32[16,38,8,128]{3,2,1,0:T(8,128)S(1)} %get-tuple-element.9), channel_id=1, replica_groups=mesh['x'=4,'zl'=4,'y'=4,'zh'=2,'c'=2] {'zl','y'}, dimensions={0} | all-to-all | bytes 4980736 | tf_op jit(solution)/shard_map/all_to_all | solution.py:24
  198.4 2.6 %shard_map.96 = (f32[280,8,128]{2,1,0:T(8,128)S(1)}, f32[280,8,128]{2,1,0:T(8,128)S(1)}) custom-call(s32[256]{0:T(256)S(1)} %fusion.6.index_ref, s32[2]{0:T(128)S(1)} %pad_add_fusion.where_ref.refs_0_, f32[16,38,8,128]{3,2,1,0:T(8,128)S(1)} %all_to_all.21.got_ref), custom_call_target="tpu_custom_call" | custom-call | bytes 5242880 | tf_op jit(solution)/shard_map/pallas_call | solution.py:219
  201.0 2.5 collective-permute-start.8
  203.5 2.4 collective-permute-done.8
  205.9 0.1 add.56
  206.1 0.1 collective-permute-start.11
  206.2 1.5 collective-permute-start.10
  207.7 1.2 collective-permute-start.9
  208.9 12.7 %collective-permute-done.11 = f32[70,8,128]{2,1,0:T(8,128)S(1)} collective-permute-done((f32[70,8,128]{2,1,0:T(8,128)S(1)}, f32[70,8,128]{2,1,0:T(8,128)S(1)}, u32[]{:S(2)}, u32[]{:S(2)}) %collective-permute-start.11) | collective-permute-done | bytes 286752 | tf_op jit(solution)/shard_map/ppermute | solution.py:20
  221.6 0.3 collective-permute-done.9
  222.1 4.3 %collective-permute-start.12 = (f32[38,8,128]{2,1,0:T(8,128)S(1)}, f32[38,8,128]{2,1,0:T(8,128)S(1)}, u32[]{:S(2)}, u32[]{:S(2)}) collective-permute-start(f32[38,8,128]{2,1,0:T(8,128)S(1)} %pad_maximum_fusion.3), channel_id=1, source_target_pairs={{0,2},{2,0},{1,3},{3,1},{4,6},{6,4},{5,7},{7,5},{8,10},{10,8},{9,1... | collective-permute-start | bytes 466952 | tf_op jit(solution)/shard_map/ppermute | solution.py:20
  226.4 3.9 %collective-permute-done.12 = f32[38,8,128]{2,1,0:T(8,128)S(1)} collective-permute-done((f32[38,8,128]{2,1,0:T(8,128)S(1)}, f32[38,8,128]{2,1,0:T(8,128)S(1)}, u32[]{:S(2)}, u32[]{:S(2)}) %collective-permute-start.12) | collective-permute-done | bytes 155680 | tf_op jit(solution)/shard_map/ppermute | solution.py:20
  230.3 0.8 pad_maximum_fusion.1
  231.1 7.8 %all-to-all-start.3 = ((f32[16,6,8,128]{3,2,1,0:T(8,128)}), f32[16,6,8,128]{3,2,1,0:T(8,128)S(1)}, u32[]{:S(2)}, u32[]{:S(2)}) async-start(f32[16,6,8,128]{3,2,1,0:T(8,128)} %pad_maximum_fusion.1), calls=%async_computation.3 | async-start | bytes 786432 | tf_op jit(solution)/shard_map/all_to_all | solution.py:24
  238.9 11.1 %all-to-all-done.3 = f32[16,6,8,128]{3,2,1,0:T(8,128)S(1)} async-done(((f32[16,6,8,128]{3,2,1,0:T(8,128)}), f32[16,6,8,128]{3,2,1,0:T(8,128)S(1)}, u32[]{:S(2)}, u32[]{:S(2)}) %all-to-all-start.3) | async-done | bytes 393248 | tf_op jit(solution)/shard_map/all_to_all | solution.py:24
  250.0 3.1 %collective-permute-start.13 = (f32[128,128]{1,0:T(8,128)S(1)}, f32[128,128]{1,0:T(8,128)S(1)}, u32[]{:S(2)}, u32[]{:S(2)}) collective-permute-start(f32[128,128]{1,0:T(8,128)S(1)} %get-tuple-element.18), channel_id=1, source_target_pairs={{0,1},{1,0},{2,3},{3,2},{4,5},{5,4},{6,7},{7,6},{8,9},{9,8},{10,11... | collective-permute-start | bytes 196616 | tf_op jit(solution)/shard_map/ppermute | solution.py:20
  253.1 0.6 slice.69
  253.7 0.7 slice.68
  254.4 0.7 maximum_select_fusion.1
  (37 shorter events, 0.7 us)
Async XLA Ops:
  0.6 1.1 copy-start
  21.4 7.8 %collective-permute-start.4 = (f32[64,8,128]{2,1,0:T(8,128)S(1)}, f32[64,8,128]{2,1,0:T(8,128)S(1)}, u32[]{:S(2)}, u32[]{:S(2)}) collective-permute-start(f32[64,8,128]{2,1,0:T(8,128)S(1)} %bitcast.34), channel_id=1, source_target_pairs={{0,192},{64,0},{128,64},{192,128},{1,193},{65,1},{129,65},{193,129... | collective-permute-start | bytes 786440 | tf_op jit(solution)/shard_map/ppermute | solution.py:20
  24.0 6.8 %collective-permute-start.3 = (f32[64,8,128]{2,1,0:T(8,128)S(1)}, f32[64,8,128]{2,1,0:T(8,128)S(1)}, u32[]{:S(2)}, u32[]{:S(2)}) collective-permute-start(f32[64,8,128]{2,1,0:T(8,128)S(1)} %bitcast.35), channel_id=1, source_target_pairs={{0,128},{64,192},{128,0},{192,64},{1,129},{65,193},{129,1},{193,65... | collective-permute-start | bytes 786440 | tf_op jit(solution)/shard_map/ppermute | solution.py:20
  24.5 14.5 %collective-permute-start.2 = (f32[64,8,128]{2,1,0:T(8,128)S(1)}, f32[64,8,128]{2,1,0:T(8,128)S(1)}, u32[]{:S(2)}, u32[]{:S(2)}) collective-permute-start(f32[64,8,128]{2,1,0:T(8,128)S(1)} %bitcast.36), channel_id=1, source_target_pairs={{0,64},{64,128},{128,192},{192,0},{1,65},{65,129},{129,193},{193,1... | collective-permute-start | bytes 786440 | tf_op jit(solution)/shard_map/ppermute | solution.py:20
  39.0 7.7 %collective-permute-start.5 = (f32[256,8,128]{2,1,0:T(8,128)S(1)}, f32[256,8,128]{2,1,0:T(8,128)S(1)}, u32[]{:S(2)}, u32[]{:S(2)}) collective-permute-start(f32[256,8,128]{2,1,0:T(8,128)S(1)} %pad_maximum_fusion.near_ref), channel_id=1, source_target_pairs={{0,1},{1,0},{2,3},{3,2},{4,5},{5,4},{6,7},{7,6},{8,9},{9,8},{10,11... | collective-permute-start | bytes 3145736 | tf_op jit(solution)/shard_map/ppermute | solution.py:20
  40.1 6.4 %collective-permute-start.1 = (f32[16,16]{0,1:T(8,128)S(1)}, f32[16,16]{0,1:T(8,128)S(1)}, u32[]{:S(2)}, u32[]{:S(2)}) collective-permute-start(f32[16,16]{0,1:T(8,128)S(1)} %bitcast.44), channel_id=1, source_target_pairs={{0,2},{2,0},{1,3},{3,1},{4,6},{6,4},{5,7},{7,5},{8,10},{10,8},{9,1... | collective-permute-start | bytes 3080 | tf_op jit(solution)/shard_map/ppermute | solution.py:20
  49.4 68.3 %all-to-all-start.1 = ((f32[16,32,8,128]{3,2,1,0:T(8,128)}), f32[16,32,8,128]{3,2,1,0:T(8,128)S(1)}, u32[]{:S(2)}, u32[]{:S(2)}) async-start(f32[16,32,8,128]{3,2,1,0:T(8,128)} %shard_map.93), calls=%async_computation.1 | async-start | bytes 4194304 | tf_op jit(solution)/shard_map/all_to_all | solution.py:24
  53.7 70.1 %copy-start.5 = (f32[128,256]{1,0:T(8,128)S(1)}, f32[128,256]{1,0:T(8,128)}, u32[]{:S(2)}) copy-start(f32[128,256]{1,0:T(8,128)} %param.11) | copy-start | bytes 393220
  53.7 71.5 %copy-start.4 = (f32[256]{0:T(256)S(1)}, f32[256]{0:T(256)}, u32[]{:S(2)}) copy-start(f32[256]{0:T(256)} %param.10) | copy-start | bytes 3076
  54.9 58.9 %collective-permute-start = (f32[2,4,128,128]{3,2,1,0:T(8,128)S(1)}, f32[2,4,128,128]{3,2,1,0:T(8,128)S(1)}, u32[]{:S(2)}, u32[]{:S(2)}) collective-permute-start(f32[2,4,128,128]{3,2,1,0:T(8,128)S(1)} %constant_dynamic-slice_fusion.3), channel_id=1, source_target_pairs={{0,2},{2,0},{1,3},{3,1},{4,6},{6,4},{5,7},{7,5},{8,10},{10,8},{9,1... | collective-permute-start | bytes 1572872 | tf_op jit(solution)/shard_map/ppermute | solution.py:20
  117.7 1.2 copy-start.1
  121.2 4.0 %collective-permute-start.6 = (f32[2,128,256]{2,1,0:T(8,128)S(1)}, f32[2,128,256]{2,1,0:T(8,128)S(1)}, u32[]{:S(2)}, u32[]{:S(2)}) collective-permute-start(f32[2,128,256]{2,1,0:T(8,128)S(1)} %shard_map.94.refs_3_), channel_id=1, source_target_pairs={{0,1},{1,0},{2,3},{3,2},{4,5},{5,4},{6,7},{7,6},{8,9},{9,8},{10,11... | collective-permute-start | bytes 786440 | tf_op jit(solution)/shard_map/ppermute | solution.py:20
  123.9 1.3 collective-permute-start.7
  125.3 1.2 copy-start.2
  126.5 0.9 copy-start.3
  201.0 4.9 %collective-permute-start.8 = (f32[280,8,128]{2,1,0:T(8,128)S(1)}, f32[280,8,128]{2,1,0:T(8,128)S(1)}, u32[]{:S(2)}, u32[]{:S(2)}) collective-permute-start(f32[280,8,128]{2,1,0:T(8,128)S(1)} %get-tuple-element.11), channel_id=1, source_target_pairs={{0,1},{1,0},{2,3},{3,2},{4,5},{5,4},{6,7},{7,6},{8,9},{9,8},{10,11... | collective-permute-start | bytes 3440648 | tf_op jit(solution)/shard_map/ppermute | solution.py:20
  206.1 15.5 %collective-permute-start.11 = (f32[70,8,128]{2,1,0:T(8,128)S(1)}, f32[70,8,128]{2,1,0:T(8,128)S(1)}, u32[]{:S(2)}, u32[]{:S(2)}) collective-permute-start(f32[70,8,128]{2,1,0:T(8,128)S(1)} %get-tuple-element.13), channel_id=1, source_target_pairs={{0,64},{64,128},{128,192},{192,0},{1,65},{65,129},{129,193},{193,1... | collective-permute-start | bytes 860168 | tf_op jit(solution)/shard_map/ppermute | solution.py:20
  206.2 15.4 %collective-permute-start.10 = (f32[70,8,128]{2,1,0:T(8,128)S(1)}, f32[70,8,128]{2,1,0:T(8,128)S(1)}, u32[]{:S(2)}, u32[]{:S(2)}) collective-permute-start(f32[70,8,128]{2,1,0:T(8,128)S(1)} %get-tuple-element.14), channel_id=1, source_target_pairs={{0,128},{64,192},{128,0},{192,64},{1,129},{65,193},{129,1},{193,65... | collective-permute-start | bytes 860168 | tf_op jit(solution)/shard_map/ppermute | solution.py:20
  207.7 14.2 %collective-permute-start.9 = (f32[70,8,128]{2,1,0:T(8,128)S(1)}, f32[70,8,128]{2,1,0:T(8,128)S(1)}, u32[]{:S(2)}, u32[]{:S(2)}) collective-permute-start(f32[70,8,128]{2,1,0:T(8,128)S(1)} %get-tuple-element.12), channel_id=1, source_target_pairs={{0,192},{64,0},{128,64},{192,128},{1,193},{65,1},{129,65},{193,129... | collective-permute-start | bytes 860168 | tf_op jit(solution)/shard_map/ppermute | solution.py:20
  222.1 8.2 %collective-permute-start.12 = (f32[38,8,128]{2,1,0:T(8,128)S(1)}, f32[38,8,128]{2,1,0:T(8,128)S(1)}, u32[]{:S(2)}, u32[]{:S(2)}) collective-permute-start(f32[38,8,128]{2,1,0:T(8,128)S(1)} %pad_maximum_fusion.3), channel_id=1, source_target_pairs={{0,2},{2,0},{1,3},{3,1},{4,6},{6,4},{5,7},{7,5},{8,10},{10,8},{9,1... | collective-permute-start | bytes 466952 | tf_op jit(solution)/shard_map/ppermute | solution.py:20
  231.1 18.9 %all-to-all-start.3 = ((f32[16,6,8,128]{3,2,1,0:T(8,128)}), f32[16,6,8,128]{3,2,1,0:T(8,128)S(1)}, u32[]{:S(2)}, u32[]{:S(2)}) async-start(f32[16,6,8,128]{3,2,1,0:T(8,128)} %pad_maximum_fusion.1), calls=%async_computation.3 | async-start | bytes 786432 | tf_op jit(solution)/shard_map/all_to_all | solution.py:24
  250.0 4.4 %collective-permute-start.13 = (f32[128,128]{1,0:T(8,128)S(1)}, f32[128,128]{1,0:T(8,128)S(1)}, u32[]{:S(2)}, u32[]{:S(2)}) collective-permute-start(f32[128,128]{1,0:T(8,128)S(1)} %get-tuple-element.18), channel_id=1, source_target_pairs={{0,1},{1,0},{2,3},{3,2},{4,5},{5,4},{6,7},{7,6},{8,9},{9,8},{10,11... | collective-permute-start | bytes 196616 | tf_op jit(solution)/shard_map/ppermute | solution.py:20

commit v2 on v1

--- a/solution.py
+++ b/solution.py
@@ -9,7 +9,7 @@
 from jax.sharding import PartitionSpec as P
 
 AXES = ("x", "zl", "y", "zh", "c")
-PLANE = ("zl", "y")
+PLANE = ("x", "y")
 TOP = lax.Precision.HIGHEST
 F32 = jnp.float32
 LIMIT = 48 * 1024 * 1024
@@ -18,6 +18,14 @@
 def shift(value, axis, steps):
     count = lax.axis_size(axis)
     return lax.ppermute(value, axis, [(s, (s + steps) % count) for s in range(count)])
+
+
+def ring(value, steps):
+    pairs = []
+    for s in range(8):
+        d = (s + steps) % 8
+        pairs.append(((s % 4) * 2 + s // 4, (d % 4) * 2 + d // 4))
+    return lax.ppermute(value, ("zl", "zh"), pairs)
 
 
 def plane_exchange(value):
@@ -65,7 +73,7 @@
     def one(source, carry):
         for slot in range(16):
             row = index_ref[source * 16 + slot]
-            spot = row + 6 * (row // 64)
+            spot = row + 6 * (row // 64) + 6
             keep_ref[spot] += got_ref[source, 2 * slot + core]
             send_ref[spot] += got_ref[source, 2 * slot + 1 - core]
         return carry
@@ -74,8 +82,8 @@
     for part in range(6):
         total = jnp.sum(got_ref[:, 32 + part], axis=0)
         for plane in range(4):
-            keep_ref[plane * 70 + 64 + part] = total
-            send_ref[plane * 70 + 64 + part] = total
+            keep_ref[plane * 70 + part] = total
+            send_ref[plane * 70 + part] = total
 
 
 def dot(a, b):
@@ -96,14 +104,15 @@
     )
 
 
-def forward_kernel(where_ref, own_ref, swapped_ref, got_ref, out_ref):
+def forward_kernel(where_ref, own_ref, first_ref, second_ref, got_ref, out_ref):
+    swapped = (first_ref, second_ref)
     half = where_ref[1]
     for block in range(2):
         total = [jnp.zeros((128, 128), F32), jnp.zeros((128, 128), F32)]
         for source in range(2):
             for k in range(4):
                 slot = block * 8 + source * 4 + k
-                tile = own_ref[2 * half + block, k] if source == 0 else swapped_ref[block, k]
+                tile = own_ref[2 * half + block, k] if source == 0 else swapped[block][k]
                 for h in range(2):
                     total[h] += dot(tile, got_ref[:, 2 * slot + h].reshape(128, 128))
         for h in range(2):
@@ -114,7 +123,8 @@
     scale,
     where_ref,
     own_ref,
-    swapped_ref,
+    first_ref,
+    second_ref,
     mine_ref,
     other_ref,
     cot_ref,
@@ -125,6 +135,7 @@
 ):
     core = where_ref[0]
     half = where_ref[1]
+    swapped = (first_ref, second_ref)
     for block in range(2):
         hidden = mine_ref[block] + other_ref[block]
         pre = dot(hidden, weight_ref[...]) + bias_ref[...]
@@ -150,7 +161,7 @@
         for source in range(2):
             for k in range(4):
                 slot = block * 8 + source * 4 + k
-                tile = own_ref[2 * half + block, k] if source == 0 else swapped_ref[block, k]
+                tile = own_ref[2 * half + block, k] if source == 0 else swapped[block][k]
                 term = dot_first(tile, grad_hidden)
                 for h in range(2):
                     out_ref[:, 2 * slot + h] = term[:, 128 * h : 128 * (h + 1)].reshape(
@@ -159,13 +170,16 @@
 
 
 def body(node_feats, operator_tiles, tile_cols, weight, layer_bias, cotangent):
-    x = lax.axis_index("x")
+    level = lax.axis_index("zl")
     half = lax.axis_index("zh")
     core = lax.axis_index("c")
     where = jnp.stack([core, half]).astype(jnp.int32)
     scale = 1.0 / math.sqrt(32768)
 
-    swapped = shift(lax.dynamic_slice_in_dim(operator_tiles, 2 * (1 - half), 2, 0), "zh", 1)
+    def theirs(block):
+        return lax.dynamic_index_in_dim(operator_tiles, 2 * (1 - half) + block, 0, keepdims=False)
+
+    first = shift(theirs(0), "zh", 1)
     cot_other = shift(cotangent, "c", 1)
     cots = jnp.where(
         core == 0, jnp.stack([cotangent, cot_other]), jnp.stack([cot_other, cotangent])
@@ -176,15 +190,22 @@
     wanted = jnp.pad(tile_cols.astype(F32).reshape(1, 16), ((0, 7), (0, 112)))
     wanted = jnp.broadcast_to(wanted[None, None], (16, 1, 8, 128))
     arrived = plane_exchange(jnp.concatenate([chunks, wanted], axis=1))
+    arrived, first = lax.optimization_barrier((arrived, first))
     plane = arrived[:, :4].reshape(64, 8, 128)
-    near = jnp.concatenate([plane] + [shift(plane, "x", d) for d in (1, 2, 3)], axis=0)
+    near = jnp.concatenate(
+        [plane, ring(plane, -1), ring(plane[:32], -2), ring(plane[32:], 2), ring(plane, 1)], axis=0
+    )
+    near, leaving = lax.optimization_barrier((near, theirs(1)))
+    second = shift(leaving, "zh", 1)
     far = shift(near, "c", 1)
 
     asked = arrived[:, 4, 0, :16]
     asked_other = shift(asked, "zh", 1)
     asked = jnp.stack([asked.reshape(16, 4, 4), asked_other.reshape(16, 4, 4)], axis=2)
     asked = lax.dynamic_slice_in_dim(asked, 2 * half, 2, 1).reshape(256).astype(jnp.int32)
-    index = jnp.mod(x - asked // 64, 4) * 64 + asked % 64
+    owner = asked // 4
+    spot = (owner // 16 * 4 + owner % 4) * 4 + asked % 4
+    index = jnp.mod(owner // 4 % 4 - level, 4) * 64 + spot
 
     sent = call(
         gather_kernel,
@@ -196,10 +217,10 @@
     mine = call(
         forward_kernel,
         jax.ShapeDtypeStruct((2, 128, 256), F32),
-        [smem(), vmem(), vmem(), vmem()],
+        [smem(), vmem(), vmem(), vmem(), vmem()],
         flops=134217728 * 6,
         moved=4 << 20,
-    )(where, operator_tiles, swapped, got)
+    )(where, operator_tiles, first, second, got)
     other = shift(mine, "c", 1)
 
     def middle(*refs):
@@ -211,10 +232,10 @@
             jax.ShapeDtypeStruct((128, 256), F32),
             jax.ShapeDtypeStruct((16, 38, 8, 128), F32),
         ),
-        [smem()] + [vmem()] * 7,
+        [smem()] + [vmem()] * 8,
         flops=234217728 * 6,
         moved=5 << 20,
-    )(where, operator_tiles, swapped, mine, other, cots, weight, layer_bias.reshape(1, 256))
+    )(where, operator_tiles, first, second, mine, other, cots, weight, layer_bias.reshape(1, 256))
     back = plane_exchange(terms)
     keep, send = call(
         scatter_kernel,
@@ -226,14 +247,13 @@
         moved=5 << 20,
     )(index, where, back)
     table = (keep + shift(send, "c", 1)).reshape(4, 70, 8, 128)
-    total = table[0]
-    for d in (1, 2, 3):
-        total = total + shift(table[d], "x", -d)
-    by_owner = total[:64].reshape(16, 4, 8, 128)
+    total = table[0] + ring(table[1], 1) + ring(table[3], -1)
+    total = total + jnp.concatenate([ring(table[2, :38], 2), ring(table[2, 38:], -2)], axis=0)
+    by_owner = total[6:].reshape(16, 4, 8, 128)
     staying = lax.dynamic_slice_in_dim(by_owner, 2 * half, 2, 1).reshape(32, 8, 128)
     leaving = lax.dynamic_slice_in_dim(by_owner, 2 * (1 - half), 2, 1).reshape(32, 8, 128)
-    final = jnp.concatenate([staying, total[64:]], axis=0) + shift(
-        jnp.concatenate([leaving, total[64:]], axis=0), "zh", 1
+    final = jnp.concatenate([staying, total[:6]], axis=0) + shift(
+        jnp.concatenate([leaving, total[:6]], axis=0), "zh", 1
     )
     home = plane_exchange(
         jnp.concatenate(

time: 256 us -> 199 us (0.78)
  blocking collectives: 86.1 us -> 34.4 us
  waiting for transfers between devices: 106 us -> 78.9 us
  starting transfers between devices: 40.5 us -> 59.3 us
  local copies, waits for them, and re-layouts: 6.68 us -> 9.98 us
    ppermute x14 -> x9, waiting for transfers between devices: 91.2 us -> 37.7 us  [shift(): lax.ppermute(value, axis, [(s, (s + steps) % count) for s in range(count)])]
    all_to_all x2 -> x1, blocking collectives: 86.1 us -> 34.4 us  [plane_exchange(): return lax.all_to_all(value, PLANE, 0, 0, tiled=True)]
    ppermute x0 -> x8, waiting for transfers between devices: none -> 17.9 us  [ring(): return lax.ppermute(value, ('zl', 'zh'), pairs)]
    ppermute x0 -> x8, starting transfers between devices: none -> 16.8 us  [ring(): return lax.ppermute(value, ('zl', 'zh'), pairs)]
    all_to_all x2 -> x3, waiting for transfers between devices: 15 us -> 23.3 us  [plane_exchange(): return lax.all_to_all(value, PLANE, 0, 0, tiled=True)]
    all_to_all x2 -> x3, starting transfers between devices: 12.1 us -> 18 us  [plane_exchange(): return lax.all_to_all(value, PLANE, 0, 0, tiled=True)]
    ppermute x14 -> x9, starting transfers between devices: 28.4 us -> 24.5 us  [shift(): lax.ppermute(value, axis, [(s, (s + steps) % count) for s in range(count)])]
  transfers between devices with their start and end apart: 16 -> 20, of which waited for: 12 -> 12; matrix products, arithmetic and copies ran while one was open for 1% -> 3% of each run, Pallas kernels for 0% -> 0%
where the time goes in v2:
time: 199 us; the launch traced here: 198 us
  waiting for transfers between devices  78.9 us (40%)
  starting transfers between devices  59.3 us (30%)
  blocking collectives  34.4 us (17%)
  Pallas kernels  12.3 us (6%)
  local copies, waits for them, and re-layouts  9.98 us (5%)
  other arithmetic  2.59 us (1%)
    ppermute x9, waiting for transfers between devices, shift(): lax.ppermute(value, axis, [(s, (s + steps) % count) for s in range(count)])  37.7 us
    all_to_all x1, blocking collectives, plane_exchange(): return lax.all_to_all(value, PLANE, 0, 0, tiled=True)  34.4 us
    ppermute x9, starting transfers between devices, shift(): lax.ppermute(value, axis, [(s, (s + steps) % count) for s in range(count)])  24.5 us
    all_to_all x3, waiting for transfers between devices, plane_exchange(): return lax.all_to_all(value, PLANE, 0, 0, tiled=True)  23.3 us
    all_to_all x3, starting transfers between devices, plane_exchange(): return lax.all_to_all(value, PLANE, 0, 0, tiled=True)  18 us
    ppermute x8, waiting for transfers between devices, ring(): return lax.ppermute(value, ('zl', 'zh'), pairs)  17.9 us
    ppermute x8, starting transfers between devices, ring(): return lax.ppermute(value, ('zl', 'zh'), pairs)  16.8 us
    pallas_call x1, Pallas kernels, body(): call(middle, (jax.ShapeDtypeStruct((128, 256), F32), jax.ShapeDtypeStruct...  4.64 us
  transfers between devices with their start and end apart: 20, of which 12 were waited for; matrix products, arithmetic and copies ran while one was open for 3% of the time, Pallas kernels for 0%

profile of v2, /device:TPU:1, one launch (start us, length us, event | category | flops | bytes accessed | tf_op | source)
XLA Modules:
  0.0 198.5 jit_solution(7826299745701338078)
XLA Ops:
  0.7 0.7 convert_element_type.11
  1.5 0.2 copy-done
  1.8 0.7 copy.18
  2.5 7.6 %all-to-all-start = ((f32[16,5,8,128]{3,2,1,0:T(8,128)}), f32[16,5,8,128]{3,2,1,0:T(8,128)S(1)}, u32[]{:S(2)}, u32[]{:S(2)}) async-start(f32[16,5,8,128]{3,2,1,0:T(8,128)} %copy.18), calls=%async_computation | async-start | bytes 655360 | tf_op jit(solution)/shard_map/all_to_all | solution.py:32
  10.1 0.7 dynamic-slice_bitcast_fusion
  10.9 6.9 %collective-permute-start = (f32[4,128,128]{2,1,0:T(8,128)S(1)}, f32[4,128,128]{2,1,0:T(8,128)S(1)}, u32[]{:S(2)}, u32[]{:S(2)}) collective-permute-start(f32[4,128,128]{2,1,0:T(8,128)S(1)} %get-tuple-element.25), channel_id=1, source_target_pairs={{0,2},{2,0},{1,3},{3,1},{4,6},{6,4},{5,7},{7,5},{8,10},{10,8},{9,1... | collective-permute-start | bytes 786440 | tf_op jit(solution)/shard_map/ppermute | solution.py:20
  17.8 6.7 %collective-permute-done.first_ref.refs_2_ = f32[4,128,128]{2,1,0:T(8,128)S(1)} collective-permute-done((f32[4,128,128]{2,1,0:T(8,128)S(1)}, f32[4,128,128]{2,1,0:T(8,128)S(1)}, u32[]{:S(2)}, u32[]{:S(2)}) %collective-permute-start) | collective-permute-done | bytes 262176 | tf_op jit(solution)/shard_map/ppermute | solution.py:20
  24.5 6.7 %collective-permute-start.1 = (f32[64,8,128]{2,1,0:T(8,128)S(1)}, f32[64,8,128]{2,1,0:T(8,128)S(1)}, u32[]{:S(2)}, u32[]{:S(2)}) collective-permute-start(f32[64,8,128]{2,1,0:T(8,128)S(1)} %bitcast.47), channel_id=1, source_target_pairs={{0,50},{16,0},{32,16},{48,32},{2,48},{18,2},{34,18},{50,34},{1,51}... | collective-permute-start | bytes 786440 | tf_op jit(solution)/shard_map/ppermute | solution.py:28
  31.2 3.0 %collective-permute-start.2 = (f32[32,8,128]{2,1,0:T(8,128)S(1)}, f32[32,8,128]{2,1,0:T(8,128)S(1)}, u32[]{:S(2)}, u32[]{:S(2)}) collective-permute-start(f32[32,8,128]{2,1,0:T(8,128)S(1)} %bitcast.58), channel_id=1, source_target_pairs={{0,34},{16,50},{32,0},{48,16},{2,32},{18,48},{34,2},{50,18},{1,35}... | collective-permute-start | bytes 393224 | tf_op jit(solution)/shard_map/ppermute | solution.py:28
  34.3 1.1 collective-permute-start.4
  35.4 0.4 collective-permute-done.1
  35.8 4.9 %collective-permute-done.2 = f32[32,8,128]{2,1,0:T(8,128)S(1)} collective-permute-done((f32[32,8,128]{2,1,0:T(8,128)S(1)}, f32[32,8,128]{2,1,0:T(8,128)S(1)}, u32[]{:S(2)}, u32[]{:S(2)}) %collective-permute-start.2) | collective-permute-done | bytes 131104 | tf_op jit(solution)/shard_map/ppermute | solution.py:28
  40.7 3.1 %collective-permute-done.3 = f32[32,8,128]{2,1,0:T(8,128)S(1)} collective-permute-done((f32[32,8,128]{2,1,0:T(8,128)S(1)}, f32[32,8,128]{2,1,0:T(8,128)S(1)}, u32[]{:S(2)}, u32[]{:S(2)}) %collective-permute-start.3) | collective-permute-done | bytes 131104 | tf_op jit(solution)/shard_map/ppermute | solution.py:28
  43.9 4.7 %collective-permute-start.7 = (f32[256,8,128]{2,1,0:T(8,128)S(1)}, f32[256,8,128]{2,1,0:T(8,128)S(1)}, u32[]{:S(2)}, u32[]{:S(2)}) collective-permute-start(f32[256,8,128]{2,1,0:T(8,128)S(1)} %constant_dynamic-update-slice_fusion.near_ref), channel_id=1, source_target_pairs={{0,1},{1,0},{2,3},{3,2},{4,5},{5,4},{6,7},{7,6},{8,9},{9,8},{10,11... | collective-permute-start | bytes 3145736 | tf_op jit(solution)/shard_map/ppermute | solution.py:20
  48.6 2.2 %copy.19 = f32[16,5,8,128]{0,3,2,1:T(8,128)} copy(f32[16,5,8,128]{3,2,1,0:T(8,128)S(1)} %all-to-all-done) | data formatting | bytes 655360 | tf_op jit(solution)/shard_map/optimization_barrier | solution.py:193
  50.9 0.7 slice_bitcast_fusion.3
  51.6 0.4 collective-permute-start.6
  52.0 6.0 %collective-permute-done.6 = f32[16,16]{0,1:T(8,128)S(1)} collective-permute-done((f32[16,16]{0,1:T(8,128)S(1)}, f32[16,16]{0,1:T(8,128)S(1)}, u32[]{:S(2)}, u32[]{:S(2)}) %collective-permute-start.6) | collective-permute-done | bytes 1056 | tf_op jit(solution)/shard_map/ppermute | solution.py:20
  58.3 2.6 %shard_map.93 = f32[16,32,8,128]{3,2,1,0:T(8,128)} custom-call(s32[256]{0:T(256)S(1)} %fusion.7.index_ref, s32[2]{0:T(128)S(1)} %pad_add_fusion.where_ref.refs_0_, f32[256,8,128]{2,1,0:T(8,128)S(1)} %constant_dynamic-update-slice_fusion.near_ref, f32[256,8,128]{2,1,0:T(8,128)S(1)} %collective-permute-done.7.far_ref), custom_call_target="tpu_custom_call" | custom-call | bytes 4194304 | tf_op jit(solution)/shard_map/pallas_call | solution.py:210
  60.9 6.9 %all-to-all-start.1 = ((f32[16,32,8,128]{3,2,1,0:T(8,128)}), f32[16,32,8,128]{3,2,1,0:T(8,128)S(1)}, u32[]{:S(2)}, u32[]{:S(2)}) async-start(f32[16,32,8,128]{3,2,1,0:T(8,128)} %shard_map.93), calls=%async_computation.1 | async-start | bytes 4194304 | tf_op jit(solution)/shard_map/all_to_all | solution.py:32
  67.8 0.2 collective-permute-start.5
  67.9 10.2 %collective-permute-done.5.second_ref.refs_3_ = f32[4,128,128]{2,1,0:T(8,128)S(1)} collective-permute-done((f32[4,128,128]{2,1,0:T(8,128)S(1)}, f32[4,128,128]{2,1,0:T(8,128)S(1)}, u32[]{:S(2)}, u32[]{:S(2)}) %collective-permute-start.5) | collective-permute-done | bytes 262176 | tf_op jit(solution)/shard_map/ppermute | solution.py:20
  78.1 15.2 %all-to-all-done.1.got_ref = f32[16,32,8,128]{3,2,1,0:T(8,128)S(1)} async-done(((f32[16,32,8,128]{3,2,1,0:T(8,128)}), f32[16,32,8,128]{3,2,1,0:T(8,128)S(1)}, u32[]{:S(2)}, u32[]{:S(2)}) %all-to-all-start.1) | async-done | bytes 2097184 | tf_op jit(solution)/shard_map/all_to_all | solution.py:32
  93.3 1.2 copy-done.2
  94.5 2.4 %shard_map.94.refs_4_ = f32[2,128,256]{2,1,0:T(8,128)S(1)} custom-call(s32[2]{0:T(128)S(1)} %pad_add_fusion.where_ref.refs_0_, f32[4,4,128,128]{3,2,1,0:T(8,128)S(1)} %copy-done.2, f32[4,128,128]{2,1,0:T(8,128)S(1)} %collective-permute-done.first_ref.refs_2_, f32[4,128,128]{2,1,0:T(8,128)S(1)} %collective-permute-done.5.second_ref.refs_3_, ...), custom_call_target="tpu_custom_call" | custom-call | flops 805306368 | bytes 4194304 | tf_op jit(solution)/shard_map/pallas_call | solution.py:217
  96.9 5.4 %collective-permute-start.8 = (f32[2,128,256]{2,1,0:T(8,128)S(1)}, f32[2,128,256]{2,1,0:T(8,128)S(1)}, u32[]{:S(2)}, u32[]{:S(2)}) collective-permute-start(f32[2,128,256]{2,1,0:T(8,128)S(1)} %shard_map.94.refs_4_), channel_id=1, source_target_pairs={{0,1},{1,0},{2,3},{3,2},{4,5},{5,4},{6,7},{7,6},{8,9},{9,8},{10,11... | collective-permute-start | bytes 786440 | tf_op jit(solution)/shard_map/ppermute | solution.py:20
  102.4 1.2 collective-permute-done.9
  103.7 1.2 copy-done.3
  104.9 0.9 copy-done.4
  105.9 4.6 %shard_map.95 = (f32[128,256]{1,0:T(8,128)}, f32[16,38,8,128]{3,2,1,0:T(8,128)S(1)}) custom-call(s32[2]{0:T(128)S(1)} %pad_add_fusion.where_ref.refs_0_, f32[4,4,128,128]{3,2,1,0:T(8,128)S(1)} %copy-done.3, f32[4,128,128]{2,1,0:T(8,128)S(1)} %collective-permute-done.first_ref.refs_2_, f32[4,128,128]{2,1,0:T(8,128)S(1)} %collective-permute-done.5.second_ref.refs_3_, ...), custom_call_target="tpu_custom_call" | custom-call | flops 1405306368 | bytes 5242880 | tf_op jit(solution)/shard_map/pallas_call | solution.py:229
  110.5 34.4 %all_to_all.20.got_ref = f32[16,38,8,128]{3,2,1,0:T(8,128)S(1)} all-to-all(f32[16,38,8,128]{3,2,1,0:T(8,128)S(1)} %get-tuple-element.17), channel_id=1, replica_groups=mesh['x'=4,'zl'=4,'y'=4,'zh'=2,'c'=2] {'x','y'}, dimensions={0} | all-to-all | bytes 4980736 | tf_op jit(solution)/shard_map/all_to_all | solution.py:32
  144.9 2.6 %shard_map.96 = (f32[280,8,128]{2,1,0:T(8,128)S(1)}, f32[280,8,128]{2,1,0:T(8,128)S(1)}) custom-call(s32[256]{0:T(256)S(1)} %fusion.7.index_ref, s32[2]{0:T(128)S(1)} %pad_add_fusion.where_ref.refs_0_, f32[16,38,8,128]{3,2,1,0:T(8,128)S(1)} %all_to_all.20.got_ref), custom_call_target="tpu_custom_call" | custom-call | bytes 5242880 | tf_op jit(solution)/shard_map/pallas_call | solution.py:240
  147.6 2.4 %collective-permute-start.10 = (f32[280,8,128]{2,1,0:T(8,128)S(1)}, f32[280,8,128]{2,1,0:T(8,128)S(1)}, u32[]{:S(2)}, u32[]{:S(2)}) collective-permute-start(f32[280,8,128]{2,1,0:T(8,128)S(1)} %get-tuple-element.19), channel_id=1, source_target_pairs={{0,1},{1,0},{2,3},{3,2},{4,5},{5,4},{6,7},{7,6},{8,9},{9,8},{10,11... | collective-permute-start | bytes 3440648 | tf_op jit(solution)/shard_map/ppermute | solution.py:20
  150.0 2.4 %collective-permute-done.10 = f32[280,8,128]{2,1,0:T(8,128)S(1)} collective-permute-done((f32[280,8,128]{2,1,0:T(8,128)S(1)}, f32[280,8,128]{2,1,0:T(8,128)S(1)}, u32[]{:S(2)}, u32[]{:S(2)}) %collective-permute-start.10) | collective-permute-done | bytes 1146912 | tf_op jit(solution)/shard_map/ppermute | solution.py:20
  152.6 0.4 collective-permute-start.12
  153.0 1.8 collective-permute-start.11
  154.9 1.2 collective-permute-start.13
  156.0 2.6 %collective-permute-start.14 = (f32[32,8,128]{2,1,0:T(8,128)S(1)}, f32[32,8,128]{2,1,0:T(8,128)S(1)}, u32[]{:S(2)}, u32[]{:S(2)}) collective-permute-start(f32[32,8,128]{2,1,0:T(8,128)S(1)} %slice_bitcast_fusion.2), channel_id=1, source_target_pairs={{0,34},{16,50},{32,0},{48,16},{2,32},{18,48},{34,2},{50,18},{1,35}... | collective-permute-start | bytes 393224 | tf_op jit(solution)/shard_map/ppermute | solution.py:28
  158.6 9.5 %collective-permute-done.14 = f32[32,8,128]{2,1,0:T(8,128)S(1)} collective-permute-done((f32[32,8,128]{2,1,0:T(8,128)S(1)}, f32[32,8,128]{2,1,0:T(8,128)S(1)}, u32[]{:S(2)}, u32[]{:S(2)}) %collective-permute-start.14) | collective-permute-done | bytes 131104 | tf_op jit(solution)/shard_map/ppermute | solution.py:28
  168.3 1.8 collective-permute-start.15
  170.1 11.1 %collective-permute-done.15 = f32[38,8,128]{2,1,0:T(8,128)S(1)} collective-permute-done((f32[38,8,128]{2,1,0:T(8,128)S(1)}, f32[38,8,128]{2,1,0:T(8,128)S(1)}, u32[]{:S(2)}, u32[]{:S(2)}) %collective-permute-start.15) | collective-permute-done | bytes 155680 | tf_op jit(solution)/shard_map/ppermute | solution.py:20
  181.3 0.8 pad_maximum_fusion
  182.1 3.6 %all-to-all-start.3 = ((f32[16,6,8,128]{3,2,1,0:T(8,128)}), f32[16,6,8,128]{3,2,1,0:T(8,128)S(1)}, u32[]{:S(2)}, u32[]{:S(2)}) async-start(f32[16,6,8,128]{3,2,1,0:T(8,128)} %pad_maximum_fusion), calls=%async_computation.3 | async-start | bytes 786432 | tf_op jit(solution)/shard_map/all_to_all | solution.py:32
  185.7 8.1 %all-to-all-done.3 = f32[16,6,8,128]{3,2,1,0:T(8,128)S(1)} async-done(((f32[16,6,8,128]{3,2,1,0:T(8,128)}), f32[16,6,8,128]{3,2,1,0:T(8,128)S(1)}, u32[]{:S(2)}, u32[]{:S(2)}) %all-to-all-start.3) | async-done | bytes 393248 | tf_op jit(solution)/shard_map/all_to_all | solution.py:32
  193.9 2.7 %collective-permute-start.16 = (f32[128,128]{1,0:T(8,128)S(1)}, f32[128,128]{1,0:T(8,128)S(1)}, u32[]{:S(2)}, u32[]{:S(2)}) collective-permute-start(f32[128,128]{1,0:T(8,128)S(1)} %get-tuple-element.31), channel_id=1, source_target_pairs={{0,1},{1,0},{2,3},{3,2},{4,5},{5,4},{6,7},{7,6},{8,9},{9,8},{10,11... | collective-permute-start | bytes 196616 | tf_op jit(solution)/shard_map/ppermute | solution.py:20
  196.5 0.6 slice.90
  197.1 0.7 slice.89
  197.8 0.7 maximum_select_fusion.1
  (55 shorter events, 1.2 us)
Async XLA Ops:
  0.6 1.1 copy-start
  1.7 8.4 %copy-start.1 = (f32[4,4,128,128]{3,2,1,0:T(8,128)S(1)}, f32[4,4,128,128]{3,2,1,0:T(8,128)}, u32[]{:S(2)}) copy-start(f32[4,4,128,128]{3,2,1,0:T(8,128)} %refs_1_.1) | copy-start | bytes 3145732
  2.5 22.0 %all-to-all-start = ((f32[16,5,8,128]{3,2,1,0:T(8,128)}), f32[16,5,8,128]{3,2,1,0:T(8,128)S(1)}, u32[]{:S(2)}, u32[]{:S(2)}) async-start(f32[16,5,8,128]{3,2,1,0:T(8,128)} %copy.18), calls=%async_computation | async-start | bytes 655360 | tf_op jit(solution)/shard_map/all_to_all | solution.py:32
  10.9 13.6 %collective-permute-start = (f32[4,128,128]{2,1,0:T(8,128)S(1)}, f32[4,128,128]{2,1,0:T(8,128)S(1)}, u32[]{:S(2)}, u32[]{:S(2)}) collective-permute-start(f32[4,128,128]{2,1,0:T(8,128)S(1)} %get-tuple-element.25), channel_id=1, source_target_pairs={{0,2},{2,0},{1,3},{3,1},{4,6},{6,4},{5,7},{7,5},{8,10},{10,8},{9,1... | collective-permute-start | bytes 786440 | tf_op jit(solution)/shard_map/ppermute | solution.py:20
  24.5 11.3 %collective-permute-start.1 = (f32[64,8,128]{2,1,0:T(8,128)S(1)}, f32[64,8,128]{2,1,0:T(8,128)S(1)}, u32[]{:S(2)}, u32[]{:S(2)}) collective-permute-start(f32[64,8,128]{2,1,0:T(8,128)S(1)} %bitcast.47), channel_id=1, source_target_pairs={{0,50},{16,0},{32,16},{48,32},{2,48},{18,2},{34,18},{50,34},{1,51}... | collective-permute-start | bytes 786440 | tf_op jit(solution)/shard_map/ppermute | solution.py:28
  31.2 9.5 %collective-permute-start.2 = (f32[32,8,128]{2,1,0:T(8,128)S(1)}, f32[32,8,128]{2,1,0:T(8,128)S(1)}, u32[]{:S(2)}, u32[]{:S(2)}) collective-permute-start(f32[32,8,128]{2,1,0:T(8,128)S(1)} %bitcast.58), channel_id=1, source_target_pairs={{0,34},{16,50},{32,0},{48,16},{2,32},{18,48},{34,2},{50,18},{1,35}... | collective-permute-start | bytes 393224 | tf_op jit(solution)/shard_map/ppermute | solution.py:28
  34.3 9.6 %collective-permute-start.4 = (f32[64,8,128]{2,1,0:T(8,128)S(1)}, f32[64,8,128]{2,1,0:T(8,128)S(1)}, u32[]{:S(2)}, u32[]{:S(2)}) collective-permute-start(f32[64,8,128]{2,1,0:T(8,128)S(1)} %bitcast.49), channel_id=1, source_target_pairs={{0,16},{16,32},{32,48},{48,2},{2,18},{18,34},{34,50},{50,0},{1,17}... | collective-permute-start | bytes 786440 | tf_op jit(solution)/shard_map/ppermute | solution.py:28
  35.4 8.4 %collective-permute-start.3 = (f32[32,8,128]{2,1,0:T(8,128)S(1)}, f32[32,8,128]{2,1,0:T(8,128)S(1)}, u32[]{:S(2)}, u32[]{:S(2)}) collective-permute-start(f32[32,8,128]{2,1,0:T(8,128)S(1)} %bitcast.57), channel_id=1, source_target_pairs={{0,32},{16,48},{32,2},{48,18},{2,34},{18,50},{34,0},{50,16},{1,33}... | collective-permute-start | bytes 393224 | tf_op jit(solution)/shard_map/ppermute | solution.py:28
  43.9 14.4 %collective-permute-start.7 = (f32[256,8,128]{2,1,0:T(8,128)S(1)}, f32[256,8,128]{2,1,0:T(8,128)S(1)}, u32[]{:S(2)}, u32[]{:S(2)}) collective-permute-start(f32[256,8,128]{2,1,0:T(8,128)S(1)} %constant_dynamic-update-slice_fusion.near_ref), channel_id=1, source_target_pairs={{0,1},{1,0},{2,3},{3,2},{4,5},{5,4},{6,7},{7,6},{8,9},{9,8},{10,11... | collective-permute-start | bytes 3145736 | tf_op jit(solution)/shard_map/ppermute | solution.py:20
  51.6 6.4 %collective-permute-start.6 = (f32[16,16]{0,1:T(8,128)S(1)}, f32[16,16]{0,1:T(8,128)S(1)}, u32[]{:S(2)}, u32[]{:S(2)}) collective-permute-start(f32[16,16]{0,1:T(8,128)S(1)} %get-tuple-element.20), channel_id=1, source_target_pairs={{0,2},{2,0},{1,3},{3,1},{4,6},{6,4},{5,7},{7,5},{8,10},{10,8},{9,1... | collective-permute-start | bytes 3080 | tf_op jit(solution)/shard_map/ppermute | solution.py:20
  60.9 6.9 %copy-start.6 = (f32[4,128,128]{2,1,0:T(8,128)S(1)}, f32[4,128,128]{2,1,0:T(8,128)}, u32[]{:S(2)}) copy-start(f32[4,128,128]{2,1,0:T(8,128)} %get-tuple-element.14) | copy-start | bytes 786436
  60.9 41.4 %copy-start.7 = (f32[128,256]{1,0:T(8,128)S(1)}, f32[128,256]{1,0:T(8,128)}, u32[]{:S(2)}) copy-start(f32[128,256]{1,0:T(8,128)} %param.11) | copy-start | bytes 393220
  60.9 42.8 %copy-start.5 = (f32[256]{0:T(256)S(1)}, f32[256]{0:T(256)}, u32[]{:S(2)}) copy-start(f32[256]{0:T(256)} %param.10) | copy-start | bytes 3076
  60.9 32.4 %all-to-all-start.1 = ((f32[16,32,8,128]{3,2,1,0:T(8,128)}), f32[16,32,8,128]{3,2,1,0:T(8,128)S(1)}, u32[]{:S(2)}, u32[]{:S(2)}) async-start(f32[16,32,8,128]{3,2,1,0:T(8,128)} %shard_map.93), calls=%async_computation.1 | async-start | bytes 4194304 | tf_op jit(solution)/shard_map/all_to_all | solution.py:32
  67.8 10.3 %collective-permute-start.5 = (f32[4,128,128]{2,1,0:T(8,128)S(1)}, f32[4,128,128]{2,1,0:T(8,128)S(1)}, u32[]{:S(2)}, u32[]{:S(2)}) collective-permute-start(f32[4,128,128]{2,1,0:T(8,128)S(1)} %copy-done.6), channel_id=1, source_target_pairs={{0,2},{2,0},{1,3},{3,1},{4,6},{6,4},{5,7},{7,5},{8,10},{10,8},{9,1... | collective-permute-start | bytes 786440 | tf_op jit(solution)/shard_map/ppermute | solution.py:20
  93.3 1.2 copy-start.2
  96.9 6.7 %collective-permute-start.8 = (f32[2,128,256]{2,1,0:T(8,128)S(1)}, f32[2,128,256]{2,1,0:T(8,128)S(1)}, u32[]{:S(2)}, u32[]{:S(2)}) collective-permute-start(f32[2,128,256]{2,1,0:T(8,128)S(1)} %shard_map.94.refs_4_), channel_id=1, source_target_pairs={{0,1},{1,0},{2,3},{3,2},{4,5},{5,4},{6,7},{7,6},{8,9},{9,8},{10,11... | collective-permute-start | bytes 786440 | tf_op jit(solution)/shard_map/ppermute | solution.py:20
  102.3 1.3 collective-permute-start.9
  103.7 1.2 copy-start.3
  104.9 0.9 copy-start.4
  147.6 4.8 %collective-permute-start.10 = (f32[280,8,128]{2,1,0:T(8,128)S(1)}, f32[280,8,128]{2,1,0:T(8,128)S(1)}, u32[]{:S(2)}, u32[]{:S(2)}) collective-permute-start(f32[280,8,128]{2,1,0:T(8,128)S(1)} %get-tuple-element.19), channel_id=1, source_target_pairs={{0,1},{1,0},{2,3},{3,2},{4,5},{5,4},{6,7},{7,6},{8,9},{9,8},{10,11... | collective-permute-start | bytes 3440648 | tf_op jit(solution)/shard_map/ppermute | solution.py:20
  152.6 15.6 %collective-permute-start.12 = (f32[70,8,128]{2,1,0:T(8,128)S(1)}, f32[70,8,128]{2,1,0:T(8,128)S(1)}, u32[]{:S(2)}, u32[]{:S(2)}) collective-permute-start(f32[70,8,128]{2,1,0:T(8,128)S(1)} %get-tuple-element.23), channel_id=1, source_target_pairs={{0,50},{16,0},{32,16},{48,32},{2,48},{18,2},{34,18},{50,34},{1,51}... | collective-permute-start | bytes 860168 | tf_op jit(solution)/shard_map/ppermute | solution.py:28
  153.0 15.1 %collective-permute-start.11 = (f32[70,8,128]{2,1,0:T(8,128)S(1)}, f32[70,8,128]{2,1,0:T(8,128)S(1)}, u32[]{:S(2)}, u32[]{:S(2)}) collective-permute-start(f32[70,8,128]{2,1,0:T(8,128)S(1)} %get-tuple-element.22), channel_id=1, source_target_pairs={{0,16},{16,32},{32,48},{48,2},{2,18},{18,34},{34,50},{50,0},{1,17}... | collective-permute-start | bytes 860168 | tf_op jit(solution)/shard_map/ppermute | solution.py:28
  154.9 13.3 %collective-permute-start.13 = (f32[38,8,128]{2,1,0:T(8,128)S(1)}, f32[38,8,128]{2,1,0:T(8,128)S(1)}, u32[]{:S(2)}, u32[]{:S(2)}) collective-permute-start(f32[38,8,128]{2,1,0:T(8,128)S(1)} %slice_bitcast_fusion), channel_id=1, source_target_pairs={{0,32},{16,48},{32,2},{48,18},{2,34},{18,50},{34,0},{50,16},{1,33}... | collective-permute-start | bytes 466952 | tf_op jit(solution)/shard_map/ppermute | solution.py:28
  156.0 12.1 %collective-permute-start.14 = (f32[32,8,128]{2,1,0:T(8,128)S(1)}, f32[32,8,128]{2,1,0:T(8,128)S(1)}, u32[]{:S(2)}, u32[]{:S(2)}) collective-permute-start(f32[32,8,128]{2,1,0:T(8,128)S(1)} %slice_bitcast_fusion.2), channel_id=1, source_target_pairs={{0,34},{16,50},{32,0},{48,16},{2,32},{18,48},{34,2},{50,18},{1,35}... | collective-permute-start | bytes 393224 | tf_op jit(solution)/shard_map/ppermute | solution.py:28
  168.3 12.9 %collective-permute-start.15 = (f32[38,8,128]{2,1,0:T(8,128)S(1)}, f32[38,8,128]{2,1,0:T(8,128)S(1)}, u32[]{:S(2)}, u32[]{:S(2)}) collective-permute-start(f32[38,8,128]{2,1,0:T(8,128)S(1)} %pad_maximum_fusion.2), channel_id=1, source_target_pairs={{0,2},{2,0},{1,3},{3,1},{4,6},{6,4},{5,7},{7,5},{8,10},{10,8},{9,1... | collective-permute-start | bytes 466952 | tf_op jit(solution)/shard_map/ppermute | solution.py:20
  182.1 11.7 %all-to-all-start.3 = ((f32[16,6,8,128]{3,2,1,0:T(8,128)}), f32[16,6,8,128]{3,2,1,0:T(8,128)S(1)}, u32[]{:S(2)}, u32[]{:S(2)}) async-start(f32[16,6,8,128]{3,2,1,0:T(8,128)} %pad_maximum_fusion), calls=%async_computation.3 | async-start | bytes 786432 | tf_op jit(solution)/shard_map/all_to_all | solution.py:32
  193.9 4.0 %collective-permute-start.16 = (f32[128,128]{1,0:T(8,128)S(1)}, f32[128,128]{1,0:T(8,128)S(1)}, u32[]{:S(2)}, u32[]{:S(2)}) collective-permute-start(f32[128,128]{1,0:T(8,128)S(1)} %get-tuple-element.31), channel_id=1, source_target_pairs={{0,1},{1,0},{2,3},{3,2},{4,5},{5,4},{6,7},{7,6},{8,9},{9,8},{10,11... | collective-permute-start | bytes 196616 | tf_op jit(solution)/shard_map/ppermute | solution.py:20

commit v3 on v2

v3 whole, which is shorter than its diff:
```python
import math

import jax
import jax.numpy as jnp
from jax import lax
from jax.experimental import pallas as pl
from jax.experimental.pallas import tpu as pltpu
from jax.sharding import Mesh
from jax.sharding import PartitionSpec as P

AXES = ("x", "zl", "y", "zh", "c")
PLANE = ("x", "y")
GROUP = ("x", "y", "c")
TOP = lax.Precision.HIGHEST
F32 = jnp.float32
LIMIT = 10 * 1024 * 1024


def shift(value, axis, steps):
    count = lax.axis_size(axis)
    return lax.ppermute(value, axis, [(s, (s + steps) % count) for s in range(count)])


def ring(value, steps):
    pairs = []
    for s in range(8):
        d = (s + steps) % 8
        pairs.append(((s % 4) * 2 + s // 4, (d % 4) * 2 + d // 4))
    return lax.ppermute(value, ("zl", "zh"), pairs)


def exchange(value, axes):
    return lax.all_to_all(value, axes, 0, 0, tiled=True)


def vmem():
    return pl.BlockSpec(memory_space=pltpu.VMEM)


def smem():
    return pl.BlockSpec(memory_space=pltpu.SMEM)


def call(kernel, out_shape, specs, scratch=(), flops=0, moved=0):
    return pl.pallas_call(
        kernel,
        out_shape=out_shape,
        in_specs=specs,
        out_specs=jax.tree.map(lambda _: vmem(), out_shape),
        scratch_shapes=scratch,
        compiler_params=pltpu.CompilerParams(vmem_limit_bytes=LIMIT),
        cost_estimate=pl.CostEstimate(flops=flops, bytes_accessed=moved, transcendentals=0),
    )


def pack_kernel(where_ref, rows_ref, wanted_ref, out_ref):
    for h in range(2):

        @pl.when(where_ref[0] == h)
        def _():
            for b in range(4):
                half = rows_ref[128 * b : 128 * (b + 1), 128 * h : 128 * (h + 1)]
                out_ref[:, b] = half.reshape(16, 8, 128)

    out_ref[:, 4] = jnp.broadcast_to(wanted_ref[...].reshape(1, 1, 128), (16, 8, 128))


def row_of(near_ref, far_ref, q, c, slot):
    block, source, k = slot // 8, slot // 4 % 2, slot % 4
    index_ref = far_ref if source else near_ref
    return index_ref[q, 16 * c + 8 * source + 4 * block + k]


def gather_kernel(near_ref, far_ref, table_ref, out_ref):
    def one(q, carry):
        for c in range(2):
            for slot in range(16):
                row = row_of(near_ref, far_ref, q, c, slot)
                out_ref[q * 2 + c, slot] = table_ref[row]
        return carry

    lax.fori_loop(0, 16, one, 0)


def scatter_kernel(near_ref, far_ref, got_ref, out_ref, even_ref, odd_ref):
    even_ref[...] = jnp.zeros_like(even_ref)
    odd_ref[...] = jnp.zeros_like(odd_ref)

    def one(q, carry):
        for slot in range(16):
            even_ref[row_of(near_ref, far_ref, q, 0, slot)] += got_ref[q, 0, slot]
            odd_ref[row_of(near_ref, far_ref, q, 1, slot)] += got_ref[q, 1, slot]
        return carry

    lax.fori_loop(0, 16, one, 0)
    sums = [
        jnp.sum(got_ref[:, 0, 16], axis=0),
        jnp.sum(got_ref[:, 1, 16], axis=0),
        jnp.sum(got_ref[:, 0, 17] + got_ref[:, 1, 17], axis=0),
    ]
    for plane in range(4):
        for part in range(3):
            out_ref[plane, part] = sums[part]
        rows = pl.ds(plane * 64, 64)
        out_ref[plane, 3:67] = even_ref[rows] + odd_ref[rows]


def dot(a, b):
    return lax.dot_general(
        a, b, (((1,), (0,)), ((), ())), precision=TOP, preferred_element_type=F32
    )


def dot_first(a, b):
    return lax.dot_general(
        a, b, (((0,), (0,)), ((), ())), precision=TOP, preferred_element_type=F32
    )


def dot_last(a, b):
    return lax.dot_general(
        a, b, (((1,), (1,)), ((), ())), precision=TOP, preferred_element_type=F32
    )


def tile_of(half, refs, block, source, k):
    own_ref, first_ref, second_ref = refs
    place = 4 * block + k
    if source == 0:
        return own_ref[8 * half + place]
    return first_ref[place] if place < 2 else second_ref[place - 2]


def forward_kernel(where_ref, own_ref, first_ref, second_ref, got_ref, out_ref):
    half = where_ref[1]
    for block in range(2):
        total = [jnp.zeros((128, 128), F32), jnp.zeros((128, 128), F32)]
        for source in range(2):
            for k in range(4):
                slot = block * 8 + source * 4 + k
                tile = tile_of(half, (own_ref, first_ref, second_ref), block, source, k)
                for h in range(2):
                    total[h] += dot(tile, got_ref[:, h, slot].reshape(128, 128))
        for h in range(2):
            out_ref[block, :, 128 * h : 128 * (h + 1)] = total[h]


def middle_kernel(
    scale,
    where_ref,
    own_ref,
    first_ref,
    second_ref,
    mine_ref,
    other_ref,
    cot_ref,
    cot_other_ref,
    weight_ref,
    bias_ref,
    layer_ref,
    out_ref,
):
    core = where_ref[0]
    half = where_ref[1]
    hiddens = []
    grads = []
    for block in range(2):
        hidden = mine_ref[block] + other_ref[block]
        pre = dot(hidden, weight_ref[...]) + bias_ref[...]
        grow = jnp.exp(jnp.minimum(pre, 0.0))
        layer = jnp.where(pre > 0, pre, grow - 1.0)
        cot = jnp.where(core == block, cot_ref[...], cot_other_ref[...])
        grad_pre = cot * jnp.where(pre > 0, 1.0, grow)
        grad_hidden = dot_last(grad_pre, weight_ref[...])
        hiddens.append(hidden)
        grads.append(grad_pre)

        @pl.when(core == block)
        def _():
            layer_ref[...] = layer

        for source in range(2):
            for k in range(4):
                slot = block * 8 + source * 4 + k
                tile = tile_of(half, (own_ref, first_ref, second_ref), block, source, k)
                term = dot_first(tile, grad_hidden)
                for h in range(2):
                    out_ref[:, h, slot] = term[:, 128 * h : 128 * (h + 1)].reshape(16, 8, 128)

    for h in range(2):

        @pl.when(core == h)
        def _():
            columns = slice(128 * h, 128 * (h + 1))
            grad_weight = dot_first(hiddens[0], grads[0][:, columns])
            grad_weight = (grad_weight + dot_first(hiddens[1], grads[1][:, columns])) * scale
            out_ref[:, :, 16] = grad_weight.reshape(16, 2, 8, 128)
            both = grads[0][:, columns] + grads[1][:, columns]
            grad_bias = jnp.sum(both, axis=0, keepdims=True) * scale
            rows = lax.broadcasted_iota(jnp.int32, (8, 128), 0)
            grad_bias = jnp.where(rows == h, jnp.broadcast_to(grad_bias, (8, 128)), 0.0)
            out_ref[:, :, 17] = jnp.broadcast_to(grad_bias.reshape(1, 1, 8, 128), (16, 2, 8, 128))


def body(node_feats, operator_tiles, tile_cols, weight, layer_bias, cotangent):
    level = lax.axis_index("zl")
    half = lax.axis_index("zh")
    core = lax.axis_index("c")
    where = jnp.stack([core, half]).astype(jnp.int32)
    scale = 1.0 / math.sqrt(32768)

    tiles = operator_tiles.reshape(16, 128, 128)
    first = shift(lax.dynamic_slice_in_dim(tiles, 8 * (1 - half), 2, 0), "zh", 1)
    cot_other = shift(cotangent, "c", 1)

    asked = tile_cols.reshape(2, 8)
    owner = asked // 4
    spot = (owner // 16 * 4 + owner % 4) * 4 + asked % 4
    asked = jnp.mod(owner // 4 % 4 - level, 4) * 64 + spot
    asked = jnp.where(half == 0, asked, asked[::-1]).astype(F32).reshape(1, 16)
    beside = shift(asked, "c", 1)
    wanted = jnp.where(
        core == 0,
        jnp.concatenate([asked, beside], axis=1),
        jnp.concatenate([beside, asked], axis=1),
    )
    wanted = jnp.pad(wanted, ((0, 0), (0, 96)))

    packed = call(
        pack_kernel,
        jax.ShapeDtypeStruct((16, 5, 8, 128), F32),
        [smem(), vmem(), vmem()],
        moved=1 << 20,
    )(where, node_feats, wanted)
    arrived = exchange(packed, PLANE)
    plane = arrived[:, :4].reshape(64, 8, 128)
    table = jnp.concatenate(
        [plane, ring(plane, -1), ring(plane[:32], -2), ring(plane[32:], 2), ring(plane, 1)], axis=0
    )
    asked = arrived[:, 4, 0]
    index = (asked.astype(jnp.int32), shift(asked, "zh", 1).astype(jnp.int32))

    table, leaving = lax.optimization_barrier(
        (table, lax.dynamic_slice_in_dim(tiles, 8 * (1 - half) + 2, 6, 0))
    )
    second = shift(leaving, "zh", 1)
    sent = call(
        gather_kernel,
        jax.ShapeDtypeStruct((32, 16, 8, 128), F32),
        [smem(), smem(), vmem()],
        moved=3 << 20,
    )(*index, table)
    sent, first = lax.optimization_barrier((sent, first))
    got = exchange(sent, GROUP).reshape(16, 2, 16, 8, 128)
    mine = call(
        forward_kernel,
        jax.ShapeDtypeStruct((2, 128, 256), F32),
        [smem()] + [vmem()] * 4,
        flops=134217728 * 6,
        moved=3 << 20,
    )(where, tiles, first, second, got)
    other = shift(mine, "c", 1)

    def middle(*refs):
        middle_kernel(scale, *refs)

    layer_out, terms = call(
        middle,
        (
            jax.ShapeDtypeStruct((128, 256), F32),
            jax.ShapeDtypeStruct((16, 2, 18, 8, 128), F32),
        ),
        [smem()] + [vmem()] * 9,
        flops=234217728 * 6,
        moved=4 << 20,
    )(where, tiles, first, second, mine, other, cotangent, cot_other, weight, layer_bias.reshape(1, 256))
    back = exchange(terms.reshape(32, 18, 8, 128), GROUP).reshape(16, 2, 18, 8, 128)
    sums = call(
        scatter_kernel,
        jax.ShapeDtypeStruct((4, 67, 8, 128), F32),
        [smem(), smem(), vmem()],
        scratch=[pltpu.VMEM((256, 8, 128), F32)] * 2,
        moved=4 << 20,
    )(*index, back)
    total = sums[0] + ring(sums[1], 1) + ring(sums[3], -1)
    total = total + jnp.concatenate([ring(sums[2, :35], 2), ring(sums[2, 35:], -2)], axis=0)
    by_owner = total[3:].reshape(16, 4, 8, 128)
    staying = lax.dynamic_slice_in_dim(by_owner, 2 * half, 2, 1).reshape(32, 8, 128)
    leaving = lax.dynamic_slice_in_dim(by_owner, 2 * (1 - half), 2, 1).reshape(32, 8, 128)
    final = jnp.concatenate([staying, total[:3]], axis=0) + shift(
        jnp.concatenate([leaving, total[:3]], axis=0), "zh", 1
    )
    home = exchange(
        jnp.concatenate(
            [
                final[:32, None],
                jnp.broadcast_to(final[None, 32:34], (32, 2, 8, 128)),
            ],
            axis=1,
        ),
        GROUP,
    ).reshape(16, 2, 3, 8, 128)
    grad_feats = home[:, :, 0].transpose(0, 2, 1, 3).reshape(128, 256)
    grad_weight = home[:, :, 1:].transpose(0, 1, 3, 2, 4).reshape(256, 256)
    grad_bias = final[34, :2].reshape(256)
    return layer_out, grad_feats, grad_weight, grad_bias


def solution(mesh):
    fine = Mesh(mesh.devices.reshape(4, 4, 4, 2, 2), AXES)
    blk, rep = ("x", "zl", "y"), ("zh", "c")
    return jax.shard_map(
        body,
        mesh=fine,
        in_specs=(
            P(blk, None),
            P(blk, rep, None, None),
            P(blk, rep),
            P(),
            P(),
            P(AXES, None),
        ),
        out_specs=(P(AXES, None), P(AXES, None), P(), P()),
        check_vma=False,
    )
```

time: 199 us -> 174 us (0.87)
  waiting for transfers between devices: 78.9 us -> 56.9 us
  local copies, waits for them, and re-layouts: 9.98 us -> 7.26 us
    ppermute x9 -> x7, waiting for transfers between devices: 37.7 us -> 25.6 us  [shift(): lax.ppermute(value, axis, [(s, (s + steps) % count) for s in range(count)])]
    all_to_all x3, waiting for transfers between devices: 23.3 us -> 15.1 us  [exchange(): return lax.all_to_all(value, axes, 0, 0, tiled=True)]
    ppermute x8, starting transfers between devices: 16.8 us -> 10.6 us  [ring(): return lax.ppermute(value, ('zl', 'zh'), pairs)]
    all_to_all x3, starting transfers between devices: 18 us -> 21.5 us  [exchange(): return lax.all_to_all(value, axes, 0, 0, tiled=True)]
    optimization_barrier x1 -> x0, local copies, waits for them, and re-layouts: 2.25 us -> none  [body(): arrived, first = lax.optimization_barrier((arrived, first))]
    ppermute x9 -> x7, starting transfers between devices: 24.5 us -> 26.6 us  [shift(): lax.ppermute(value, axis, [(s, (s + steps) % count) for s in range(count)])]
    pallas_call x3 -> x4, Pallas kernels: 7.65 us -> 8.53 us  [the longest x1 2.76 us: body(): call(gather_kernel, jax.ShapeDtypeStruct((32, 16, 8, 128), F32), [smem(),...]
  transfers between devices with their start and end apart: 20 -> 18, of which waited for: 12 -> 12; matrix products, arithmetic and copies ran while one was open for 3% -> 1% of each run, Pallas kernels for 0% -> 2%
where the time goes in v3:
time: 174 us
  starting transfers between devices  58.7 us (34%)
  waiting for transfers between devices  56.9 us (33%)
  blocking collectives  34.6 us (20%)
  Pallas kernels  14.1 us (8%)
  local copies, waits for them, and re-layouts  7.26 us (4%)
    all_to_all x1, blocking collectives, exchange(): return lax.all_to_all(value, axes, 0, 0, tiled=True)  34.6 us
    ppermute x7, starting transfers between devices, shift(): lax.ppermute(value, axis, [(s, (s + steps) % count) for s in range(count)])  26.6 us
    ppermute x7, waiting for transfers between devices, shift(): lax.ppermute(value, axis, [(s, (s + steps) % count) for s in range(count)])  25.6 us
    all_to_all x3, starting transfers between devices, exchange(): return lax.all_to_all(value, axes, 0, 0, tiled=True)  21.5 us
    ppermute x8, waiting for transfers between devices, ring(): return lax.ppermute(value, ('zl', 'zh'), pairs)  16.2 us
    all_to_all x3, waiting for transfers between devices, exchange(): return lax.all_to_all(value, axes, 0, 0, tiled=True)  15.1 us
    ppermute x8, starting transfers between devices, ring(): return lax.ppermute(value, ('zl', 'zh'), pairs)  10.6 us
    pallas_call x1, Pallas kernels, body(): call(middle, (jax.ShapeDtypeStruct((128, 256), F32), jax.ShapeDtypeStruct...  5.55 us
  transfers between devices with their start and end apart: 18, of which 12 were waited for; matrix products, arithmetic and copies ran while one was open for 1% of the time, Pallas kernels for 2%

profile of v3, /device:TPU:1, one launch (start us, length us, event | category | flops | bytes accessed | tf_op | source)
XLA Modules:
  0.0 173.6 jit_solution(4883584497794157011)
XLA Ops:
  0.6 0.8 reshape.112
  1.6 0.1 concatenate.39
  1.7 3.3 %collective-permute-start = (f32[1,16]{1,0:T(1,128)S(1)}, f32[1,16]{1,0:T(1,128)S(1)}, u32[]{:S(2)}, u32[]{:S(2)}) collective-permute-start(f32[1,16]{1,0:T(1,128)S(1)} %concatenate.39), channel_id=1, source_target_pairs={{0,1},{1,0},{2,3},{3,2},{4,5},{5,4},{6,7},{7,6},{8,9},{9,8},{10,11... | collective-permute-start | bytes 200 | tf_op jit(solution)/shard_map/ppermute | solution.py:21
  4.9 0.1 pad_add_fusion.where_ref.refs_0_
  5.0 0.7 collective-permute-done
  5.8 0.1 broadcast_select_fusion
  5.8 1.0 copy-done.1
  6.9 1.3 shard_map.93
  8.2 5.0 %all-to-all-start = ((f32[16,5,8,128]{3,2,1,0:T(8,128)}), f32[16,5,8,128]{3,2,1,0:T(8,128)S(1)}, u32[]{:S(2)}, u32[]{:S(2)}) async-start(f32[16,5,8,128]{3,2,1,0:T(8,128)} %shard_map.93), calls=%async_computation | async-start | bytes 655360 | tf_op jit(solution)/shard_map/all_to_all | solution.py:33
  13.3 7.0 %collective-permute-start.6 = (f32[2,128,128]{2,1,0:T(8,128)S(1)}, f32[2,128,128]{2,1,0:T(8,128)S(1)}, u32[]{:S(2)}, u32[]{:S(2)}) collective-permute-start(f32[2,128,128]{2,1,0:T(8,128)S(1)} %constant_dynamic-slice_fusion.2), channel_id=1, source_target_pairs={{0,2},{2,0},{1,3},{3,1},{4,6},{6,4},{5,7},{7,5},{8,10},{10,8},{9,1... | collective-permute-start | bytes 393224 | tf_op jit(solution)/shard_map/ppermute | solution.py:21
  20.3 0.8 constant_dynamic-slice_fusion.3
  21.0 0.2 all-to-all-done
  21.2 6.9 %collective-permute-start.1 = (f32[16,128]{1,0:T(8,128)S(1)}, f32[16,128]{1,0:T(8,128)S(1)}, u32[]{:S(2)}, u32[]{:S(2)}) collective-permute-start(f32[16,128]{1,0:T(8,128)S(1)} %bitcast.65), channel_id=1, source_target_pairs={{0,2},{2,0},{1,3},{3,1},{4,6},{6,4},{5,7},{7,5},{8,10},{10,8},{9,1... | collective-permute-start | bytes 24584 | tf_op jit(solution)/shard_map/ppermute | solution.py:21
  28.2 0.1 collective-permute-start.2
  28.3 0.1 collective-permute-start.3
  28.4 1.5 collective-permute-start.5
  29.9 2.3 %collective-permute-start.4 = (f32[32,8,128]{2,1,0:T(8,128)S(1)}, f32[32,8,128]{2,1,0:T(8,128)S(1)}, u32[]{:S(2)}, u32[]{:S(2)}) collective-permute-start(f32[32,8,128]{2,1,0:T(8,128)S(1)} %bitcast.63), channel_id=1, source_target_pairs={{0,32},{16,48},{32,2},{48,18},{2,34},{18,50},{34,0},{50,16},{1,33}... | collective-permute-start | bytes 393224 | tf_op jit(solution)/shard_map/ppermute | solution.py:29
  32.3 1.9 %collective-permute-done.2 = f32[64,8,128]{2,1,0:T(8,128)S(1)} collective-permute-done((f32[64,8,128]{2,1,0:T(8,128)S(1)}, f32[64,8,128]{2,1,0:T(8,128)S(1)}, u32[]{:S(2)}, u32[]{:S(2)}) %collective-permute-start.2) | collective-permute-done | bytes 262176 | tf_op jit(solution)/shard_map/ppermute | solution.py:29
  34.2 4.5 %collective-permute-done.3 = f32[32,8,128]{2,1,0:T(8,128)S(1)} collective-permute-done((f32[32,8,128]{2,1,0:T(8,128)S(1)}, f32[32,8,128]{2,1,0:T(8,128)S(1)}, u32[]{:S(2)}, u32[]{:S(2)}) %collective-permute-start.3) | collective-permute-done | bytes 131104 | tf_op jit(solution)/shard_map/ppermute | solution.py:29
  38.7 1.0 collective-permute-done.4
  39.7 2.8 %shard_map.94 = f32[32,16,8,128]{3,2,1,0:T(8,128)} custom-call(s32[16,128]{1,0:T(8,128)S(1)} %convert_element_type.12.near_ref, s32[16,128]{1,0:T(8,128)S(1)} %convert_element_type.13.far_ref, f32[256,8,128]{2,1,0:T(8,128)S(1)} %constant_dynamic-update-slice_fusion.table_ref), custom_call_target="tpu_custom_call" | custom-call | bytes 3145728 | tf_op jit(solution)/shard_map/pallas_call | solution.py:247
  42.5 0.7 copy-done.2
  43.1 9.1 %all-to-all-start.1 = ((f32[32,16,8,128]{3,2,1,0:T(8,128)}), f32[32,16,8,128]{3,2,1,0:T(8,128)S(1)}, u32[]{:S(2)}, u32[]{:S(2)}) async-start(f32[32,16,8,128]{3,2,1,0:T(8,128)} %shard_map.94), calls=%async_computation.1 | async-start | bytes 4194304 | tf_op jit(solution)/shard_map/all_to_all | solution.py:33
  52.2 4.3 %collective-permute-start.7 = (f32[6,128,128]{2,1,0:T(8,128)}, f32[6,128,128]{2,1,0:T(8,128)S(1)}, u32[]{:S(2)}, u32[]{:S(2)}) collective-permute-start(f32[6,128,128]{2,1,0:T(8,128)} %constant_dynamic-slice_fusion.3), channel_id=1, source_target_pairs={{0,2},{2,0},{1,3},{3,1},{4,6},{6,4},{5,7},{7,5},{8,10},{10,8},{9,1... | collective-permute-start | bytes 1179656 | tf_op jit(solution)/shard_map/ppermute | solution.py:21
  56.5 18.9 %collective-permute-done.7.second_ref.refs_3_ = f32[6,128,128]{2,1,0:T(8,128)S(1)} collective-permute-done((f32[6,128,128]{2,1,0:T(8,128)}, f32[6,128,128]{2,1,0:T(8,128)S(1)}, u32[]{:S(2)}, u32[]{:S(2)}) %collective-permute-start.7) | collective-permute-done | bytes 393248 | tf_op jit(solution)/shard_map/ppermute | solution.py:21
  75.4 5.1 %all-to-all-done.1 = f32[32,16,8,128]{3,2,1,0:T(8,128)S(1)} async-done(((f32[32,16,8,128]{3,2,1,0:T(8,128)}), f32[32,16,8,128]{3,2,1,0:T(8,128)S(1)}, u32[]{:S(2)}, u32[]{:S(2)}) %all-to-all-start.1) | async-done | bytes 2097184 | tf_op jit(solution)/shard_map/all_to_all | solution.py:33
  80.5 0.9 copy-done.3
  81.4 0.7 copy-done.5
  82.1 2.4 %shard_map.95.refs_4_ = f32[2,128,256]{2,1,0:T(8,128)S(1)} custom-call(s32[2]{0:T(128)S(1)} %copy-done.5, f32[16,128,128]{2,1,0:T(8,128)S(1)} %bitcast.51, f32[2,128,128]{2,1,0:T(8,128)S(1)} %copy-done.3, f32[6,128,128]{2,1,0:T(8,128)S(1)} %collective-permute-done.7.second_ref.refs_3_, f32[16,2,16,8,128]{4,3,2,1,0:T(8,128)S(1)} %bitcast.47), custom_call_target="tpu_custom_call" | custom-call | flops 805306368 | bytes 3145728 | tf_op jit(solution)/shard_map/pallas_call | solution.py:255
  84.4 1.0 collective-permute-start.8
  85.4 0.1 collective-permute-start.9
  85.5 1.2 collective-permute-done.9.refs_7_
  86.8 5.6 %shard_map.96 = (f32[128,256]{1,0:T(8,128)}, f32[16,2,18,8,128]{4,3,2,1,0:T(8,128)S(1)}) custom-call(s32[2]{0:T(128)S(1)} %copy-done.5, f32[16,128,128]{2,1,0:T(8,128)S(1)} %bitcast.52, f32[2,128,128]{2,1,0:T(8,128)S(1)} %copy-done.3, f32[6,128,128]{2,1,0:T(8,128)S(1)} %collective-permute-done.7.second_ref.refs_3_, f32[2,128,256]{2,1,0:T(8,128)S(1)} %shard_map.95.refs_4_, ...), custom_call_target="tpu_custom_call" | custom-call | flops 1405306368 | bytes 4194304 | tf_op jit(solution)/shard_map/pallas_call | solution.py:267
  92.3 34.6 %all_to_all.20 = f32[32,18,8,128]{3,2,1,0:T(8,128)S(1)} all-to-all(f32[32,18,8,128]{3,2,1,0:T(8,128)S(1)} %bitcast.48), channel_id=1, replica_groups=mesh['x'=4,'zl'=4,'y'=4,'zh'=2,'c'=2] {'x','y','c'}, dimensions={0} | all-to-all | bytes 4718592 | tf_op jit(solution)/shard_map/all_to_all | solution.py:33
  126.9 2.1 %shard_map.97 = f32[4,67,8,128]{3,2,1,0:T(8,128)S(1)} custom-call(s32[16,128]{1,0:T(8,128)S(1)} %convert_element_type.12.near_ref, s32[16,128]{1,0:T(8,128)S(1)} %convert_element_type.13.far_ref, f32[16,2,18,8,128]{4,3,2,1,0:T(8,128)S(1)} %bitcast.46), custom_call_target="tpu_custom_call" | custom-call | bytes 4194304 | tf_op jit(solution)/shard_map/pallas_call | solution.py:278
  129.1 2.9 %collective-permute-start.11 = (f32[67,8,128]{2,1,0:T(8,128)S(1)}, f32[67,8,128]{2,1,0:T(8,128)S(1)}, u32[]{:S(2)}, u32[]{:S(2)}) collective-permute-start(f32[67,8,128]{2,1,0:T(8,128)S(1)} %get-tuple-element.17), channel_id=1, source_target_pairs={{0,50},{16,0},{32,16},{48,32},{2,48},{18,2},{34,18},{50,34},{1,51}... | collective-permute-start | bytes 823304 | tf_op jit(solution)/shard_map/ppermute | solution.py:29
  132.0 3.6 %collective-permute-start.13 = (f32[32,8,128]{2,1,0:T(8,128)S(1)}, f32[32,8,128]{2,1,0:T(8,128)S(1)}, u32[]{:S(2)}, u32[]{:S(2)}) collective-permute-start(f32[32,8,128]{2,1,0:T(8,128)S(1)} %slice_bitcast_fusion.6), channel_id=1, source_target_pairs={{0,34},{16,50},{32,0},{48,16},{2,32},{18,48},{34,2},{50,18},{1,35}... | collective-permute-start | bytes 393224 | tf_op jit(solution)/shard_map/ppermute | solution.py:29
  135.7 8.4 %collective-permute-done.13 = f32[32,8,128]{2,1,0:T(8,128)S(1)} collective-permute-done((f32[32,8,128]{2,1,0:T(8,128)S(1)}, f32[32,8,128]{2,1,0:T(8,128)S(1)}, u32[]{:S(2)}, u32[]{:S(2)}) %collective-permute-start.13) | collective-permute-done | bytes 131104 | tf_op jit(solution)/shard_map/ppermute | solution.py:29
  144.1 0.4 collective-permute-done.12
  144.5 0.1 fusion.2
  144.7 4.1 %collective-permute-start.14 = (f32[35,8,128]{2,1,0:T(8,128)S(1)}, f32[35,8,128]{2,1,0:T(8,128)S(1)}, u32[]{:S(2)}, u32[]{:S(2)}) collective-permute-start(f32[35,8,128]{2,1,0:T(8,128)S(1)} %pad_maximum_fusion.1), channel_id=1, source_target_pairs={{0,2},{2,0},{1,3},{3,1},{4,6},{6,4},{5,7},{7,5},{8,10},{10,8},{9,1... | collective-permute-start | bytes 430088 | tf_op jit(solution)/shard_map/ppermute | solution.py:21
  148.8 4.7 %collective-permute-done.14 = f32[35,8,128]{2,1,0:T(8,128)S(1)} collective-permute-done((f32[35,8,128]{2,1,0:T(8,128)S(1)}, f32[35,8,128]{2,1,0:T(8,128)S(1)}, u32[]{:S(2)}, u32[]{:S(2)}) %collective-permute-start.14) | collective-permute-done | bytes 143392 | tf_op jit(solution)/shard_map/ppermute | solution.py:21
  153.6 0.8 pad_maximum_fusion
  154.4 7.4 %all-to-all-start.3 = ((f32[32,3,8,128]{3,2,1,0:T(8,128)}), f32[32,3,8,128]{3,2,1,0:T(8,128)S(1)}, u32[]{:S(2)}, u32[]{:S(2)}) async-start(f32[32,3,8,128]{3,2,1,0:T(8,128)} %pad_maximum_fusion), calls=%async_computation.3 | async-start | bytes 786432 | tf_op jit(solution)/shard_map/all_to_all | solution.py:33
  161.8 0.6 slice_bitcast_fusion.7
  162.4 9.9 %all-to-all-done.3 = f32[32,3,8,128]{3,2,1,0:T(8,128)S(1)} async-done(((f32[32,3,8,128]{3,2,1,0:T(8,128)}), f32[32,3,8,128]{3,2,1,0:T(8,128)S(1)}, u32[]{:S(2)}, u32[]{:S(2)}) %all-to-all-start.3) | async-done | bytes 393248 | tf_op jit(solution)/shard_map/all_to_all | solution.py:33
  172.2 0.7 slice_bitcast_fusion.4
  172.9 0.7 slice.89
  (48 shorter events, 0.5 us)
Async XLA Ops:
  0.6 12.6 %copy-start = (f32[4,4,128,128]{3,2,1,0:T(8,128)S(1)}, f32[4,4,128,128]{3,2,1,0:T(8,128)}, u32[]{:S(2)}) copy-start(f32[4,4,128,128]{3,2,1,0:T(8,128)} %param.7) | copy-start | bytes 3145732
  1.7 4.1 %collective-permute-start = (f32[1,16]{1,0:T(1,128)S(1)}, f32[1,16]{1,0:T(1,128)S(1)}, u32[]{:S(2)}, u32[]{:S(2)}) collective-permute-start(f32[1,16]{1,0:T(1,128)S(1)} %concatenate.39), channel_id=1, source_target_pairs={{0,1},{1,0},{2,3},{3,2},{4,5},{5,4},{6,7},{7,6},{8,9},{9,8},{10,11... | collective-permute-start | bytes 200 | tf_op jit(solution)/shard_map/ppermute | solution.py:21
  5.0 8.2 %copy-start.4 = (s32[2]{0:T(128)}, s32[2]{0:T(128)S(1)}, u32[]{:S(2)}) copy-start(s32[2]{0:T(128)S(1)} %pad_add_fusion.where_ref.refs_0_) | copy-start | bytes 28
  5.8 1.0 copy-start.1
  8.2 13.0 %all-to-all-start = ((f32[16,5,8,128]{3,2,1,0:T(8,128)}), f32[16,5,8,128]{3,2,1,0:T(8,128)S(1)}, u32[]{:S(2)}, u32[]{:S(2)}) async-start(f32[16,5,8,128]{3,2,1,0:T(8,128)} %shard_map.93), calls=%async_computation | async-start | bytes 655360 | tf_op jit(solution)/shard_map/all_to_all | solution.py:33
  13.3 29.2 %collective-permute-start.6 = (f32[2,128,128]{2,1,0:T(8,128)S(1)}, f32[2,128,128]{2,1,0:T(8,128)S(1)}, u32[]{:S(2)}, u32[]{:S(2)}) collective-permute-start(f32[2,128,128]{2,1,0:T(8,128)S(1)} %constant_dynamic-slice_fusion.2), channel_id=1, source_target_pairs={{0,2},{2,0},{1,3},{3,1},{4,6},{6,4},{5,7},{7,5},{8,10},{10,8},{9,1... | collective-permute-start | bytes 393224 | tf_op jit(solution)/shard_map/ppermute | solution.py:21
  21.2 8.7 %collective-permute-start.1 = (f32[16,128]{1,0:T(8,128)S(1)}, f32[16,128]{1,0:T(8,128)S(1)}, u32[]{:S(2)}, u32[]{:S(2)}) collective-permute-start(f32[16,128]{1,0:T(8,128)S(1)} %bitcast.65), channel_id=1, source_target_pairs={{0,2},{2,0},{1,3},{3,1},{4,6},{6,4},{5,7},{7,5},{8,10},{10,8},{9,1... | collective-permute-start | bytes 24584 | tf_op jit(solution)/shard_map/ppermute | solution.py:21
  28.2 6.0 %collective-permute-start.2 = (f32[64,8,128]{2,1,0:T(8,128)S(1)}, f32[64,8,128]{2,1,0:T(8,128)S(1)}, u32[]{:S(2)}, u32[]{:S(2)}) collective-permute-start(f32[64,8,128]{2,1,0:T(8,128)S(1)} %bitcast.56), channel_id=1, source_target_pairs={{0,50},{16,0},{32,16},{48,32},{2,48},{18,2},{34,18},{50,34},{1,51}... | collective-permute-start | bytes 786440 | tf_op jit(solution)/shard_map/ppermute | solution.py:29
  28.3 10.4 %collective-permute-start.3 = (f32[32,8,128]{2,1,0:T(8,128)S(1)}, f32[32,8,128]{2,1,0:T(8,128)S(1)}, u32[]{:S(2)}, u32[]{:S(2)}) collective-permute-start(f32[32,8,128]{2,1,0:T(8,128)S(1)} %bitcast.64), channel_id=1, source_target_pairs={{0,34},{16,50},{32,0},{48,16},{2,32},{18,48},{34,2},{50,18},{1,35}... | collective-permute-start | bytes 393224 | tf_op jit(solution)/shard_map/ppermute | solution.py:29
  28.4 11.3 %collective-permute-start.5 = (f32[64,8,128]{2,1,0:T(8,128)S(1)}, f32[64,8,128]{2,1,0:T(8,128)S(1)}, u32[]{:S(2)}, u32[]{:S(2)}) collective-permute-start(f32[64,8,128]{2,1,0:T(8,128)S(1)} %bitcast.58), channel_id=1, source_target_pairs={{0,16},{16,32},{32,48},{48,2},{2,18},{18,34},{34,50},{50,0},{1,17}... | collective-permute-start | bytes 786440 | tf_op jit(solution)/shard_map/ppermute | solution.py:29
  29.9 9.7 %collective-permute-start.4 = (f32[32,8,128]{2,1,0:T(8,128)S(1)}, f32[32,8,128]{2,1,0:T(8,128)S(1)}, u32[]{:S(2)}, u32[]{:S(2)}) collective-permute-start(f32[32,8,128]{2,1,0:T(8,128)S(1)} %bitcast.63), channel_id=1, source_target_pairs={{0,32},{16,48},{32,2},{48,18},{2,34},{18,50},{34,0},{50,16},{1,33}... | collective-permute-start | bytes 393224 | tf_op jit(solution)/shard_map/ppermute | solution.py:29
  42.5 0.7 copy-start.2
  43.1 37.4 %all-to-all-start.1 = ((f32[32,16,8,128]{3,2,1,0:T(8,128)}), f32[32,16,8,128]{3,2,1,0:T(8,128)S(1)}, u32[]{:S(2)}, u32[]{:S(2)}) async-start(f32[32,16,8,128]{3,2,1,0:T(8,128)} %shard_map.94), calls=%async_computation.1 | async-start | bytes 4194304 | tf_op jit(solution)/shard_map/all_to_all | solution.py:33
  52.2 23.2 %collective-permute-start.7 = (f32[6,128,128]{2,1,0:T(8,128)}, f32[6,128,128]{2,1,0:T(8,128)S(1)}, u32[]{:S(2)}, u32[]{:S(2)}) collective-permute-start(f32[6,128,128]{2,1,0:T(8,128)} %constant_dynamic-slice_fusion.3), channel_id=1, source_target_pairs={{0,2},{2,0},{1,3},{3,1},{4,6},{6,4},{5,7},{7,5},{8,10},{10,8},{9,1... | collective-permute-start | bytes 1179656 | tf_op jit(solution)/shard_map/ppermute | solution.py:21
  80.5 0.9 copy-start.3
  81.4 0.7 copy-start.5
  82.1 3.3 %copy-start.7 = (f32[128,256]{1,0:T(8,128)S(1)}, f32[128,256]{1,0:T(8,128)}, u32[]{:S(2)}) copy-start(f32[128,256]{1,0:T(8,128)} %refs_6_.1) | copy-start | bytes 393220
  82.1 4.7 %copy-start.6 = (f32[256,256]{1,0:T(8,128)S(1)}, f32[256,256]{1,0:T(8,128)}, u32[]{:S(2)}) copy-start(f32[256,256]{1,0:T(8,128)} %refs_8_.1) | copy-start | bytes 786436
  82.1 4.7 %copy-start.8 = (f32[256]{0:T(256)S(1)}, f32[256]{0:T(256)}, u32[]{:S(2)}) copy-start(f32[256]{0:T(256)} %param.10) | copy-start | bytes 3076
  84.4 2.3 %collective-permute-start.8 = (f32[2,128,256]{2,1,0:T(8,128)S(1)}, f32[2,128,256]{2,1,0:T(8,128)S(1)}, u32[]{:S(2)}, u32[]{:S(2)}) collective-permute-start(f32[2,128,256]{2,1,0:T(8,128)S(1)} %shard_map.95.refs_4_), channel_id=1, source_target_pairs={{0,1},{1,0},{2,3},{3,2},{4,5},{5,4},{6,7},{7,6},{8,9},{9,8},{10,11... | collective-permute-start | bytes 786440 | tf_op jit(solution)/shard_map/ppermute | solution.py:21
  85.4 1.3 collective-permute-start.9
  129.1 15.4 %collective-permute-start.11 = (f32[67,8,128]{2,1,0:T(8,128)S(1)}, f32[67,8,128]{2,1,0:T(8,128)S(1)}, u32[]{:S(2)}, u32[]{:S(2)}) collective-permute-start(f32[67,8,128]{2,1,0:T(8,128)S(1)} %get-tuple-element.17), channel_id=1, source_target_pairs={{0,50},{16,0},{32,16},{48,32},{2,48},{18,2},{34,18},{50,34},{1,51}... | collective-permute-start | bytes 823304 | tf_op jit(solution)/shard_map/ppermute | solution.py:29
  132.0 12.5 %collective-permute-start.10 = (f32[67,8,128]{2,1,0:T(8,128)S(1)}, f32[67,8,128]{2,1,0:T(8,128)S(1)}, u32[]{:S(2)}, u32[]{:S(2)}) collective-permute-start(f32[67,8,128]{2,1,0:T(8,128)S(1)} %get-tuple-element.16), channel_id=1, source_target_pairs={{0,16},{16,32},{32,48},{48,2},{2,18},{18,34},{34,50},{50,0},{1,17}... | collective-permute-start | bytes 823304 | tf_op jit(solution)/shard_map/ppermute | solution.py:29
  132.0 12.5 %collective-permute-start.12 = (f32[35,8,128]{2,1,0:T(8,128)S(1)}, f32[35,8,128]{2,1,0:T(8,128)S(1)}, u32[]{:S(2)}, u32[]{:S(2)}) collective-permute-start(f32[35,8,128]{2,1,0:T(8,128)S(1)} %slice_bitcast_fusion.3), channel_id=1, source_target_pairs={{0,32},{16,48},{32,2},{48,18},{2,34},{18,50},{34,0},{50,16},{1,33}... | collective-permute-start | bytes 430088 | tf_op jit(solution)/shard_map/ppermute | solution.py:29
  132.0 12.1 %collective-permute-start.13 = (f32[32,8,128]{2,1,0:T(8,128)S(1)}, f32[32,8,128]{2,1,0:T(8,128)S(1)}, u32[]{:S(2)}, u32[]{:S(2)}) collective-permute-start(f32[32,8,128]{2,1,0:T(8,128)S(1)} %slice_bitcast_fusion.6), channel_id=1, source_target_pairs={{0,34},{16,50},{32,0},{48,16},{2,32},{18,48},{34,2},{50,18},{1,35}... | collective-permute-start | bytes 393224 | tf_op jit(solution)/shard_map/ppermute | solution.py:29
  144.7 8.9 %collective-permute-start.14 = (f32[35,8,128]{2,1,0:T(8,128)S(1)}, f32[35,8,128]{2,1,0:T(8,128)S(1)}, u32[]{:S(2)}, u32[]{:S(2)}) collective-permute-start(f32[35,8,128]{2,1,0:T(8,128)S(1)} %pad_maximum_fusion.1), channel_id=1, source_target_pairs={{0,2},{2,0},{1,3},{3,1},{4,6},{6,4},{5,7},{7,5},{8,10},{10,8},{9,1... | collective-permute-start | bytes 430088 | tf_op jit(solution)/shard_map/ppermute | solution.py:21
  154.4 17.8 %all-to-all-start.3 = ((f32[32,3,8,128]{3,2,1,0:T(8,128)}), f32[32,3,8,128]{3,2,1,0:T(8,128)S(1)}, u32[]{:S(2)}, u32[]{:S(2)}) async-start(f32[32,3,8,128]{3,2,1,0:T(8,128)} %pad_maximum_fusion), calls=%async_computation.3 | async-start | bytes 786432 | tf_op jit(solution)/shard_map/all_to_all | solution.py:33

commit v4 on v3

v4 whole, which is shorter than its diff:
```python
import math

import jax
import jax.numpy as jnp
from jax import lax
from jax.experimental import pallas as pl
from jax.experimental.pallas import tpu as pltpu
from jax.sharding import Mesh
from jax.sharding import PartitionSpec as P

AXES = ("x", "zl", "y", "zh", "c")
PLANE = ("x", "y")
GROUP = ("x", "y", "c")
TOP = lax.Precision.HIGH
F32 = jnp.float32
LIMIT = 10 * 1024 * 1024


def shift(value, axis, steps):
    count = lax.axis_size(axis)
    return lax.ppermute(value, axis, [(s, (s + steps) % count) for s in range(count)])


def ring(value, steps):
    pairs = []
    for s in range(8):
        for c in range(2):
            d = (s + (steps if abs(steps) == 1 or c == 0 else -steps)) % 8
            source, target = (s % 4) * 2 + s // 4, (d % 4) * 2 + d // 4
            pairs.append((source * 2 + c, target * 2 + c))
    return lax.ppermute(value, ("zl", "zh", "c"), pairs)


def exchange(value, axes):
    return lax.all_to_all(value, axes, 0, 0, tiled=True)


def vmem():
    return pl.BlockSpec(memory_space=pltpu.VMEM)


def smem():
    return pl.BlockSpec(memory_space=pltpu.SMEM)


def call(kernel, out_shape, specs, scratch=(), flops=0, moved=0):
    return pl.pallas_call(
        kernel,
        out_shape=out_shape,
        in_specs=specs,
        out_specs=jax.tree.map(lambda _: vmem(), out_shape),
        scratch_shapes=scratch,
        compiler_params=pltpu.CompilerParams(vmem_limit_bytes=LIMIT),
        cost_estimate=pl.CostEstimate(flops=flops, bytes_accessed=moved, transcendentals=0),
    )


def pack_kernel(where_ref, rows_ref, wanted_ref, out_ref):
    for h in range(2):

        @pl.when(where_ref[0] == h)
        def _():
            for b in range(4):
                half = rows_ref[128 * b : 128 * (b + 1), 128 * h : 128 * (h + 1)]
                out_ref[:, b] = half.reshape(16, 8, 128)

    out_ref[:, 4] = jnp.broadcast_to(wanted_ref[...].reshape(1, 1, 128), (16, 8, 128))


def row_of(where_ref, near_ref, far_ref, q, c, place):
    def asked(slot):
        source, core, k = slot // 8, slot // 4 % 2, slot % 4
        index_ref = far_ref if source else near_ref
        return index_ref[q, 16 * core + 8 * source + 4 * c + k]

    if place in (0, 8):
        return jnp.where(8 * where_ref[1] == place, asked(15), asked(place))
    return asked(place)


def gather_kernel(where_ref, near_ref, far_ref, table_ref, out_ref):
    def one(q, carry):
        for c in range(2):
            for slot in range(15):
                row = row_of(where_ref, near_ref, far_ref, q, c, slot)
                out_ref[q * 2 + c, slot] = table_ref[row]
        return carry

    lax.fori_loop(0, 16, one, 0)


def scatter_kernel(where_ref, near_ref, far_ref, got_ref, out_ref, even_ref, odd_ref):
    even_ref[...] = jnp.zeros_like(even_ref)
    odd_ref[...] = jnp.zeros_like(odd_ref)

    def one(q, carry):
        for slot in range(15):
            even_ref[row_of(where_ref, near_ref, far_ref, q, 0, slot)] += got_ref[q, 0, slot]
            odd_ref[row_of(where_ref, near_ref, far_ref, q, 1, slot)] += got_ref[q, 1, slot]
        return carry

    lax.fori_loop(0, 16, one, 0)
    sums = [jnp.sum(got_ref[:, 0, 15 + t] + got_ref[:, 1, 15 + t], axis=0) for t in range(3)]
    for plane in range(4):
        for part in range(3):
            out_ref[plane, part] = sums[part]
        rows = pl.ds(plane * 64, 64)
        out_ref[plane, 3:67] = even_ref[rows] + odd_ref[rows]


def unpack_kernel(home_ref, local_ref, feats_ref, weight_ref):
    for h in range(2):
        columns = slice(128 * h, 128 * (h + 1))
        feats_ref[:, columns] = home_ref[:, h, 0].reshape(128, 128) + local_ref[:, columns]
        weight_ref[:, columns] = home_ref[:, h, 1:].reshape(256, 128)


def dot(a, b):
    return lax.dot_general(
        a, b, (((1,), (0,)), ((), ())), precision=TOP, preferred_element_type=F32
    )


def dot_first(a, b):
    return lax.dot_general(
        a, b, (((0,), (0,)), ((), ())), precision=TOP, preferred_element_type=F32
    )


def dot_last(a, b):
    return lax.dot_general(
        a, b, (((1,), (1,)), ((), ())), precision=TOP, preferred_element_type=F32
    )


def middle_kernel(
    scale,
    where_ref,
    own_ref,
    beside_ref,
    across_ref,
    opposite_ref,
    rows_ref,
    got_ref,
    cot_ref,
    weight_ref,
    bias_ref,
    layer_ref,
    out_ref,
    local_ref,
):
    core, half = where_ref[0], where_ref[1]
    tiles = []
    for near_ref, far_ref in ((own_ref, beside_ref), (across_ref, opposite_ref)):
        for c in range(2):
            for k in range(4):
                tiles.append(jnp.where(core == c, near_ref[k], far_ref[k]))
    alone = jnp.where(half == 0, tiles[0], tiles[8])
    for j in (0, 8):
        tiles[j] = jnp.where(8 * half == j, tiles[15], tiles[j])
    tiles = jnp.concatenate(tiles[:15] + [alone], axis=1)
    rows = [
        jnp.concatenate([got_ref[:, h, j].reshape(128, 128) for h in range(2)], axis=1)
        for j in range(15)
    ]
    hidden = dot(tiles, jnp.concatenate(rows + [rows_ref[...]], axis=0))
    pre = dot(hidden, weight_ref[...]) + bias_ref[...]
    grow = jnp.exp(jnp.minimum(pre, 0.0))
    layer_ref[...] = jnp.where(pre > 0, pre, grow - 1.0)
    grad_pre = cot_ref[...] * jnp.where(pre > 0, 1.0, grow)
    grad_hidden = dot_last(grad_pre, weight_ref[...])
    terms = dot_first(tiles, grad_hidden)
    local_ref[...] = terms[1920:]
    grad_weight = dot_first(hidden, grad_pre) * scale
    grad_bias = jnp.sum(grad_pre, axis=0, keepdims=True) * scale
    row_ids = lax.broadcasted_iota(jnp.int32, (8, 128), 0)
    bias_tile = jnp.where(row_ids == 0, grad_bias[:, :128], 0.0)
    bias_tile = jnp.where(row_ids == 1, grad_bias[:, 128:], bias_tile)
    for h in range(2):
        columns = slice(128 * h, 128 * (h + 1))
        for j in range(15):
            out_ref[:, h, j] = terms[128 * j : 128 * (j + 1), columns].reshape(16, 8, 128)
        out_ref[:, h, 15:17] = grad_weight[:, columns].reshape(16, 2, 8, 128)
        out_ref[:, h, 17] = jnp.broadcast_to(bias_tile.reshape(1, 8, 128), (16, 8, 128))


def body(node_feats, operator_tiles, tile_cols, weight, layer_bias, cotangent):
    level = lax.axis_index("zl")
    half = lax.axis_index("zh")
    core = lax.axis_index("c")
    where = jnp.stack([core, half]).astype(jnp.int32)
    scale = 1.0 / math.sqrt(32768)

    mine = 2 * half + core

    def swapped(tiles, pairs):
        return lax.ppermute(tiles, ("zh", "c"), pairs)

    def tiles_for(block):
        return lax.dynamic_index_in_dim(operator_tiles, block, 0, keepdims=False)

    beside = swapped(tiles_for(2 * half + 1 - core), [(0, 1), (1, 0), (2, 3), (3, 2)])
    rows = lax.dynamic_slice_in_dim(node_feats, 128 * mine, 128, 0)

    asked = tile_cols.reshape(2, 8)
    owner = asked // 4
    spot = (owner // 16 * 4 + owner % 4) * 4 + asked % 4
    asked = jnp.mod(owner // 4 % 4 - level, 4) * 64 + spot
    asked = jnp.where(half == 0, asked, asked[::-1]).astype(F32).reshape(1, 16)
    asked_beside = shift(asked, "c", 1)
    wanted = jnp.where(
        core == 0,
        jnp.concatenate([asked, asked_beside], axis=1),
        jnp.concatenate([asked_beside, asked], axis=1),
    )
    wanted = jnp.pad(wanted, ((0, 0), (0, 96)))

    packed = call(
        pack_kernel,
        jax.ShapeDtypeStruct((16, 5, 8, 128), F32),
        [smem(), vmem(), vmem()],
        moved=1 << 20,
    )(where, node_feats, wanted)
    arrived = exchange(packed, PLANE)
    plane = arrived[:, :4].reshape(64, 8, 128)
    table = jnp.concatenate(
        [plane, ring(plane, -1), ring(plane, -2), ring(plane, 1)], axis=0
    )
    asked = arrived[:, 4, 0]
    index = (asked.astype(jnp.int32), shift(asked, "zh", 1).astype(jnp.int32))

    leaving = (tiles_for(2 * (1 - half) + core), tiles_for(2 * (1 - half) + 1 - core))
    table, leaving = lax.optimization_barrier((table, leaving))
    across = swapped(leaving[0], [(0, 2), (2, 0), (1, 3), (3, 1)])
    opposite = swapped(leaving[1], [(0, 3), (3, 0), (1, 2), (2, 1)])
    sent = call(
        gather_kernel,
        jax.ShapeDtypeStruct((32, 15, 8, 128), F32),
        [smem(), smem(), smem(), vmem()],
        moved=3 << 20,
    )(where, *index, table)
    got = exchange(sent, GROUP).reshape(16, 2, 15, 8, 128)
    def middle(*refs):
        middle_kernel(scale, *refs)

    layer_out, terms, local = call(
        middle,
        (
            jax.ShapeDtypeStruct((128, 256), F32),
            jax.ShapeDtypeStruct((16, 2, 18, 8, 128), F32),
            jax.ShapeDtypeStruct((128, 256), F32),
        ),
        [smem()] + [vmem()] * 9,
        flops=318767104 * 3,
        moved=6 << 20,
    )(
        where,
        tiles_for(mine),
        beside,
        across,
        opposite,
        rows,
        got,
        cotangent,
        weight,
        layer_bias.reshape(1, 256),
    )
    back = exchange(terms.reshape(32, 18, 8, 128), GROUP).reshape(16, 2, 18, 8, 128)
    sums = call(
        scatter_kernel,
        jax.ShapeDtypeStruct((4, 67, 8, 128), F32),
        [smem(), smem(), smem(), vmem()],
        scratch=[pltpu.VMEM((256, 8, 128), F32)] * 2,
        moved=4 << 20,
    )(where, *index, back)
    total = sums[0] + ring(sums[1], 1) + ring(sums[3], -1) + ring(sums[2], 2)
    by_owner = total[3:].reshape(16, 4, 8, 128)
    staying = lax.dynamic_slice_in_dim(by_owner, 2 * half, 2, 1).reshape(32, 8, 128)
    leaving = lax.dynamic_slice_in_dim(by_owner, 2 * (1 - half), 2, 1).reshape(32, 8, 128)
    final = jnp.concatenate([staying, total[:3]], axis=0) + shift(
        jnp.concatenate([leaving, total[:3]], axis=0), "zh", 1
    )
    home = exchange(
        jnp.concatenate(
            [
                final[:32, None],
                jnp.broadcast_to(final[None, 32:34], (32, 2, 8, 128)),
            ],
            axis=1,
        ),
        GROUP,
    ).reshape(16, 2, 3, 8, 128)
    grad_feats, grad_weight = call(
        unpack_kernel,
        (jax.ShapeDtypeStruct((128, 256), F32), jax.ShapeDtypeStruct((256, 256), F32)),
        [vmem(), vmem()],
        moved=1 << 20,
    )(home, local)
    grad_bias = final[34, :2].reshape(256)
    return layer_out, grad_feats, grad_weight, grad_bias


def solution(mesh):
    fine = Mesh(mesh.devices.reshape(4, 4, 4, 2, 2), AXES)
    blk, rep = ("x", "zl", "y"), ("zh", "c")
    return jax.shard_map(
        body,
        mesh=fine,
        in_specs=(
            P(blk, None),
            P(blk, rep, None, None),
            P(blk, rep),
            P(),
            P(),
            P(AXES, None),
        ),
        out_specs=(P(AXES, None), P(AXES, None), P(), P()),
        check_vma=False,
    )
```

time: 174 us -> 171 us (0.983)
  starting transfers between devices: 58.7 us -> 39.9 us
  blocking collectives: 34.6 us -> 51.4 us
  Pallas kernels: 14.1 us -> 9.65 us
  waiting for transfers between devices: 56.9 us -> 61.2 us
    ppermute x8 -> x9, waiting for transfers between devices: 16.2 us -> 33.7 us  [the longest x3 21 us: swapped(): return lax.ppermute(tiles, ('zh', 'c'), pairs)]
    all_to_all x1 -> x2, blocking collectives: 34.6 us -> 51.4 us  [exchange(): return lax.all_to_all(value, axes, 0, 0, tiled=True)]
    ppermute x7 -> x3, starting transfers between devices: 26.6 us -> 10.4 us  [shift(): lax.ppermute(value, axis, [(s, (s + steps) % count) for s in range(count)])]
    all_to_all x3 -> x2, starting transfers between devices: 21.5 us -> 9.92 us  [exchange(): return lax.all_to_all(value, axes, 0, 0, tiled=True)]
    ppermute x8 -> x9, starting transfers between devices: 10.6 us -> 19.7 us  [the longest x6 13.5 us: ring(): return lax.ppermute(value, ('zl', 'zh', 'c'), pairs)]
    ppermute x7 -> x3, waiting for transfers between devices: 25.6 us -> 17.7 us  [shift(): lax.ppermute(value, axis, [(s, (s + steps) % count) for s in range(count)])]
    all_to_all x3 -> x2, waiting for transfers between devices: 15.1 us -> 9.85 us  [exchange(): return lax.all_to_all(value, axes, 0, 0, tiled=True)]
    pallas_call x1, Pallas kernels: 5.55 us -> 3.3 us  [body(): call(middle, (jax.ShapeDtypeStruct((128, 256), F32), jax.ShapeDtypeStruct...]
  transfers between devices with their start and end apart: 18 -> 14, of which waited for: 12 -> 10; matrix products, arithmetic and copies ran while one was open for 1% -> 1% of each run, Pallas kernels for 2% -> 0%
where the time goes in v4:
time: 171 us
  waiting for transfers between devices  61.2 us (36%)
  blocking collectives  51.4 us (30%)
  starting transfers between devices  39.9 us (23%)
  Pallas kernels  9.65 us (6%)
  local copies, waits for them, and re-layouts  6.46 us (4%)
    all_to_all x2, blocking collectives, exchange(): return lax.all_to_all(value, axes, 0, 0, tiled=True)  51.4 us
    ppermute x3, waiting for transfers between devices, swapped(): return lax.ppermute(tiles, ('zh', 'c'), pairs)  21 us
    ppermute x3, waiting for transfers between devices, shift(): lax.ppermute(value, axis, [(s, (s + steps) % count) for s in range(count)])  17.7 us
    ppermute x6, starting transfers between devices, ring(): return lax.ppermute(value, ('zl', 'zh', 'c'), pairs)  13.5 us
    ppermute x6, waiting for transfers between devices, ring(): return lax.ppermute(value, ('zl', 'zh', 'c'), pairs)  12.7 us
    ppermute x3, starting transfers between devices, shift(): lax.ppermute(value, axis, [(s, (s + steps) % count) for s in range(count)])  10.4 us
    all_to_all x2, starting transfers between devices, exchange(): return lax.all_to_all(value, axes, 0, 0, tiled=True)  9.92 us
    all_to_all x2, waiting for transfers between devices, exchange(): return lax.all_to_all(value, axes, 0, 0, tiled=True)  9.85 us
  transfers between devices with their start and end apart: 14, of which 10 were waited for; matrix products, arithmetic and copies ran while one was open for 1% of the time, Pallas kernels for 0%

profile of v4, /device:TPU:1, one launch (start us, length us, event | category | flops | bytes accessed | tf_op | source)
XLA Modules:
  0.0 170.6 jit_solution(1682531265173829333)
XLA Ops:
  0.6 0.8 reshape.100
  1.5 0.1 concatenate.36
  1.6 3.3 %collective-permute-start.1 = (f32[1,16]{1,0:T(1,128)S(1)}, f32[1,16]{1,0:T(1,128)S(1)}, u32[]{:S(2)}, u32[]{:S(2)}) collective-permute-start(f32[1,16]{1,0:T(1,128)S(1)} %concatenate.36), channel_id=1, source_target_pairs={{0,1},{1,0},{2,3},{3,2},{4,5},{5,4},{6,7},{7,6},{8,9},{9,8},{10,11... | collective-permute-start | bytes 200 | tf_op jit(solution)/shard_map/ppermute | solution.py:21
  4.8 0.1 pad_add_fusion.where_ref.refs_0_
  4.9 0.7 collective-permute-done.1
  5.7 0.1 broadcast_select_fusion
  5.7 1.0 copy-done
  6.8 0.6 shard_map.93
  7.4 12.8 %all_to_all.20 = f32[16,5,8,128]{3,2,1,0:T(8,128)S(1)} all-to-all(f32[16,5,8,128]{3,2,1,0:T(8,128)S(1)} %shard_map.93), channel_id=1, replica_groups=mesh['x'=4,'zl'=4,'y'=4,'zh'=2,'c'=2] {'x','y'}, dimensions={0} | all-to-all | bytes 655360 | tf_op jit(solution)/shard_map/all_to_all | solution.py:35
  20.2 1.7 %collective-permute-start.4 = (f32[64,8,128]{2,1,0:T(8,128)S(1)}, f32[64,8,128]{2,1,0:T(8,128)S(1)}, u32[]{:S(2)}, u32[]{:S(2)}) collective-permute-start(f32[64,8,128]{2,1,0:T(8,128)S(1)} %bitcast.46), channel_id=1, source_target_pairs={{0,16},{1,17},{16,32},{17,33},{32,48},{33,49},{48,2},{49,3},{2,18}... | collective-permute-start | bytes 786440 | tf_op jit(solution)/shard_map/ppermute | solution.py:31
  21.9 3.0 %collective-permute-start.3 = (f32[64,8,128]{2,1,0:T(8,128)S(1)}, f32[64,8,128]{2,1,0:T(8,128)S(1)}, u32[]{:S(2)}, u32[]{:S(2)}) collective-permute-start(f32[64,8,128]{2,1,0:T(8,128)S(1)} %bitcast.47), channel_id=1, source_target_pairs={{0,34},{1,33},{16,50},{17,49},{32,0},{33,3},{48,16},{49,19},{2,32}... | collective-permute-start | bytes 786440 | tf_op jit(solution)/shard_map/ppermute | solution.py:31
  24.9 1.1 collective-permute-start.2
  26.1 5.0 %collective-permute-start.7 = (f32[16,128]{1,0:T(8,128)S(1)}, f32[16,128]{1,0:T(8,128)S(1)}, u32[]{:S(2)}, u32[]{:S(2)}) collective-permute-start(f32[16,128]{1,0:T(8,128)S(1)} %bitcast.52), channel_id=1, source_target_pairs={{0,2},{2,0},{1,3},{3,1},{4,6},{6,4},{5,7},{7,5},{8,10},{10,8},{9,1... | collective-permute-start | bytes 24584 | tf_op jit(solution)/shard_map/ppermute | solution.py:21
  31.1 0.9 dynamic-slice_bitcast_fusion
  32.0 6.7 %collective-permute-done.7 = f32[16,128]{1,0:T(8,128)S(1)} collective-permute-done((f32[16,128]{1,0:T(8,128)S(1)}, f32[16,128]{1,0:T(8,128)S(1)}, u32[]{:S(2)}, u32[]{:S(2)}) %collective-permute-start.7) | collective-permute-done | bytes 8224 | tf_op jit(solution)/shard_map/ppermute | solution.py:21
  38.7 0.0 collective-permute-done.4
  38.7 0.2 collective-permute-done.3
  39.0 0.1 pad_maximum_fusion.table_ref
  39.1 2.7 %shard_map.94 = f32[32,15,8,128]{3,2,1,0:T(8,128)} custom-call(s32[2]{0:T(128)S(1)} %pad_add_fusion.where_ref.refs_0_, s32[16,128]{1,0:T(8,128)S(1)} %convert_element_type.12.near_ref, s32[16,128]{1,0:T(8,128)S(1)} %convert_element_type.13.far_ref, f32[256,8,128]{2,1,0:T(8,128)S(1)} %pad_maximum_fusion.table_ref), custom_call_target="tpu_custom_call" | custom-call | bytes 3145728 | tf_op jit(solution)/shard_map/pallas_call | solution.py:236
  41.8 5.4 %all-to-all-start.1 = ((f32[32,15,8,128]{3,2,1,0:T(8,128)}), f32[32,15,8,128]{3,2,1,0:T(8,128)S(1)}, u32[]{:S(2)}, u32[]{:S(2)}) async-start(f32[32,15,8,128]{3,2,1,0:T(8,128)} %shard_map.94), calls=%async_computation.1 | async-start | bytes 3932160 | tf_op jit(solution)/shard_map/all_to_all | solution.py:35
  47.2 0.4 collective-permute-start
  47.6 3.8 %collective-permute-start.5 = (f32[4,128,128]{2,1,0:T(8,128)}, f32[4,128,128]{2,1,0:T(8,128)S(1)}, u32[]{:S(2)}, u32[]{:S(2)}) collective-permute-start(f32[4,128,128]{2,1,0:T(8,128)} %get-tuple-element.12), channel_id=1, source_target_pairs={{0,2},{2,0},{1,3},{3,1},{4,6},{6,4},{5,7},{7,5},{8,10},{10,8},{9,1... | collective-permute-start | bytes 786440 | tf_op jit(solution)/shard_map/ppermute | solution.py:197
  51.4 2.0 %collective-permute-start.6 = (f32[4,128,128]{2,1,0:T(8,128)}, f32[4,128,128]{2,1,0:T(8,128)S(1)}, u32[]{:S(2)}, u32[]{:S(2)}) collective-permute-start(f32[4,128,128]{2,1,0:T(8,128)} %get-tuple-element.13), channel_id=1, source_target_pairs={{0,3},{3,0},{1,2},{2,1},{4,7},{7,4},{5,6},{6,5},{8,11},{11,8},{9,1... | collective-permute-start | bytes 786440 | tf_op jit(solution)/shard_map/ppermute | solution.py:197
  53.4 0.9 constant_dynamic-slice_fusion.2.refs_5_
  54.3 9.7 %collective-permute-done.5.refs_3_ = f32[4,128,128]{2,1,0:T(8,128)S(1)} collective-permute-done((f32[4,128,128]{2,1,0:T(8,128)}, f32[4,128,128]{2,1,0:T(8,128)S(1)}, u32[]{:S(2)}, u32[]{:S(2)}) %collective-permute-start.5) | collective-permute-done | bytes 262176 | tf_op jit(solution)/shard_map/ppermute | solution.py:197
  64.0 11.3 %collective-permute-done.6.refs_4_ = f32[4,128,128]{2,1,0:T(8,128)S(1)} collective-permute-done((f32[4,128,128]{2,1,0:T(8,128)}, f32[4,128,128]{2,1,0:T(8,128)S(1)}, u32[]{:S(2)}, u32[]{:S(2)}) %collective-permute-start.6) | collective-permute-done | bytes 262176 | tf_op jit(solution)/shard_map/ppermute | solution.py:197
  75.3 0.0 copy-start.6
  75.3 0.6 copy-done.6
  76.0 0.7 copy-done.7
  76.7 3.3 %shard_map.95 = (f32[128,256]{1,0:T(8,128)}, f32[16,2,18,8,128]{4,3,2,1,0:T(8,128)S(1)}, f32[128,256]{1,0:T(8,128)S(1)}) custom-call(s32[2]{0:T(128)S(1)} %copy-done.6, f32[4,128,128]{2,1,0:T(8,128)S(1)} %get-tuple-element.25.refs_1_, f32[4,128,128]{2,1,0:T(8,128)S(1)} %collective-permute-done.refs_2_, f32[4,128,128]{2,1,0:T(8,128)S(1)} %collective-permute-done.5.refs_3_, ...), custom_call_target="tpu_custom_call" | custom-call | flops 956301312 | bytes 6291456 | tf_op jit(solution)/shard_map/pallas_call | solution.py:246
  80.0 0.0 copy-start.3
  80.0 0.6 copy-done.3
  80.6 38.5 %all_to_all.21 = f32[32,18,8,128]{3,2,1,0:T(8,128)S(1)} all-to-all(f32[32,18,8,128]{3,2,1,0:T(8,128)S(1)} %bitcast.42), channel_id=1, replica_groups=mesh['x'=4,'zl'=4,'y'=4,'zh'=2,'c'=2] {'x','y','c'}, dimensions={0} | all-to-all | bytes 4718592 | tf_op jit(solution)/shard_map/all_to_all | solution.py:35
  119.2 2.3 %shard_map.96 = f32[4,67,8,128]{3,2,1,0:T(8,128)S(1)} custom-call(s32[2]{0:T(128)S(1)} %copy-done.6, s32[16,128]{1,0:T(8,128)S(1)} %convert_element_type.12.near_ref, s32[16,128]{1,0:T(8,128)S(1)} %convert_element_type.13.far_ref, f32[16,2,18,8,128]{4,3,2,1,0:T(8,128)S(1)} %bitcast.40), custom_call_target="tpu_custom_call" | custom-call | bytes 4194304 | tf_op jit(solution)/shard_map/pallas_call | solution.py:269
  121.4 0.1 slice_bitcast_fusion.2
  121.5 3.0 %collective-permute-start.8 = (f32[67,8,128]{2,1,0:T(8,128)S(1)}, f32[67,8,128]{2,1,0:T(8,128)S(1)}, u32[]{:S(2)}, u32[]{:S(2)}) collective-permute-start(f32[67,8,128]{2,1,0:T(8,128)S(1)} %get-tuple-element.20), channel_id=1, source_target_pairs={{0,16},{1,17},{16,32},{17,33},{32,48},{33,49},{48,2},{49,3},{2,18}... | collective-permute-start | bytes 823304 | tf_op jit(solution)/shard_map/ppermute | solution.py:31
  124.5 4.7 %collective-permute-start.10 = (f32[67,8,128]{2,1,0:T(8,128)S(1)}, f32[67,8,128]{2,1,0:T(8,128)S(1)}, u32[]{:S(2)}, u32[]{:S(2)}) collective-permute-start(f32[67,8,128]{2,1,0:T(8,128)S(1)} %get-tuple-element.21), channel_id=1, source_target_pairs={{0,32},{1,35},{16,48},{17,51},{32,2},{33,1},{48,18},{49,17},{2,34}... | collective-permute-start | bytes 823304 | tf_op jit(solution)/shard_map/ppermute | solution.py:31
  129.2 5.7 %collective-permute-done.8 = f32[67,8,128]{2,1,0:T(8,128)S(1)} collective-permute-done((f32[67,8,128]{2,1,0:T(8,128)S(1)}, f32[67,8,128]{2,1,0:T(8,128)S(1)}, u32[]{:S(2)}, u32[]{:S(2)}) %collective-permute-start.8) | collective-permute-done | bytes 274464 | tf_op jit(solution)/shard_map/ppermute | solution.py:31
  134.8 3.3 %collective-permute-done.10 = f32[67,8,128]{2,1,0:T(8,128)S(1)} collective-permute-done((f32[67,8,128]{2,1,0:T(8,128)S(1)}, f32[67,8,128]{2,1,0:T(8,128)S(1)}, u32[]{:S(2)}, u32[]{:S(2)}) %collective-permute-start.10) | collective-permute-done | bytes 274464 | tf_op jit(solution)/shard_map/ppermute | solution.py:31
  138.1 3.5 %collective-permute-done.9 = f32[67,8,128]{2,1,0:T(8,128)S(1)} collective-permute-done((f32[67,8,128]{2,1,0:T(8,128)S(1)}, f32[67,8,128]{2,1,0:T(8,128)S(1)}, u32[]{:S(2)}, u32[]{:S(2)}) %collective-permute-start.9) | collective-permute-done | bytes 274464 | tf_op jit(solution)/shard_map/ppermute | solution.py:31
  141.6 0.1 fusion.2
  141.8 2.1 %collective-permute-start.11 = (f32[35,8,128]{2,1,0:T(8,128)S(1)}, f32[35,8,128]{2,1,0:T(8,128)S(1)}, u32[]{:S(2)}, u32[]{:S(2)}) collective-permute-start(f32[35,8,128]{2,1,0:T(8,128)S(1)} %pad_maximum_fusion.2), channel_id=1, source_target_pairs={{0,2},{2,0},{1,3},{3,1},{4,6},{6,4},{5,7},{7,5},{8,10},{10,8},{9,1... | collective-permute-start | bytes 430088 | tf_op jit(solution)/shard_map/ppermute | solution.py:21
  143.9 10.2 %collective-permute-done.11 = f32[35,8,128]{2,1,0:T(8,128)S(1)} collective-permute-done((f32[35,8,128]{2,1,0:T(8,128)S(1)}, f32[35,8,128]{2,1,0:T(8,128)S(1)}, u32[]{:S(2)}, u32[]{:S(2)}) %collective-permute-start.11) | collective-permute-done | bytes 143392 | tf_op jit(solution)/shard_map/ppermute | solution.py:21
  154.2 0.8 pad_maximum_fusion.1
  155.0 4.5 %all-to-all-start.3 = ((f32[32,3,8,128]{3,2,1,0:T(8,128)}), f32[32,3,8,128]{3,2,1,0:T(8,128)S(1)}, u32[]{:S(2)}, u32[]{:S(2)}) async-start(f32[32,3,8,128]{3,2,1,0:T(8,128)} %pad_maximum_fusion.1), calls=%async_computation.3 | async-start | bytes 786432 | tf_op jit(solution)/shard_map/all_to_all | solution.py:35
  159.4 0.6 slice_bitcast_fusion.5
  160.0 9.9 %all-to-all-done.3 = f32[32,3,8,128]{3,2,1,0:T(8,128)S(1)} async-done(((f32[32,3,8,128]{3,2,1,0:T(8,128)}), f32[32,3,8,128]{3,2,1,0:T(8,128)S(1)}, u32[]{:S(2)}, u32[]{:S(2)}) %all-to-all-start.3) | async-done | bytes 393248 | tf_op jit(solution)/shard_map/all_to_all | solution.py:35
  169.9 0.8 shard_map.97
  (32 shorter events, 0.3 us)
Async XLA Ops:
  1.6 4.1 %collective-permute-start.1 = (f32[1,16]{1,0:T(1,128)S(1)}, f32[1,16]{1,0:T(1,128)S(1)}, u32[]{:S(2)}, u32[]{:S(2)}) collective-permute-start(f32[1,16]{1,0:T(1,128)S(1)} %concatenate.36), channel_id=1, source_target_pairs={{0,1},{1,0},{2,3},{3,2},{4,5},{5,4},{6,7},{7,6},{8,9},{9,8},{10,11... | collective-permute-start | bytes 200 | tf_op jit(solution)/shard_map/ppermute | solution.py:21
  4.9 34.1 %copy-start.5 = (s32[2]{0:T(128)}, s32[2]{0:T(128)S(1)}, u32[]{:S(2)}) copy-start(s32[2]{0:T(128)S(1)} %pad_add_fusion.where_ref.refs_0_) | copy-start | bytes 28
  5.7 1.0 copy-start
  6.8 24.3 %copy-start.8 = (f32[4,4,128,128]{3,2,1,0:T(8,128)S(1)}, f32[4,4,128,128]{3,2,1,0:T(8,128)}, u32[]{:S(2)}) copy-start(f32[4,4,128,128]{3,2,1,0:T(8,128)} %param.7) | copy-start | bytes 3145732
  20.2 18.5 %collective-permute-start.4 = (f32[64,8,128]{2,1,0:T(8,128)S(1)}, f32[64,8,128]{2,1,0:T(8,128)S(1)}, u32[]{:S(2)}, u32[]{:S(2)}) collective-permute-start(f32[64,8,128]{2,1,0:T(8,128)S(1)} %bitcast.46), channel_id=1, source_target_pairs={{0,16},{1,17},{16,32},{17,33},{32,48},{33,49},{48,2},{49,3},{2,18}... | collective-permute-start | bytes 786440 | tf_op jit(solution)/shard_map/ppermute | solution.py:31
  21.9 17.0 %collective-permute-start.3 = (f32[64,8,128]{2,1,0:T(8,128)S(1)}, f32[64,8,128]{2,1,0:T(8,128)S(1)}, u32[]{:S(2)}, u32[]{:S(2)}) collective-permute-start(f32[64,8,128]{2,1,0:T(8,128)S(1)} %bitcast.47), channel_id=1, source_target_pairs={{0,34},{1,33},{16,50},{17,49},{32,0},{33,3},{48,16},{49,19},{2,32}... | collective-permute-start | bytes 786440 | tf_op jit(solution)/shard_map/ppermute | solution.py:31
  24.9 14.0 %collective-permute-start.2 = (f32[64,8,128]{2,1,0:T(8,128)S(1)}, f32[64,8,128]{2,1,0:T(8,128)S(1)}, u32[]{:S(2)}, u32[]{:S(2)}) collective-permute-start(f32[64,8,128]{2,1,0:T(8,128)S(1)} %bitcast.48), channel_id=1, source_target_pairs={{0,50},{1,51},{16,0},{17,1},{32,16},{33,17},{48,32},{49,33},{2,48}... | collective-permute-start | bytes 786440 | tf_op jit(solution)/shard_map/ppermute | solution.py:31
  26.1 12.7 %collective-permute-start.7 = (f32[16,128]{1,0:T(8,128)S(1)}, f32[16,128]{1,0:T(8,128)S(1)}, u32[]{:S(2)}, u32[]{:S(2)}) collective-permute-start(f32[16,128]{1,0:T(8,128)S(1)} %bitcast.52), channel_id=1, source_target_pairs={{0,2},{2,0},{1,3},{3,1},{4,6},{6,4},{5,7},{7,5},{8,10},{10,8},{9,1... | collective-permute-start | bytes 24584 | tf_op jit(solution)/shard_map/ppermute | solution.py:21
  41.8 33.5 %copy-start.1 = (f32[256,256]{1,0:T(8,128)S(1)}, f32[256,256]{1,0:T(8,128)}, u32[]{:S(2)}) copy-start(f32[256,256]{1,0:T(8,128)} %refs_8_.1) | copy-start | bytes 786436
  41.8 33.5 %copy-start.2 = (f32[128,256]{1,0:T(8,128)S(1)}, f32[128,256]{1,0:T(8,128)}, u32[]{:S(2)}) copy-start(f32[128,256]{1,0:T(8,128)} %refs_7_.1) | copy-start | bytes 393220
  41.8 33.5 %all-to-all-start.1 = ((f32[32,15,8,128]{3,2,1,0:T(8,128)}), f32[32,15,8,128]{3,2,1,0:T(8,128)S(1)}, u32[]{:S(2)}, u32[]{:S(2)}) async-start(f32[32,15,8,128]{3,2,1,0:T(8,128)} %shard_map.94), calls=%async_computation.1 | async-start | bytes 3932160 | tf_op jit(solution)/shard_map/all_to_all | solution.py:35
  47.2 7.1 %collective-permute-start = (f32[4,128,128]{2,1,0:T(8,128)}, f32[4,128,128]{2,1,0:T(8,128)S(1)}, u32[]{:S(2)}, u32[]{:S(2)}) collective-permute-start(f32[4,128,128]{2,1,0:T(8,128)} %get-tuple-element.24), channel_id=1, source_target_pairs={{0,1},{1,0},{2,3},{3,2},{4,5},{5,4},{6,7},{7,6},{8,9},{9,8},{10,11... | collective-permute-start | bytes 786440 | tf_op jit(solution)/shard_map/ppermute | solution.py:197
  47.6 16.4 %collective-permute-start.5 = (f32[4,128,128]{2,1,0:T(8,128)}, f32[4,128,128]{2,1,0:T(8,128)S(1)}, u32[]{:S(2)}, u32[]{:S(2)}) collective-permute-start(f32[4,128,128]{2,1,0:T(8,128)} %get-tuple-element.12), channel_id=1, source_target_pairs={{0,2},{2,0},{1,3},{3,1},{4,6},{6,4},{5,7},{7,5},{8,10},{10,8},{9,1... | collective-permute-start | bytes 786440 | tf_op jit(solution)/shard_map/ppermute | solution.py:197
  51.4 23.9 %collective-permute-start.6 = (f32[4,128,128]{2,1,0:T(8,128)}, f32[4,128,128]{2,1,0:T(8,128)S(1)}, u32[]{:S(2)}, u32[]{:S(2)}) collective-permute-start(f32[4,128,128]{2,1,0:T(8,128)} %get-tuple-element.13), channel_id=1, source_target_pairs={{0,3},{3,0},{1,2},{2,1},{4,7},{7,4},{5,6},{6,5},{8,11},{11,8},{9,1... | collective-permute-start | bytes 786440 | tf_op jit(solution)/shard_map/ppermute | solution.py:197
  75.3 0.7 copy-start.6
  76.0 0.7 copy-start.7
  80.0 0.7 copy-start.3
  121.5 13.4 %collective-permute-start.8 = (f32[67,8,128]{2,1,0:T(8,128)S(1)}, f32[67,8,128]{2,1,0:T(8,128)S(1)}, u32[]{:S(2)}, u32[]{:S(2)}) collective-permute-start(f32[67,8,128]{2,1,0:T(8,128)S(1)} %get-tuple-element.20), channel_id=1, source_target_pairs={{0,16},{1,17},{16,32},{17,33},{32,48},{33,49},{48,2},{49,3},{2,18}... | collective-permute-start | bytes 823304 | tf_op jit(solution)/shard_map/ppermute | solution.py:31
  124.5 13.6 %collective-permute-start.10 = (f32[67,8,128]{2,1,0:T(8,128)S(1)}, f32[67,8,128]{2,1,0:T(8,128)S(1)}, u32[]{:S(2)}, u32[]{:S(2)}) collective-permute-start(f32[67,8,128]{2,1,0:T(8,128)S(1)} %get-tuple-element.21), channel_id=1, source_target_pairs={{0,32},{1,35},{16,48},{17,51},{32,2},{33,1},{48,18},{49,17},{2,34}... | collective-permute-start | bytes 823304 | tf_op jit(solution)/shard_map/ppermute | solution.py:31
  129.2 12.4 %collective-permute-start.9 = (f32[67,8,128]{2,1,0:T(8,128)S(1)}, f32[67,8,128]{2,1,0:T(8,128)S(1)}, u32[]{:S(2)}, u32[]{:S(2)}) collective-permute-start(f32[67,8,128]{2,1,0:T(8,128)S(1)} %get-tuple-element.22), channel_id=1, source_target_pairs={{0,50},{1,51},{16,0},{17,1},{32,16},{33,17},{48,32},{49,33},{2,48}... | collective-permute-start | bytes 823304 | tf_op jit(solution)/shard_map/ppermute | solution.py:31
  141.7 28.2 %copy-start.4 = (f32[128,256]{1,0:T(8,128)S(1)}, f32[128,256]{1,0:T(8,128)}, u32[]{:S(2)}) copy-start(f32[128,256]{1,0:T(8,128)} %copy-done.3) | copy-start | bytes 393220
  141.8 12.3 %collective-permute-start.11 = (f32[35,8,128]{2,1,0:T(8,128)S(1)}, f32[35,8,128]{2,1,0:T(8,128)S(1)}, u32[]{:S(2)}, u32[]{:S(2)}) collective-permute-start(f32[35,8,128]{2,1,0:T(8,128)S(1)} %pad_maximum_fusion.2), channel_id=1, source_target_pairs={{0,2},{2,0},{1,3},{3,1},{4,6},{6,4},{5,7},{7,5},{8,10},{10,8},{9,1... | collective-permute-start | bytes 430088 | tf_op jit(solution)/shard_map/ppermute | solution.py:21
  155.0 14.9 %all-to-all-start.3 = ((f32[32,3,8,128]{3,2,1,0:T(8,128)}), f32[32,3,8,128]{3,2,1,0:T(8,128)S(1)}, u32[]{:S(2)}, u32[]{:S(2)}) async-start(f32[32,3,8,128]{3,2,1,0:T(8,128)} %pad_maximum_fusion.1), calls=%async_computation.3 | async-start | bytes 786432 | tf_op jit(solution)/shard_map/all_to_all | solution.py:35

commit v5 on v4

--- a/solution.py
+++ b/solution.py
@@ -55,10 +55,10 @@
     )
 
 
-def pack_kernel(where_ref, rows_ref, wanted_ref, out_ref):
+def pack_kernel(rows_ref, wanted_ref, out_ref):
     for h in range(2):
 
-        @pl.when(where_ref[0] == h)
+        @pl.when(lax.axis_index("c") == h)
         def _():
             for b in range(4):
                 half = rows_ref[128 * b : 128 * (b + 1), 128 * h : 128 * (h + 1)]
@@ -67,40 +67,41 @@
     out_ref[:, 4] = jnp.broadcast_to(wanted_ref[...].reshape(1, 1, 128), (16, 8, 128))
 
 
-def row_of(where_ref, near_ref, far_ref, q, c, place):
+def row_of(near_ref, far_ref, q, c, place):
     def asked(slot):
         source, core, k = slot // 8, slot // 4 % 2, slot % 4
         index_ref = far_ref if source else near_ref
         return index_ref[q, 16 * core + 8 * source + 4 * c + k]
 
     if place in (0, 8):
-        return jnp.where(8 * where_ref[1] == place, asked(15), asked(place))
+        return jnp.where(8 * lax.axis_index("zh") == place, asked(15), asked(place))
     return asked(place)
 
 
-def gather_kernel(where_ref, near_ref, far_ref, table_ref, out_ref):
+def gather_kernel(near_ref, far_ref, table_ref, out_ref):
     def one(q, carry):
         for c in range(2):
             for slot in range(15):
-                row = row_of(where_ref, near_ref, far_ref, q, c, slot)
+                row = row_of(near_ref, far_ref, q, c, slot)
                 out_ref[q * 2 + c, slot] = table_ref[row]
         return carry
 
     lax.fori_loop(0, 16, one, 0)
 
 
-def scatter_kernel(where_ref, near_ref, far_ref, got_ref, out_ref, even_ref, odd_ref):
+def scatter_kernel(near_ref, far_ref, got_ref, bias_ref, out_ref, even_ref, odd_ref):
     even_ref[...] = jnp.zeros_like(even_ref)
     odd_ref[...] = jnp.zeros_like(odd_ref)
 
     def one(q, carry):
         for slot in range(15):
-            even_ref[row_of(where_ref, near_ref, far_ref, q, 0, slot)] += got_ref[q, 0, slot]
-            odd_ref[row_of(where_ref, near_ref, far_ref, q, 1, slot)] += got_ref[q, 1, slot]
+            even_ref[row_of(near_ref, far_ref, q, 0, slot)] += got_ref[q, 0, slot]
+            odd_ref[row_of(near_ref, far_ref, q, 1, slot)] += got_ref[q, 1, slot]
         return carry
 
     lax.fori_loop(0, 16, one, 0)
-    sums = [jnp.sum(got_ref[:, 0, 15 + t] + got_ref[:, 1, 15 + t], axis=0) for t in range(3)]
+    sums = [jnp.sum(got_ref[:, 0, 15 + t] + got_ref[:, 1, 15 + t], axis=0) for t in range(2)]
+    sums.append(bias_ref[...])
     for plane in range(4):
         for part in range(3):
             out_ref[plane, part] = sums[part]
@@ -108,11 +109,12 @@
         out_ref[plane, 3:67] = even_ref[rows] + odd_ref[rows]
 
 
-def unpack_kernel(home_ref, local_ref, feats_ref, weight_ref):
+def unpack_kernel(home_ref, local_ref, feats_ref, weight_ref, bias_ref):
+    bias_ref[...] = jnp.sum(home_ref[:, 0, 3] + home_ref[:, 1, 3], axis=0)
     for h in range(2):
         columns = slice(128 * h, 128 * (h + 1))
         feats_ref[:, columns] = home_ref[:, h, 0].reshape(128, 128) + local_ref[:, columns]
-        weight_ref[:, columns] = home_ref[:, h, 1:].reshape(256, 128)
+        weight_ref[:, columns] = home_ref[:, h, 1:3].reshape(256, 128)
 
 
 def dot(a, b):
@@ -135,7 +137,6 @@
 
 def middle_kernel(
     scale,
-    where_ref,
     own_ref,
     beside_ref,
     across_ref,
@@ -144,12 +145,12 @@
     got_ref,
     cot_ref,
     weight_ref,
-    bias_ref,
     layer_ref,
     out_ref,
     local_ref,
+    bias_tile_ref,
 ):
-    core, half = where_ref[0], where_ref[1]
+    core, half = lax.axis_index("c"), lax.axis_index("zh")
     tiles = []
     for near_ref, far_ref in ((own_ref, beside_ref), (across_ref, opposite_ref)):
         for c in range(2):
@@ -164,11 +165,12 @@
         for j in range(15)
     ]
     hidden = dot(tiles, jnp.concatenate(rows + [rows_ref[...]], axis=0))
-    pre = dot(hidden, weight_ref[...]) + bias_ref[...]
+    weight = weight_ref[:256]
+    pre = dot(hidden, weight) + weight_ref[256:257]
     grow = jnp.exp(jnp.minimum(pre, 0.0))
     layer_ref[...] = jnp.where(pre > 0, pre, grow - 1.0)
     grad_pre = cot_ref[...] * jnp.where(pre > 0, 1.0, grow)
-    grad_hidden = dot_last(grad_pre, weight_ref[...])
+    grad_hidden = dot_last(grad_pre, weight)
     terms = dot_first(tiles, grad_hidden)
     local_ref[...] = terms[1920:]
     grad_weight = dot_first(hidden, grad_pre) * scale
@@ -176,19 +178,18 @@
     row_ids = lax.broadcasted_iota(jnp.int32, (8, 128), 0)
     bias_tile = jnp.where(row_ids == 0, grad_bias[:, :128], 0.0)
     bias_tile = jnp.where(row_ids == 1, grad_bias[:, 128:], bias_tile)
+    bias_tile_ref[...] = bias_tile
     for h in range(2):
         columns = slice(128 * h, 128 * (h + 1))
         for j in range(15):
             out_ref[:, h, j] = terms[128 * j : 128 * (j + 1), columns].reshape(16, 8, 128)
         out_ref[:, h, 15:17] = grad_weight[:, columns].reshape(16, 2, 8, 128)
-        out_ref[:, h, 17] = jnp.broadcast_to(bias_tile.reshape(1, 8, 128), (16, 8, 128))
 
 
 def body(node_feats, operator_tiles, tile_cols, weight, layer_bias, cotangent):
     level = lax.axis_index("zl")
     half = lax.axis_index("zh")
     core = lax.axis_index("c")
-    where = jnp.stack([core, half]).astype(jnp.int32)
     scale = 1.0 / math.sqrt(32768)
 
     mine = 2 * half + core
@@ -218,9 +219,9 @@
     packed = call(
         pack_kernel,
         jax.ShapeDtypeStruct((16, 5, 8, 128), F32),
-        [smem(), vmem(), vmem()],
+        [vmem(), vmem()],
         moved=1 << 20,
-    )(where, node_feats, wanted)
+    )(node_feats, wanted)
     arrived = exchange(packed, PLANE)
     plane = arrived[:, :4].reshape(64, 8, 128)
     table = jnp.concatenate(
@@ -230,31 +231,32 @@
     index = (asked.astype(jnp.int32), shift(asked, "zh", 1).astype(jnp.int32))
 
     leaving = (tiles_for(2 * (1 - half) + core), tiles_for(2 * (1 - half) + 1 - core))
-    table, leaving = lax.optimization_barrier((table, leaving))
+    affine = jnp.concatenate([weight, jnp.broadcast_to(layer_bias, (8, 256))], axis=0)
+    table, leaving, affine = lax.optimization_barrier((table, leaving, affine))
     across = swapped(leaving[0], [(0, 2), (2, 0), (1, 3), (3, 1)])
     opposite = swapped(leaving[1], [(0, 3), (3, 0), (1, 2), (2, 1)])
     sent = call(
         gather_kernel,
         jax.ShapeDtypeStruct((32, 15, 8, 128), F32),
-        [smem(), smem(), smem(), vmem()],
+        [smem(), smem(), vmem()],
         moved=3 << 20,
-    )(where, *index, table)
+    )(*index, table)
     got = exchange(sent, GROUP).reshape(16, 2, 15, 8, 128)
     def middle(*refs):
         middle_kernel(scale, *refs)
 
-    layer_out, terms, local = call(
+    layer_out, terms, local, bias_part = call(
         middle,
         (
             jax.ShapeDtypeStruct((128, 256), F32),
-            jax.ShapeDtypeStruct((16, 2, 18, 8, 128), F32),
+            jax.ShapeDtypeStruct((16, 2, 17, 8, 128), F32),
             jax.ShapeDtypeStruct((128, 256), F32),
+            jax.ShapeDtypeStruct((8, 128), F32),
         ),
-        [smem()] + [vmem()] * 9,
+        [vmem()] * 8,
         flops=318767104 * 3,
         moved=6 << 20,
     )(
-        where,
         tiles_for(mine),
         beside,
         across,
@@ -262,17 +264,16 @@
         rows,
         got,
         cotangent,
-        weight,
-        layer_bias.reshape(1, 256),
-    )
-    back = exchange(terms.reshape(32, 18, 8, 128), GROUP).reshape(16, 2, 18, 8, 128)
+        affine,
+    )
+    back = exchange(terms.reshape(32, 17, 8, 128), GROUP).reshape(16, 2, 17, 8, 128)
     sums = call(
         scatter_kernel,
         jax.ShapeDtypeStruct((4, 67, 8, 128), F32),
-        [smem(), smem(), smem(), vmem()],
+        [smem(), smem(), vmem(), vmem()],
         scratch=[pltpu.VMEM((256, 8, 128), F32)] * 2,
         moved=4 << 20,
-    )(where, *index, back)
+    )(*index, back, bias_part)
     total = sums[0] + ring(sums[1], 1) + ring(sums[3], -1) + ring(sums[2], 2)
     by_owner = total[3:].reshape(16, 4, 8, 128)
     staying = lax.dynamic_slice_in_dim(by_owner, 2 * half, 2, 1).reshape(32, 8, 128)
@@ -284,19 +285,23 @@
         jnp.concatenate(
             [
                 final[:32, None],
-                jnp.broadcast_to(final[None, 32:34], (32, 2, 8, 128)),
+                jnp.broadcast_to(final[None, 32:35], (32, 3, 8, 128)),
             ],
             axis=1,
         ),
         GROUP,
-    ).reshape(16, 2, 3, 8, 128)
-    grad_feats, grad_weight = call(
+    ).reshape(16, 2, 4, 8, 128)
+    grad_feats, grad_weight, bias_sum = call(
         unpack_kernel,
-        (jax.ShapeDtypeStruct((128, 256), F32), jax.ShapeDtypeStruct((256, 256), F32)),
+        (
+            jax.ShapeDtypeStruct((128, 256), F32),
+            jax.ShapeDtypeStruct((256, 256), F32),
+            jax.ShapeDtypeStruct((8, 128), F32),
+        ),
         [vmem(), vmem()],
         moved=1 << 20,
     )(home, local)
-    grad_bias = final[34, :2].reshape(256)
+    grad_bias = bias_sum[:2].reshape(256)
     return layer_out, grad_feats, grad_weight, grad_bias
 
 

time: 171 us -> 168 us (0.982)
  blocking collectives: 51.4 us -> 65.9 us
  waiting for transfers between devices: 61.2 us -> 51.6 us
  starting transfers between devices: 39.9 us -> 35.2 us
  Pallas kernels: 9.65 us -> 7.34 us
    all_to_all x2 -> x3, blocking collectives: 51.4 us -> 65.9 us  [exchange(): return lax.all_to_all(value, axes, 0, 0, tiled=True)]
    all_to_all x2 -> x1, waiting for transfers between devices: 9.85 us -> 0.01 us  [exchange(): return lax.all_to_all(value, axes, 0, 0, tiled=True)]
    all_to_all x2 -> x1, starting transfers between devices: 9.92 us -> 5.42 us  [exchange(): return lax.all_to_all(value, axes, 0, 0, tiled=True)]
  transfers between devices with their start and end apart: 14 -> 13, of which waited for: 10 -> 9; matrix products, arithmetic and copies ran while one was open for 1% -> 1% of each run, Pallas kernels for 0% -> 0%
where the time goes in v5:
time: 168 us
  blocking collectives  65.9 us (39%)
  waiting for transfers between devices  51.6 us (31%)
  starting transfers between devices  35.2 us (21%)
  Pallas kernels  7.34 us (4%)
  local copies, waits for them, and re-layouts  6.43 us (4%)
    all_to_all x3, blocking collectives, exchange(): return lax.all_to_all(value, axes, 0, 0, tiled=True)  65.9 us
    ppermute x3, waiting for transfers between devices, swapped(): return lax.ppermute(tiles, ('zh', 'c'), pairs)  21 us
    ppermute x3, waiting for transfers between devices, shift(): lax.ppermute(value, axis, [(s, (s + steps) % count) for s in range(count)])  18.1 us
    ppermute x6, starting transfers between devices, ring(): return lax.ppermute(value, ('zl', 'zh', 'c'), pairs)  13.5 us
    ppermute x6, waiting for transfers between devices, ring(): return lax.ppermute(value, ('zl', 'zh', 'c'), pairs)  12.5 us
    ppermute x3, starting transfers between devices, shift(): lax.ppermute(value, axis, [(s, (s + steps) % count) for s in range(count)])  10.1 us
    ppermute x3, starting transfers between devices, swapped(): return lax.ppermute(tiles, ('zh', 'c'), pairs)  6.14 us
    all_to_all x1, starting transfers between devices, exchange(): return lax.all_to_all(value, axes, 0, 0, tiled=True)  5.42 us
  transfers between devices with their start and end apart: 13, of which 9 were waited for; matrix products, arithmetic and copies ran while one was open for 1% of the time, Pallas kernels for 0%

profile of v5, /device:TPU:1, one launch (start us, length us, event | category | flops | bytes accessed | tf_op | source)
XLA Modules:
  0.0 167.8 jit_solution(16744336120983601441)
XLA Ops:
  0.6 0.8 reshape.100
  1.5 0.1 concatenate.39
  1.6 3.3 %collective-permute-start.1 = (f32[1,16]{1,0:T(1,128)S(1)}, f32[1,16]{1,0:T(1,128)S(1)}, u32[]{:S(2)}, u32[]{:S(2)}) collective-permute-start(f32[1,16]{1,0:T(1,128)S(1)} %concatenate.39), channel_id=1, source_target_pairs={{0,1},{1,0},{2,3},{3,2},{4,5},{5,4},{6,7},{7,6},{8,9},{9,8},{10,11... | collective-permute-start | bytes 200 | tf_op jit(solution)/shard_map/ppermute | solution.py:21
  4.8 0.8 collective-permute-done.1
  5.7 0.1 broadcast_select_fusion
  5.7 1.0 copy-done.1
  6.8 13.0 %all_to_all.20 = f32[16,5,8,128]{3,2,1,0:T(8,128)S(1)} all-to-all(f32[16,5,8,128]{3,2,1,0:T(8,128)S(1)} %shard_map.93), channel_id=1, replica_groups=mesh['x'=4,'zl'=4,'y'=4,'zh'=2,'c'=2] {'x','y'}, dimensions={0} | all-to-all | bytes 655360 | tf_op jit(solution)/shard_map/all_to_all | solution.py:35
  19.8 1.7 %collective-permute-start.4 = (f32[64,8,128]{2,1,0:T(8,128)S(1)}, f32[64,8,128]{2,1,0:T(8,128)S(1)}, u32[]{:S(2)}, u32[]{:S(2)}) collective-permute-start(f32[64,8,128]{2,1,0:T(8,128)S(1)} %bitcast.42), channel_id=1, source_target_pairs={{0,16},{1,17},{16,32},{17,33},{32,48},{33,49},{48,2},{49,3},{2,18}... | collective-permute-start | bytes 786440 | tf_op jit(solution)/shard_map/ppermute | solution.py:31
  21.5 3.0 %collective-permute-start.3 = (f32[64,8,128]{2,1,0:T(8,128)S(1)}, f32[64,8,128]{2,1,0:T(8,128)S(1)}, u32[]{:S(2)}, u32[]{:S(2)}) collective-permute-start(f32[64,8,128]{2,1,0:T(8,128)S(1)} %bitcast.43), channel_id=1, source_target_pairs={{0,34},{1,33},{16,50},{17,49},{32,0},{33,3},{48,16},{49,19},{2,32}... | collective-permute-start | bytes 786440 | tf_op jit(solution)/shard_map/ppermute | solution.py:31
  24.5 1.1 collective-permute-start.2
  25.6 0.9 dynamic-slice_bitcast_fusion
  26.5 5.0 %collective-permute-start.7 = (f32[16,128]{1,0:T(8,128)S(1)}, f32[16,128]{1,0:T(8,128)S(1)}, u32[]{:S(2)}, u32[]{:S(2)}) collective-permute-start(f32[16,128]{1,0:T(8,128)S(1)} %bitcast.48), channel_id=1, source_target_pairs={{0,2},{2,0},{1,3},{3,1},{4,6},{6,4},{5,7},{7,5},{8,10},{10,8},{9,1... | collective-permute-start | bytes 24584 | tf_op jit(solution)/shard_map/ppermute | solution.py:21
  31.6 6.8 %collective-permute-done.7 = f32[16,128]{1,0:T(8,128)S(1)} collective-permute-done((f32[16,128]{1,0:T(8,128)S(1)}, f32[16,128]{1,0:T(8,128)S(1)}, u32[]{:S(2)}, u32[]{:S(2)}) %collective-permute-start.7) | collective-permute-done | bytes 8224 | tf_op jit(solution)/shard_map/ppermute | solution.py:21
  38.4 0.0 collective-permute-done.4
  38.5 0.1 collective-permute-done.3
  38.6 0.0 collective-permute-done.2
  38.6 0.1 pad_maximum_fusion.table_ref
  38.6 1.5 shard_map.94
  40.2 1.3 copy-done
  41.5 5.4 %all-to-all-start.1 = ((f32[32,15,8,128]{3,2,1,0:T(8,128)}), f32[32,15,8,128]{3,2,1,0:T(8,128)S(1)}, u32[]{:S(2)}, u32[]{:S(2)}) async-start(f32[32,15,8,128]{3,2,1,0:T(8,128)} %copy-done), calls=%async_computation.1 | async-start | bytes 3932160 | tf_op jit(solution)/shard_map/all_to_all | solution.py:35
  46.9 0.4 collective-permute-start
  47.3 3.8 %collective-permute-start.5 = (f32[4,128,128]{2,1,0:T(8,128)}, f32[4,128,128]{2,1,0:T(8,128)S(1)}, u32[]{:S(2)}, u32[]{:S(2)}) collective-permute-start(f32[4,128,128]{2,1,0:T(8,128)} %get-tuple-element.15), channel_id=1, source_target_pairs={{0,2},{2,0},{1,3},{3,1},{4,6},{6,4},{5,7},{7,5},{8,10},{10,8},{9,1... | collective-permute-start | bytes 786440 | tf_op jit(solution)/shard_map/ppermute | solution.py:198
  51.1 2.0 %collective-permute-start.6 = (f32[4,128,128]{2,1,0:T(8,128)}, f32[4,128,128]{2,1,0:T(8,128)S(1)}, u32[]{:S(2)}, u32[]{:S(2)}) collective-permute-start(f32[4,128,128]{2,1,0:T(8,128)} %get-tuple-element.16), channel_id=1, source_target_pairs={{0,3},{3,0},{1,2},{2,1},{4,7},{7,4},{5,6},{6,5},{8,11},{11,8},{9,1... | collective-permute-start | bytes 786440 | tf_op jit(solution)/shard_map/ppermute | solution.py:198
  53.0 0.9 constant_dynamic-slice_fusion.2.refs_4_
  53.9 0.0 collective-permute-done.refs_1_
  53.9 9.7 %collective-permute-done.5.refs_2_ = f32[4,128,128]{2,1,0:T(8,128)S(1)} collective-permute-done((f32[4,128,128]{2,1,0:T(8,128)}, f32[4,128,128]{2,1,0:T(8,128)S(1)}, u32[]{:S(2)}, u32[]{:S(2)}) %collective-permute-start.5) | collective-permute-done | bytes 262176 | tf_op jit(solution)/shard_map/ppermute | solution.py:198
  63.6 11.3 %collective-permute-done.6.refs_3_ = f32[4,128,128]{2,1,0:T(8,128)S(1)} collective-permute-done((f32[4,128,128]{2,1,0:T(8,128)}, f32[4,128,128]{2,1,0:T(8,128)S(1)}, u32[]{:S(2)}, u32[]{:S(2)}) %collective-permute-start.6) | collective-permute-done | bytes 262176 | tf_op jit(solution)/shard_map/ppermute | solution.py:198
  75.0 0.0 all-to-all-done.1
  75.0 2.8 %shard_map.95 = (f32[128,256]{1,0:T(8,128)}, f32[16,2,17,8,128]{4,3,2,1,0:T(8,128)S(1)}, f32[128,256]{1,0:T(8,128)S(1)}, f32[8,128]{1,0:T(8,128)S(1)}) custom-call(f32[4,128,128]{2,1,0:T(8,128)S(1)} %get-tuple-element.31.refs_0_, f32[4,128,128]{2,1,0:T(8,128)S(1)} %collective-permute-done.refs_1_, f32[4,128,128]{2,1,0:T(8,128)S(1)} %collective-permute-done.5.refs_2_, ...), custom_call_target="tpu_custom_call" | custom-call | flops 956301312 | bytes 6291456 | tf_op jit(solution)/shard_map/pallas_call | solution.py:248
  77.7 0.0 copy-start.3
  77.7 0.6 copy-done.3
  78.4 37.4 %all_to_all.21 = f32[32,17,8,128]{3,2,1,0:T(8,128)S(1)} all-to-all(f32[32,17,8,128]{3,2,1,0:T(8,128)S(1)} %bitcast.39), channel_id=1, replica_groups=mesh['x'=4,'zl'=4,'y'=4,'zh'=2,'c'=2] {'x','y','c'}, dimensions={0} | all-to-all | bytes 4456448 | tf_op jit(solution)/shard_map/all_to_all | solution.py:35
  115.8 2.3 %shard_map.96 = f32[4,67,8,128]{3,2,1,0:T(8,128)S(1)} custom-call(s32[16,128]{1,0:T(8,128)S(1)} %convert_element_type.12.near_ref, s32[16,128]{1,0:T(8,128)S(1)} %copy-done.6, f32[16,2,17,8,128]{4,3,2,1,0:T(8,128)S(1)} %bitcast.37, f32[8,128]{1,0:T(8,128)S(1)} %get-tuple-element.21.bias_ref), custom_call_target="tpu_custom_call" | custom-call | bytes 4194304 | tf_op jit(solution)/shard_map/pallas_call | solution.py:270
  118.1 0.1 slice_bitcast_fusion.2
  118.1 3.1 %collective-permute-start.8 = (f32[67,8,128]{2,1,0:T(8,128)S(1)}, f32[67,8,128]{2,1,0:T(8,128)S(1)}, u32[]{:S(2)}, u32[]{:S(2)}) collective-permute-start(f32[67,8,128]{2,1,0:T(8,128)S(1)} %get-tuple-element.26), channel_id=1, source_target_pairs={{0,16},{1,17},{16,32},{17,33},{32,48},{33,49},{48,2},{49,3},{2,18}... | collective-permute-start | bytes 823304 | tf_op jit(solution)/shard_map/ppermute | solution.py:31
  121.2 4.6 %collective-permute-start.10 = (f32[67,8,128]{2,1,0:T(8,128)S(1)}, f32[67,8,128]{2,1,0:T(8,128)S(1)}, u32[]{:S(2)}, u32[]{:S(2)}) collective-permute-start(f32[67,8,128]{2,1,0:T(8,128)S(1)} %get-tuple-element.27), channel_id=1, source_target_pairs={{0,32},{1,35},{16,48},{17,51},{32,2},{33,1},{48,18},{49,17},{2,34}... | collective-permute-start | bytes 823304 | tf_op jit(solution)/shard_map/ppermute | solution.py:31
  125.8 0.0 collective-permute-start.9
  125.8 5.4 %collective-permute-done.8 = f32[67,8,128]{2,1,0:T(8,128)S(1)} collective-permute-done((f32[67,8,128]{2,1,0:T(8,128)S(1)}, f32[67,8,128]{2,1,0:T(8,128)S(1)}, u32[]{:S(2)}, u32[]{:S(2)}) %collective-permute-start.8) | collective-permute-done | bytes 274464 | tf_op jit(solution)/shard_map/ppermute | solution.py:31
  131.2 3.7 %collective-permute-done.10 = f32[67,8,128]{2,1,0:T(8,128)S(1)} collective-permute-done((f32[67,8,128]{2,1,0:T(8,128)S(1)}, f32[67,8,128]{2,1,0:T(8,128)S(1)}, u32[]{:S(2)}, u32[]{:S(2)}) %collective-permute-start.10) | collective-permute-done | bytes 274464 | tf_op jit(solution)/shard_map/ppermute | solution.py:31
  134.9 3.3 %collective-permute-done.9 = f32[67,8,128]{2,1,0:T(8,128)S(1)} collective-permute-done((f32[67,8,128]{2,1,0:T(8,128)S(1)}, f32[67,8,128]{2,1,0:T(8,128)S(1)}, u32[]{:S(2)}, u32[]{:S(2)}) %collective-permute-start.9) | collective-permute-done | bytes 274464 | tf_op jit(solution)/shard_map/ppermute | solution.py:31
  138.2 0.1 fusion.2
  138.4 0.0 copy-start.4
  138.4 1.9 %collective-permute-start.11 = (f32[35,8,128]{2,1,0:T(8,128)S(1)}, f32[35,8,128]{2,1,0:T(8,128)S(1)}, u32[]{:S(2)}, u32[]{:S(2)}) collective-permute-start(f32[35,8,128]{2,1,0:T(8,128)S(1)} %pad_maximum_fusion.3), channel_id=1, source_target_pairs={{0,2},{2,0},{1,3},{3,1},{4,6},{6,4},{5,7},{7,5},{8,10},{10,8},{9,1... | collective-permute-start | bytes 430088 | tf_op jit(solution)/shard_map/ppermute | solution.py:21
  140.3 10.4 %collective-permute-done.11 = f32[35,8,128]{2,1,0:T(8,128)S(1)} collective-permute-done((f32[35,8,128]{2,1,0:T(8,128)S(1)}, f32[35,8,128]{2,1,0:T(8,128)S(1)}, u32[]{:S(2)}, u32[]{:S(2)}) %collective-permute-start.11) | collective-permute-done | bytes 143392 | tf_op jit(solution)/shard_map/ppermute | solution.py:21
  150.8 0.1 pad_maximum_fusion.1
  150.9 15.6 %all_to_all.22 = f32[32,4,8,128]{3,2,1,0:T(8,128)S(1)} all-to-all(f32[32,4,8,128]{3,2,1,0:T(8,128)S(1)} %pad_maximum_fusion.1), channel_id=1, replica_groups=mesh['x'=4,'zl'=4,'y'=4,'zh'=2,'c'=2] {'x','y','c'}, dimensions={0} | all-to-all | bytes 1048576 | tf_op jit(solution)/shard_map/all_to_all | solution.py:35
  166.5 0.8 shard_map.97
  167.3 0.6 slice_bitcast_fusion.5
  (34 shorter events, 0.3 us)
Async XLA Ops:
  1.6 4.1 %collective-permute-start.1 = (f32[1,16]{1,0:T(1,128)S(1)}, f32[1,16]{1,0:T(1,128)S(1)}, u32[]{:S(2)}, u32[]{:S(2)}) collective-permute-start(f32[1,16]{1,0:T(1,128)S(1)} %concatenate.39), channel_id=1, source_target_pairs={{0,1},{1,0},{2,3},{3,2},{4,5},{5,4},{6,7},{7,6},{8,9},{9,8},{10,11... | collective-permute-start | bytes 200 | tf_op jit(solution)/shard_map/ppermute | solution.py:21
  5.7 1.0 copy-start.1
  6.8 18.8 %copy-start.7 = (f32[4,4,128,128]{3,2,1,0:T(8,128)S(1)}, f32[4,4,128,128]{3,2,1,0:T(8,128)}, u32[]{:S(2)}) copy-start(f32[4,4,128,128]{3,2,1,0:T(8,128)} %param.7) | copy-start | bytes 3145732
  6.8 24.8 %copy-start.9 = (f32[256]{0:T(256)S(1)}, f32[256]{0:T(256)}, u32[]{:S(2)}) copy-start(f32[256]{0:T(256)} %param.10) | copy-start | bytes 3076
  6.8 24.8 %copy-start.8 = (f32[256,256]{1,0:T(8,128)S(1)}, f32[256,256]{1,0:T(8,128)}, u32[]{:S(2)}) copy-start(f32[256,256]{1,0:T(8,128)} %param.9) | copy-start | bytes 786436
  19.8 18.6 %collective-permute-start.4 = (f32[64,8,128]{2,1,0:T(8,128)S(1)}, f32[64,8,128]{2,1,0:T(8,128)S(1)}, u32[]{:S(2)}, u32[]{:S(2)}) collective-permute-start(f32[64,8,128]{2,1,0:T(8,128)S(1)} %bitcast.42), channel_id=1, source_target_pairs={{0,16},{1,17},{16,32},{17,33},{32,48},{33,49},{48,2},{49,3},{2,18}... | collective-permute-start | bytes 786440 | tf_op jit(solution)/shard_map/ppermute | solution.py:31
  21.5 17.0 %collective-permute-start.3 = (f32[64,8,128]{2,1,0:T(8,128)S(1)}, f32[64,8,128]{2,1,0:T(8,128)S(1)}, u32[]{:S(2)}, u32[]{:S(2)}) collective-permute-start(f32[64,8,128]{2,1,0:T(8,128)S(1)} %bitcast.43), channel_id=1, source_target_pairs={{0,34},{1,33},{16,50},{17,49},{32,0},{33,3},{48,16},{49,19},{2,32}... | collective-permute-start | bytes 786440 | tf_op jit(solution)/shard_map/ppermute | solution.py:31
  24.5 14.1 %collective-permute-start.2 = (f32[64,8,128]{2,1,0:T(8,128)S(1)}, f32[64,8,128]{2,1,0:T(8,128)S(1)}, u32[]{:S(2)}, u32[]{:S(2)}) collective-permute-start(f32[64,8,128]{2,1,0:T(8,128)S(1)} %bitcast.44), channel_id=1, source_target_pairs={{0,50},{1,51},{16,0},{17,1},{32,16},{33,17},{48,32},{49,33},{2,48}... | collective-permute-start | bytes 786440 | tf_op jit(solution)/shard_map/ppermute | solution.py:31
  26.5 11.9 %collective-permute-start.7 = (f32[16,128]{1,0:T(8,128)S(1)}, f32[16,128]{1,0:T(8,128)S(1)}, u32[]{:S(2)}, u32[]{:S(2)}) collective-permute-start(f32[16,128]{1,0:T(8,128)S(1)} %bitcast.48), channel_id=1, source_target_pairs={{0,2},{2,0},{1,3},{3,1},{4,6},{6,4},{5,7},{7,5},{8,10},{10,8},{9,1... | collective-permute-start | bytes 24584 | tf_op jit(solution)/shard_map/ppermute | solution.py:21
  38.4 1.7 %copy-start.5 = (s32[16,128]{1,0:T(8,128)}, s32[16,128]{1,0:T(8,128)S(1)}, u32[]{:S(2)}) copy-start(s32[16,128]{1,0:T(8,128)S(1)} %convert_element_type.13.far_ref) | copy-start | bytes 24580
  40.2 1.3 copy-start
  41.5 33.5 %copy-start.2 = (f32[128,256]{1,0:T(8,128)S(1)}, f32[128,256]{1,0:T(8,128)}, u32[]{:S(2)}) copy-start(f32[128,256]{1,0:T(8,128)} %refs_6_.1) | copy-start | bytes 393220
  41.5 33.5 %all-to-all-start.1 = ((f32[32,15,8,128]{3,2,1,0:T(8,128)}), f32[32,15,8,128]{3,2,1,0:T(8,128)S(1)}, u32[]{:S(2)}, u32[]{:S(2)}) async-start(f32[32,15,8,128]{3,2,1,0:T(8,128)} %copy-done), calls=%async_computation.1 | async-start | bytes 3932160 | tf_op jit(solution)/shard_map/all_to_all | solution.py:35
  46.9 7.1 %collective-permute-start = (f32[4,128,128]{2,1,0:T(8,128)}, f32[4,128,128]{2,1,0:T(8,128)S(1)}, u32[]{:S(2)}, u32[]{:S(2)}) collective-permute-start(f32[4,128,128]{2,1,0:T(8,128)} %get-tuple-element.30), channel_id=1, source_target_pairs={{0,1},{1,0},{2,3},{3,2},{4,5},{5,4},{6,7},{7,6},{8,9},{9,8},{10,11... | collective-permute-start | bytes 786440 | tf_op jit(solution)/shard_map/ppermute | solution.py:198
  47.3 16.4 %collective-permute-start.5 = (f32[4,128,128]{2,1,0:T(8,128)}, f32[4,128,128]{2,1,0:T(8,128)S(1)}, u32[]{:S(2)}, u32[]{:S(2)}) collective-permute-start(f32[4,128,128]{2,1,0:T(8,128)} %get-tuple-element.15), channel_id=1, source_target_pairs={{0,2},{2,0},{1,3},{3,1},{4,6},{6,4},{5,7},{7,5},{8,10},{10,8},{9,1... | collective-permute-start | bytes 786440 | tf_op jit(solution)/shard_map/ppermute | solution.py:198
  51.1 23.9 %collective-permute-start.6 = (f32[4,128,128]{2,1,0:T(8,128)}, f32[4,128,128]{2,1,0:T(8,128)S(1)}, u32[]{:S(2)}, u32[]{:S(2)}) collective-permute-start(f32[4,128,128]{2,1,0:T(8,128)} %get-tuple-element.16), channel_id=1, source_target_pairs={{0,3},{3,0},{1,2},{2,1},{4,7},{7,4},{5,6},{6,5},{8,11},{11,8},{9,1... | collective-permute-start | bytes 786440 | tf_op jit(solution)/shard_map/ppermute | solution.py:198
  77.7 0.7 copy-start.3
  78.4 37.4 %copy-start.6 = (s32[16,128]{1,0:T(8,128)S(1)}, s32[16,128]{1,0:T(8,128)}, u32[]{:S(2)}) copy-start(s32[16,128]{1,0:T(8,128)} %copy-done.5) | copy-start | bytes 24580
  118.1 13.1 %collective-permute-start.8 = (f32[67,8,128]{2,1,0:T(8,128)S(1)}, f32[67,8,128]{2,1,0:T(8,128)S(1)}, u32[]{:S(2)}, u32[]{:S(2)}) collective-permute-start(f32[67,8,128]{2,1,0:T(8,128)S(1)} %get-tuple-element.26), channel_id=1, source_target_pairs={{0,16},{1,17},{16,32},{17,33},{32,48},{33,49},{48,2},{49,3},{2,18}... | collective-permute-start | bytes 823304 | tf_op jit(solution)/shard_map/ppermute | solution.py:31
  121.2 13.7 %collective-permute-start.10 = (f32[67,8,128]{2,1,0:T(8,128)S(1)}, f32[67,8,128]{2,1,0:T(8,128)S(1)}, u32[]{:S(2)}, u32[]{:S(2)}) collective-permute-start(f32[67,8,128]{2,1,0:T(8,128)S(1)} %get-tuple-element.27), channel_id=1, source_target_pairs={{0,32},{1,35},{16,48},{17,51},{32,2},{33,1},{48,18},{49,17},{2,34}... | collective-permute-start | bytes 823304 | tf_op jit(solution)/shard_map/ppermute | solution.py:31
  125.8 12.4 %collective-permute-start.9 = (f32[67,8,128]{2,1,0:T(8,128)S(1)}, f32[67,8,128]{2,1,0:T(8,128)S(1)}, u32[]{:S(2)}, u32[]{:S(2)}) collective-permute-start(f32[67,8,128]{2,1,0:T(8,128)S(1)} %get-tuple-element.28), channel_id=1, source_target_pairs={{0,50},{1,51},{16,0},{17,1},{32,16},{33,17},{48,32},{49,33},{2,48}... | collective-permute-start | bytes 823304 | tf_op jit(solution)/shard_map/ppermute | solution.py:31
  138.4 28.1 %copy-start.4 = (f32[128,256]{1,0:T(8,128)S(1)}, f32[128,256]{1,0:T(8,128)}, u32[]{:S(2)}) copy-start(f32[128,256]{1,0:T(8,128)} %copy-done.3) | copy-start | bytes 393220
  138.4 12.3 %collective-permute-start.11 = (f32[35,8,128]{2,1,0:T(8,128)S(1)}, f32[35,8,128]{2,1,0:T(8,128)S(1)}, u32[]{:S(2)}, u32[]{:S(2)}) collective-permute-start(f32[35,8,128]{2,1,0:T(8,128)S(1)} %pad_maximum_fusion.3), channel_id=1, source_target_pairs={{0,2},{2,0},{1,3},{3,1},{4,6},{6,4},{5,7},{7,5},{8,10},{10,8},{9,1... | collective-permute-start | bytes 430088 | tf_op jit(solution)/shard_map/ppermute | solution.py:21

commit v6 on v5

--- a/solution.py
+++ b/solution.py
@@ -110,7 +110,9 @@
 
 
 def unpack_kernel(home_ref, local_ref, feats_ref, weight_ref, bias_ref):
-    bias_ref[...] = jnp.sum(home_ref[:, 0, 3] + home_ref[:, 1, 3], axis=0)
+    total = jnp.sum(home_ref[:, 0, 3] + home_ref[:, 1, 3], axis=0)
+    bias_ref[:, :128] = total[0:1]
+    bias_ref[:, 128:] = total[1:2]
     for h in range(2):
         columns = slice(128 * h, 128 * (h + 1))
         feats_ref[:, columns] = home_ref[:, h, 0].reshape(128, 128) + local_ref[:, columns]
@@ -224,12 +226,12 @@
     )(node_feats, wanted)
     arrived = exchange(packed, PLANE)
     plane = arrived[:, :4].reshape(64, 8, 128)
+    plane, asked = lax.optimization_barrier((plane, arrived[:, 4, 0]))
+    asked_far = shift(asked, "zh", 1)
+    index = (asked.astype(jnp.int32), asked_far.astype(jnp.int32))
     table = jnp.concatenate(
         [plane, ring(plane, -1), ring(plane, -2), ring(plane, 1)], axis=0
     )
-    asked = arrived[:, 4, 0]
-    index = (asked.astype(jnp.int32), shift(asked, "zh", 1).astype(jnp.int32))
-
     leaving = (tiles_for(2 * (1 - half) + core), tiles_for(2 * (1 - half) + 1 - core))
     affine = jnp.concatenate([weight, jnp.broadcast_to(layer_bias, (8, 256))], axis=0)
     table, leaving, affine = lax.optimization_barrier((table, leaving, affine))
@@ -296,12 +298,12 @@
         (
             jax.ShapeDtypeStruct((128, 256), F32),
             jax.ShapeDtypeStruct((256, 256), F32),
-            jax.ShapeDtypeStruct((8, 128), F32),
+            jax.ShapeDtypeStruct((1, 256), F32),
         ),
         [vmem(), vmem()],
         moved=1 << 20,
     )(home, local)
-    grad_bias = bias_sum[:2].reshape(256)
+    grad_bias = bias_sum.reshape(256)
     return layer_out, grad_feats, grad_weight, grad_bias
 
 

time: 168 us -> 168 us (level)
  no operation moved by 1% of the time
where the time goes in v6:
time: 168 us; the launch traced here: 167 us
  blocking collectives  65.9 us (39%)
  waiting for transfers between devices  51.7 us (31%)
  starting transfers between devices  35.2 us (21%)
  Pallas kernels  7.36 us (4%)
  local copies, waits for them, and re-layouts  5.87 us (3%)
    all_to_all x3, blocking collectives, exchange(): return lax.all_to_all(value, axes, 0, 0, tiled=True)  65.9 us
    ppermute x3, waiting for transfers between devices, swapped(): return lax.ppermute(tiles, ('zh', 'c'), pairs)  21 us
    ppermute x3, waiting for transfers between devices, shift(): lax.ppermute(value, axis, [(s, (s + steps) % count) for s in range(count)])  18.1 us
    ppermute x6, starting transfers between devices, ring(): return lax.ppermute(value, ('zl', 'zh', 'c'), pairs)  13.5 us
    ppermute x6, waiting for transfers between devices, ring(): return lax.ppermute(value, ('zl', 'zh', 'c'), pairs)  12.5 us
    ppermute x3, starting transfers between devices, shift(): lax.ppermute(value, axis, [(s, (s + steps) % count) for s in range(count)])  10.1 us
    ppermute x3, starting transfers between devices, swapped(): return lax.ppermute(tiles, ('zh', 'c'), pairs)  6.14 us
    all_to_all x1, starting transfers between devices, exchange(): return lax.all_to_all(value, axes, 0, 0, tiled=True)  5.42 us
  transfers between devices with their start and end apart: 13, of which 9 were waited for; matrix products, arithmetic and copies ran while one was open for 1% of the time, Pallas kernels for 0%

profile of v6, /device:TPU:1, one launch (start us, length us, event | category | flops | bytes accessed | tf_op | source)
XLA Modules:
  0.0 167.3 jit_solution(7807982993891911662)
XLA Ops:
  0.6 0.8 reshape.100
  1.5 0.1 concatenate.39
  1.6 3.3 %collective-permute-start.1 = (f32[1,16]{1,0:T(1,128)S(1)}, f32[1,16]{1,0:T(1,128)S(1)}, u32[]{:S(2)}, u32[]{:S(2)}) collective-permute-start(f32[1,16]{1,0:T(1,128)S(1)} %concatenate.39), channel_id=1, source_target_pairs={{0,1},{1,0},{2,3},{3,2},{4,5},{5,4},{6,7},{7,6},{8,9},{9,8},{10,11... | collective-permute-start | bytes 200 | tf_op jit(solution)/shard_map/ppermute | solution.py:21
  4.8 0.8 collective-permute-done.1
  5.7 0.1 broadcast_select_fusion
  5.7 1.0 copy-done.1
  6.8 13.0 %all_to_all.20 = f32[16,5,8,128]{3,2,1,0:T(8,128)S(1)} all-to-all(f32[16,5,8,128]{3,2,1,0:T(8,128)S(1)} %shard_map.93), channel_id=1, replica_groups=mesh['x'=4,'zl'=4,'y'=4,'zh'=2,'c'=2] {'x','y'}, dimensions={0} | all-to-all | bytes 655360 | tf_op jit(solution)/shard_map/all_to_all | solution.py:35
  19.8 1.7 %collective-permute-start.4 = (f32[64,8,128]{2,1,0:T(8,128)S(1)}, f32[64,8,128]{2,1,0:T(8,128)S(1)}, u32[]{:S(2)}, u32[]{:S(2)}) collective-permute-start(f32[64,8,128]{2,1,0:T(8,128)S(1)} %bitcast.41), channel_id=1, source_target_pairs={{0,16},{1,17},{16,32},{17,33},{32,48},{33,49},{48,2},{49,3},{2,18}... | collective-permute-start | bytes 786440 | tf_op jit(solution)/shard_map/ppermute | solution.py:31
  21.5 3.0 %collective-permute-start.3 = (f32[64,8,128]{2,1,0:T(8,128)S(1)}, f32[64,8,128]{2,1,0:T(8,128)S(1)}, u32[]{:S(2)}, u32[]{:S(2)}) collective-permute-start(f32[64,8,128]{2,1,0:T(8,128)S(1)} %bitcast.42), channel_id=1, source_target_pairs={{0,34},{1,33},{16,50},{17,49},{32,0},{33,3},{48,16},{49,19},{2,32}... | collective-permute-start | bytes 786440 | tf_op jit(solution)/shard_map/ppermute | solution.py:31
  24.5 1.1 collective-permute-start.2
  25.6 0.9 dynamic-slice_bitcast_fusion
  26.5 5.0 %collective-permute-start.7 = (f32[16,128]{1,0:T(8,128)S(1)}, f32[16,128]{1,0:T(8,128)S(1)}, u32[]{:S(2)}, u32[]{:S(2)}) collective-permute-start(f32[16,128]{1,0:T(8,128)S(1)} %bitcast.47), channel_id=1, source_target_pairs={{0,2},{2,0},{1,3},{3,1},{4,6},{6,4},{5,7},{7,5},{8,10},{10,8},{9,1... | collective-permute-start | bytes 24584 | tf_op jit(solution)/shard_map/ppermute | solution.py:21
  31.6 0.0 copy-done.8
  31.6 6.9 %collective-permute-done.7 = f32[16,128]{1,0:T(8,128)S(1)} collective-permute-done((f32[16,128]{1,0:T(8,128)S(1)}, f32[16,128]{1,0:T(8,128)S(1)}, u32[]{:S(2)}, u32[]{:S(2)}) %collective-permute-start.7) | collective-permute-done | bytes 8224 | tf_op jit(solution)/shard_map/ppermute | solution.py:21
  38.5 0.0 collective-permute-done.4
  38.5 0.1 collective-permute-done.3
  38.6 0.0 collective-permute-done.2
  38.6 0.1 pad_maximum_fusion.table_ref
  38.6 1.5 shard_map.94
  40.2 1.3 copy-done
  41.5 5.4 %all-to-all-start.1 = ((f32[32,15,8,128]{3,2,1,0:T(8,128)}), f32[32,15,8,128]{3,2,1,0:T(8,128)S(1)}, u32[]{:S(2)}, u32[]{:S(2)}) async-start(f32[32,15,8,128]{3,2,1,0:T(8,128)} %copy-done), calls=%async_computation.1 | async-start | bytes 3932160 | tf_op jit(solution)/shard_map/all_to_all | solution.py:35
  46.9 0.4 collective-permute-start
  47.3 3.8 %collective-permute-start.5 = (f32[4,128,128]{2,1,0:T(8,128)}, f32[4,128,128]{2,1,0:T(8,128)S(1)}, u32[]{:S(2)}, u32[]{:S(2)}) collective-permute-start(f32[4,128,128]{2,1,0:T(8,128)} %get-tuple-element.18), channel_id=1, source_target_pairs={{0,2},{2,0},{1,3},{3,1},{4,6},{6,4},{5,7},{7,5},{8,10},{10,8},{9,1... | collective-permute-start | bytes 786440 | tf_op jit(solution)/shard_map/ppermute | solution.py:200
  51.1 2.0 %collective-permute-start.6 = (f32[4,128,128]{2,1,0:T(8,128)}, f32[4,128,128]{2,1,0:T(8,128)S(1)}, u32[]{:S(2)}, u32[]{:S(2)}) collective-permute-start(f32[4,128,128]{2,1,0:T(8,128)} %get-tuple-element.19), channel_id=1, source_target_pairs={{0,3},{3,0},{1,2},{2,1},{4,7},{7,4},{5,6},{6,5},{8,11},{11,8},{9,1... | collective-permute-start | bytes 786440 | tf_op jit(solution)/shard_map/ppermute | solution.py:200
  53.0 0.9 constant_dynamic-slice_fusion.2.refs_4_
  53.9 0.0 collective-permute-done.refs_1_
  54.0 9.7 %collective-permute-done.5.refs_2_ = f32[4,128,128]{2,1,0:T(8,128)S(1)} collective-permute-done((f32[4,128,128]{2,1,0:T(8,128)}, f32[4,128,128]{2,1,0:T(8,128)S(1)}, u32[]{:S(2)}, u32[]{:S(2)}) %collective-permute-start.5) | collective-permute-done | bytes 262176 | tf_op jit(solution)/shard_map/ppermute | solution.py:200
  63.6 11.3 %collective-permute-done.6.refs_3_ = f32[4,128,128]{2,1,0:T(8,128)S(1)} collective-permute-done((f32[4,128,128]{2,1,0:T(8,128)}, f32[4,128,128]{2,1,0:T(8,128)S(1)}, u32[]{:S(2)}, u32[]{:S(2)}) %collective-permute-start.6) | collective-permute-done | bytes 262176 | tf_op jit(solution)/shard_map/ppermute | solution.py:200
  75.0 0.0 all-to-all-done.1
  75.0 2.8 %shard_map.95 = (f32[128,256]{1,0:T(8,128)}, f32[16,2,17,8,128]{4,3,2,1,0:T(8,128)S(1)}, f32[128,256]{1,0:T(8,128)S(1)}, f32[8,128]{1,0:T(8,128)S(1)}) custom-call(f32[4,128,128]{2,1,0:T(8,128)S(1)} %get-tuple-element.35.refs_0_, f32[4,128,128]{2,1,0:T(8,128)S(1)} %collective-permute-done.refs_1_, f32[4,128,128]{2,1,0:T(8,128)S(1)} %collective-permute-done.5.refs_2_, ...), custom_call_target="tpu_custom_call" | custom-call | flops 956301312 | bytes 6291456 | tf_op jit(solution)/shard_map/pallas_call | solution.py:250
  77.7 0.0 copy-start.3
  77.8 0.6 copy-done.3
  78.4 37.4 %all_to_all.21 = f32[32,17,8,128]{3,2,1,0:T(8,128)S(1)} all-to-all(f32[32,17,8,128]{3,2,1,0:T(8,128)S(1)} %bitcast.38), channel_id=1, replica_groups=mesh['x'=4,'zl'=4,'y'=4,'zh'=2,'c'=2] {'x','y','c'}, dimensions={0} | all-to-all | bytes 4456448 | tf_op jit(solution)/shard_map/all_to_all | solution.py:35
  115.8 2.3 %shard_map.96 = f32[4,67,8,128]{3,2,1,0:T(8,128)S(1)} custom-call(s32[16,128]{1,0:T(8,128)S(1)} %convert_element_type.12.near_ref, s32[16,128]{1,0:T(8,128)S(1)} %copy-done.6, f32[16,2,17,8,128]{4,3,2,1,0:T(8,128)S(1)} %bitcast.36, f32[8,128]{1,0:T(8,128)S(1)} %get-tuple-element.25.bias_ref), custom_call_target="tpu_custom_call" | custom-call | bytes 4194304 | tf_op jit(solution)/shard_map/pallas_call | solution.py:272
  118.1 0.1 slice_bitcast_fusion.2
  118.1 3.1 %collective-permute-start.8 = (f32[67,8,128]{2,1,0:T(8,128)S(1)}, f32[67,8,128]{2,1,0:T(8,128)S(1)}, u32[]{:S(2)}, u32[]{:S(2)}) collective-permute-start(f32[67,8,128]{2,1,0:T(8,128)S(1)} %get-tuple-element.30), channel_id=1, source_target_pairs={{0,16},{1,17},{16,32},{17,33},{32,48},{33,49},{48,2},{49,3},{2,18}... | collective-permute-start | bytes 823304 | tf_op jit(solution)/shard_map/ppermute | solution.py:31
  121.2 4.6 %collective-permute-start.10 = (f32[67,8,128]{2,1,0:T(8,128)S(1)}, f32[67,8,128]{2,1,0:T(8,128)S(1)}, u32[]{:S(2)}, u32[]{:S(2)}) collective-permute-start(f32[67,8,128]{2,1,0:T(8,128)S(1)} %get-tuple-element.31), channel_id=1, source_target_pairs={{0,32},{1,35},{16,48},{17,51},{32,2},{33,1},{48,18},{49,17},{2,34}... | collective-permute-start | bytes 823304 | tf_op jit(solution)/shard_map/ppermute | solution.py:31
  125.8 0.0 collective-permute-start.9
  125.8 5.4 %collective-permute-done.8 = f32[67,8,128]{2,1,0:T(8,128)S(1)} collective-permute-done((f32[67,8,128]{2,1,0:T(8,128)S(1)}, f32[67,8,128]{2,1,0:T(8,128)S(1)}, u32[]{:S(2)}, u32[]{:S(2)}) %collective-permute-start.8) | collective-permute-done | bytes 274464 | tf_op jit(solution)/shard_map/ppermute | solution.py:31
  131.3 3.7 %collective-permute-done.10 = f32[67,8,128]{2,1,0:T(8,128)S(1)} collective-permute-done((f32[67,8,128]{2,1,0:T(8,128)S(1)}, f32[67,8,128]{2,1,0:T(8,128)S(1)}, u32[]{:S(2)}, u32[]{:S(2)}) %collective-permute-start.10) | collective-permute-done | bytes 274464 | tf_op jit(solution)/shard_map/ppermute | solution.py:31
  134.9 3.3 %collective-permute-done.9 = f32[67,8,128]{2,1,0:T(8,128)S(1)} collective-permute-done((f32[67,8,128]{2,1,0:T(8,128)S(1)}, f32[67,8,128]{2,1,0:T(8,128)S(1)}, u32[]{:S(2)}, u32[]{:S(2)}) %collective-permute-start.9) | collective-permute-done | bytes 274464 | tf_op jit(solution)/shard_map/ppermute | solution.py:31
  138.3 0.1 fusion.2
  138.4 0.0 copy-start.4
  138.5 1.9 %collective-permute-start.11 = (f32[35,8,128]{2,1,0:T(8,128)S(1)}, f32[35,8,128]{2,1,0:T(8,128)S(1)}, u32[]{:S(2)}, u32[]{:S(2)}) collective-permute-start(f32[35,8,128]{2,1,0:T(8,128)S(1)} %pad_maximum_fusion.3), channel_id=1, source_target_pairs={{0,2},{2,0},{1,3},{3,1},{4,6},{6,4},{5,7},{7,5},{8,10},{10,8},{9,1... | collective-permute-start | bytes 430088 | tf_op jit(solution)/shard_map/ppermute | solution.py:21
  140.3 10.4 %collective-permute-done.11 = f32[35,8,128]{2,1,0:T(8,128)S(1)} collective-permute-done((f32[35,8,128]{2,1,0:T(8,128)S(1)}, f32[35,8,128]{2,1,0:T(8,128)S(1)}, u32[]{:S(2)}, u32[]{:S(2)}) %collective-permute-start.11) | collective-permute-done | bytes 143392 | tf_op jit(solution)/shard_map/ppermute | solution.py:21
  150.9 0.1 pad_maximum_fusion.1
  150.9 15.6 %all_to_all.22 = f32[32,4,8,128]{3,2,1,0:T(8,128)S(1)} all-to-all(f32[32,4,8,128]{3,2,1,0:T(8,128)S(1)} %pad_maximum_fusion.1), channel_id=1, replica_groups=mesh['x'=4,'zl'=4,'y'=4,'zh'=2,'c'=2] {'x','y','c'}, dimensions={0} | all-to-all | bytes 1048576 | tf_op jit(solution)/shard_map/all_to_all | solution.py:35
  166.5 0.8 shard_map.97
  (33 shorter events, 0.3 us)
Async XLA Ops:
  1.6 4.1 %collective-permute-start.1 = (f32[1,16]{1,0:T(1,128)S(1)}, f32[1,16]{1,0:T(1,128)S(1)}, u32[]{:S(2)}, u32[]{:S(2)}) collective-permute-start(f32[1,16]{1,0:T(1,128)S(1)} %concatenate.39), channel_id=1, source_target_pairs={{0,1},{1,0},{2,3},{3,2},{4,5},{5,4},{6,7},{7,6},{8,9},{9,8},{10,11... | collective-permute-start | bytes 200 | tf_op jit(solution)/shard_map/ppermute | solution.py:21
  5.7 1.0 copy-start.1
  6.8 18.9 %copy-start.7 = (f32[4,4,128,128]{3,2,1,0:T(8,128)S(1)}, f32[4,4,128,128]{3,2,1,0:T(8,128)}, u32[]{:S(2)}) copy-start(f32[4,4,128,128]{3,2,1,0:T(8,128)} %param.7) | copy-start | bytes 3145732
  6.8 24.8 %copy-start.9 = (f32[256]{0:T(256)S(1)}, f32[256]{0:T(256)}, u32[]{:S(2)}) copy-start(f32[256]{0:T(256)} %param.10) | copy-start | bytes 3076
  6.8 24.8 %copy-start.8 = (f32[256,256]{1,0:T(8,128)S(1)}, f32[256,256]{1,0:T(8,128)}, u32[]{:S(2)}) copy-start(f32[256,256]{1,0:T(8,128)} %param.9) | copy-start | bytes 786436
  19.8 18.7 %collective-permute-start.4 = (f32[64,8,128]{2,1,0:T(8,128)S(1)}, f32[64,8,128]{2,1,0:T(8,128)S(1)}, u32[]{:S(2)}, u32[]{:S(2)}) collective-permute-start(f32[64,8,128]{2,1,0:T(8,128)S(1)} %bitcast.41), channel_id=1, source_target_pairs={{0,16},{1,17},{16,32},{17,33},{32,48},{33,49},{48,2},{49,3},{2,18}... | collective-permute-start | bytes 786440 | tf_op jit(solution)/shard_map/ppermute | solution.py:31
  21.5 17.0 %collective-permute-start.3 = (f32[64,8,128]{2,1,0:T(8,128)S(1)}, f32[64,8,128]{2,1,0:T(8,128)S(1)}, u32[]{:S(2)}, u32[]{:S(2)}) collective-permute-start(f32[64,8,128]{2,1,0:T(8,128)S(1)} %bitcast.42), channel_id=1, source_target_pairs={{0,34},{1,33},{16,50},{17,49},{32,0},{33,3},{48,16},{49,19},{2,32}... | collective-permute-start | bytes 786440 | tf_op jit(solution)/shard_map/ppermute | solution.py:31
  24.5 14.1 %collective-permute-start.2 = (f32[64,8,128]{2,1,0:T(8,128)S(1)}, f32[64,8,128]{2,1,0:T(8,128)S(1)}, u32[]{:S(2)}, u32[]{:S(2)}) collective-permute-start(f32[64,8,128]{2,1,0:T(8,128)S(1)} %bitcast.43), channel_id=1, source_target_pairs={{0,50},{1,51},{16,0},{17,1},{32,16},{33,17},{48,32},{49,33},{2,48}... | collective-permute-start | bytes 786440 | tf_op jit(solution)/shard_map/ppermute | solution.py:31
  26.5 11.9 %collective-permute-start.7 = (f32[16,128]{1,0:T(8,128)S(1)}, f32[16,128]{1,0:T(8,128)S(1)}, u32[]{:S(2)}, u32[]{:S(2)}) collective-permute-start(f32[16,128]{1,0:T(8,128)S(1)} %bitcast.47), channel_id=1, source_target_pairs={{0,2},{2,0},{1,3},{3,1},{4,6},{6,4},{5,7},{7,5},{8,10},{10,8},{9,1... | collective-permute-start | bytes 24584 | tf_op jit(solution)/shard_map/ppermute | solution.py:21
  38.5 1.7 %copy-start.5 = (s32[16,128]{1,0:T(8,128)}, s32[16,128]{1,0:T(8,128)S(1)}, u32[]{:S(2)}) copy-start(s32[16,128]{1,0:T(8,128)S(1)} %convert_element_type.13.far_ref) | copy-start | bytes 24580
  40.2 1.3 copy-start
  41.5 33.5 %copy-start.2 = (f32[128,256]{1,0:T(8,128)S(1)}, f32[128,256]{1,0:T(8,128)}, u32[]{:S(2)}) copy-start(f32[128,256]{1,0:T(8,128)} %refs_6_.1) | copy-start | bytes 393220
  41.5 33.5 %all-to-all-start.1 = ((f32[32,15,8,128]{3,2,1,0:T(8,128)}), f32[32,15,8,128]{3,2,1,0:T(8,128)S(1)}, u32[]{:S(2)}, u32[]{:S(2)}) async-start(f32[32,15,8,128]{3,2,1,0:T(8,128)} %copy-done), calls=%async_computation.1 | async-start | bytes 3932160 | tf_op jit(solution)/shard_map/all_to_all | solution.py:35
  46.9 7.1 %collective-permute-start = (f32[4,128,128]{2,1,0:T(8,128)}, f32[4,128,128]{2,1,0:T(8,128)S(1)}, u32[]{:S(2)}, u32[]{:S(2)}) collective-permute-start(f32[4,128,128]{2,1,0:T(8,128)} %get-tuple-element.34), channel_id=1, source_target_pairs={{0,1},{1,0},{2,3},{3,2},{4,5},{5,4},{6,7},{7,6},{8,9},{9,8},{10,11... | collective-permute-start | bytes 786440 | tf_op jit(solution)/shard_map/ppermute | solution.py:200
  47.3 16.4 %collective-permute-start.5 = (f32[4,128,128]{2,1,0:T(8,128)}, f32[4,128,128]{2,1,0:T(8,128)S(1)}, u32[]{:S(2)}, u32[]{:S(2)}) collective-permute-start(f32[4,128,128]{2,1,0:T(8,128)} %get-tuple-element.18), channel_id=1, source_target_pairs={{0,2},{2,0},{1,3},{3,1},{4,6},{6,4},{5,7},{7,5},{8,10},{10,8},{9,1... | collective-permute-start | bytes 786440 | tf_op jit(solution)/shard_map/ppermute | solution.py:200
  51.1 23.9 %collective-permute-start.6 = (f32[4,128,128]{2,1,0:T(8,128)}, f32[4,128,128]{2,1,0:T(8,128)S(1)}, u32[]{:S(2)}, u32[]{:S(2)}) collective-permute-start(f32[4,128,128]{2,1,0:T(8,128)} %get-tuple-element.19), channel_id=1, source_target_pairs={{0,3},{3,0},{1,2},{2,1},{4,7},{7,4},{5,6},{6,5},{8,11},{11,8},{9,1... | collective-permute-start | bytes 786440 | tf_op jit(solution)/shard_map/ppermute | solution.py:200
  77.7 0.7 copy-start.3
  78.4 37.4 %copy-start.6 = (s32[16,128]{1,0:T(8,128)S(1)}, s32[16,128]{1,0:T(8,128)}, u32[]{:S(2)}) copy-start(s32[16,128]{1,0:T(8,128)} %copy-done.5) | copy-start | bytes 24580
  118.1 13.1 %collective-permute-start.8 = (f32[67,8,128]{2,1,0:T(8,128)S(1)}, f32[67,8,128]{2,1,0:T(8,128)S(1)}, u32[]{:S(2)}, u32[]{:S(2)}) collective-permute-start(f32[67,8,128]{2,1,0:T(8,128)S(1)} %get-tuple-element.30), channel_id=1, source_target_pairs={{0,16},{1,17},{16,32},{17,33},{32,48},{33,49},{48,2},{49,3},{2,18}... | collective-permute-start | bytes 823304 | tf_op jit(solution)/shard_map/ppermute | solution.py:31
  121.2 13.7 %collective-permute-start.10 = (f32[67,8,128]{2,1,0:T(8,128)S(1)}, f32[67,8,128]{2,1,0:T(8,128)S(1)}, u32[]{:S(2)}, u32[]{:S(2)}) collective-permute-start(f32[67,8,128]{2,1,0:T(8,128)S(1)} %get-tuple-element.31), channel_id=1, source_target_pairs={{0,32},{1,35},{16,48},{17,51},{32,2},{33,1},{48,18},{49,17},{2,34}... | collective-permute-start | bytes 823304 | tf_op jit(solution)/shard_map/ppermute | solution.py:31
  125.8 12.4 %collective-permute-start.9 = (f32[67,8,128]{2,1,0:T(8,128)S(1)}, f32[67,8,128]{2,1,0:T(8,128)S(1)}, u32[]{:S(2)}, u32[]{:S(2)}) collective-permute-start(f32[67,8,128]{2,1,0:T(8,128)S(1)} %get-tuple-element.32), channel_id=1, source_target_pairs={{0,50},{1,51},{16,0},{17,1},{32,16},{33,17},{48,32},{49,33},{2,48}... | collective-permute-start | bytes 823304 | tf_op jit(solution)/shard_map/ppermute | solution.py:31
  138.4 28.1 %copy-start.4 = (f32[128,256]{1,0:T(8,128)S(1)}, f32[128,256]{1,0:T(8,128)}, u32[]{:S(2)}) copy-start(f32[128,256]{1,0:T(8,128)} %copy-done.3) | copy-start | bytes 393220
  138.5 12.3 %collective-permute-start.11 = (f32[35,8,128]{2,1,0:T(8,128)S(1)}, f32[35,8,128]{2,1,0:T(8,128)S(1)}, u32[]{:S(2)}, u32[]{:S(2)}) collective-permute-start(f32[35,8,128]{2,1,0:T(8,128)S(1)} %pad_maximum_fusion.3), channel_id=1, source_target_pairs={{0,2},{2,0},{1,3},{3,1},{4,6},{6,4},{5,7},{7,5},{8,10},{10,8},{9,1... | collective-permute-start | bytes 430088 | tf_op jit(solution)/shard_map/ppermute | solution.py:21

commit v7 on v6

--- a/solution.py
+++ b/solution.py
@@ -141,6 +141,7 @@
     scale,
     own_ref,
     beside_ref,
+    early_ref,
     across_ref,
     opposite_ref,
     rows_ref,
@@ -154,10 +155,13 @@
 ):
     core, half = lax.axis_index("c"), lax.axis_index("zh")
     tiles = []
-    for near_ref, far_ref in ((own_ref, beside_ref), (across_ref, opposite_ref)):
+    across = [early_ref[0]] + [across_ref[k] for k in range(3)]
+    near = [own_ref[k] for k in range(4)] + across
+    far = [beside_ref[k] for k in range(4)] + [opposite_ref[k] for k in range(4)]
+    for source in range(2):
         for c in range(2):
-            for k in range(4):
-                tiles.append(jnp.where(core == c, near_ref[k], far_ref[k]))
+            for k in range(4 * source, 4 * source + 4):
+                tiles.append(jnp.where(core == c, near[k], far[k]))
     alone = jnp.where(half == 0, tiles[0], tiles[8])
     for j in (0, 8):
         tiles[j] = jnp.where(8 * half == j, tiles[15], tiles[j])
@@ -234,6 +238,9 @@
     )
     leaving = (tiles_for(2 * (1 - half) + core), tiles_for(2 * (1 - half) + 1 - core))
     affine = jnp.concatenate([weight, jnp.broadcast_to(layer_bias, (8, 256))], axis=0)
+    over = [(0, 2), (2, 0), (1, 3), (3, 1)]
+    early = swapped(leaving[0][:1], over)
+    leaving = (leaving[0][1:], leaving[1])
     table, leaving, affine = lax.optimization_barrier((table, leaving, affine))
     across = swapped(leaving[0], [(0, 2), (2, 0), (1, 3), (3, 1)])
     opposite = swapped(leaving[1], [(0, 3), (3, 0), (1, 2), (2, 1)])
@@ -243,6 +250,7 @@
         [smem(), smem(), vmem()],
         moved=3 << 20,
     )(*index, table)
+    sent, early = lax.optimization_barrier((sent, early))
     got = exchange(sent, GROUP).reshape(16, 2, 15, 8, 128)
     def middle(*refs):
         middle_kernel(scale, *refs)
@@ -255,12 +263,13 @@
             jax.ShapeDtypeStruct((128, 256), F32),
             jax.ShapeDtypeStruct((8, 128), F32),
         ),
-        [vmem()] * 8,
+        [vmem()] * 9,
         flops=318767104 * 3,
         moved=6 << 20,
     )(
         tiles_for(mine),
         beside,
+        early,
         across,
         opposite,
         rows,

time: 168 us -> 164 us (0.976)
  blocking collectives: 65.9 us -> 49.5 us
  starting transfers between devices: 35.2 us -> 48.9 us
  waiting for transfers between devices: 51.7 us -> 45.6 us
  local copies, waits for them, and re-layouts: 5.87 us -> 8.82 us
    all_to_all x3 -> x2, blocking collectives: 65.9 us -> 49.5 us  [exchange(): return lax.all_to_all(value, axes, 0, 0, tiled=True)]
    ppermute x3 -> x4, waiting for transfers between devices: 21 us -> 12.4 us  [swapped(): return lax.ppermute(tiles, ('zh', 'c'), pairs)]
    all_to_all x1 -> x2, waiting for transfers between devices: 0.01 us -> 7.93 us  [exchange(): return lax.all_to_all(value, axes, 0, 0, tiled=True)]
    ppermute x3 -> x4, starting transfers between devices: 6.14 us -> 12.8 us  [swapped(): return lax.ppermute(tiles, ('zh', 'c'), pairs)]
    all_to_all x1 -> x2, starting transfers between devices: 5.42 us -> 11.1 us  [exchange(): return lax.all_to_all(value, axes, 0, 0, tiled=True)]
    ppermute x3, waiting for transfers between devices: 18.1 us -> 13.5 us  [shift(): lax.ppermute(value, axis, [(s, (s + steps) % count) for s in range(count)])]
  transfers between devices with their start and end apart: 13 -> 15, of which waited for: 9 -> 10; matrix products, arithmetic and copies ran while one was open for 1% -> 2% of each run, Pallas kernels for 0% -> 1%
where the time goes in v7:
time: 164 us; the launch traced here: 162 us
  blocking collectives  49.5 us (30%)
  starting transfers between devices  48.9 us (30%)
  waiting for transfers between devices  45.6 us (28%)
  local copies, waits for them, and re-layouts  8.82 us (5%)
  Pallas kernels  8.11 us (5%)
    all_to_all x2, blocking collectives, exchange(): return lax.all_to_all(value, axes, 0, 0, tiled=True)  49.5 us
    ppermute x6, starting transfers between devices, ring(): return lax.ppermute(value, ('zl', 'zh', 'c'), pairs)  14.3 us
    ppermute x3, waiting for transfers between devices, shift(): lax.ppermute(value, axis, [(s, (s + steps) % count) for s in range(count)])  13.5 us
    ppermute x4, starting transfers between devices, swapped(): return lax.ppermute(tiles, ('zh', 'c'), pairs)  12.8 us
    ppermute x4, waiting for transfers between devices, swapped(): return lax.ppermute(tiles, ('zh', 'c'), pairs)  12.4 us
    ppermute x6, waiting for transfers between devices, ring(): return lax.ppermute(value, ('zl', 'zh', 'c'), pairs)  11.7 us
    all_to_all x2, starting transfers between devices, exchange(): return lax.all_to_all(value, axes, 0, 0, tiled=True)  11.1 us
    ppermute x3, starting transfers between devices, shift(): lax.ppermute(value, axis, [(s, (s + steps) % count) for s in range(count)])  10.7 us
  transfers between devices with their start and end apart: 15, of which 10 were waited for; matrix products, arithmetic and copies ran while one was open for 2% of the time, Pallas kernels for 1%

profile of v7, /device:TPU:1, one launch (start us, length us, event | category | flops | bytes accessed | tf_op | source)
XLA Modules:
  0.0 162.2 jit_solution(9570889818570623797)
XLA Ops:
  0.6 0.8 reshape.102
  1.5 0.1 concatenate.39
  1.6 3.3 %collective-permute-start.1 = (f32[1,16]{1,0:T(1,128)S(1)}, f32[1,16]{1,0:T(1,128)S(1)}, u32[]{:S(2)}, u32[]{:S(2)}) collective-permute-start(f32[1,16]{1,0:T(1,128)S(1)} %concatenate.39), channel_id=1, source_target_pairs={{0,1},{1,0},{2,3},{3,2},{4,5},{5,4},{6,7},{7,6},{8,9},{9,8},{10,11... | collective-permute-start | bytes 200 | tf_op jit(solution)/shard_map/ppermute | solution.py:21
  4.9 0.8 collective-permute-done.1
  5.7 0.1 broadcast_select_fusion
  5.8 1.0 copy-done.1
  6.8 0.7 shard_map.93
  7.6 5.0 %all-to-all-start = ((f32[16,5,8,128]{3,2,1,0:T(8,128)}), f32[16,5,8,128]{3,2,1,0:T(8,128)S(1)}, u32[]{:S(2)}, u32[]{:S(2)}) async-start(f32[16,5,8,128]{3,2,1,0:T(8,128)} %shard_map.93), calls=%async_computation | async-start | bytes 655360 | tf_op jit(solution)/shard_map/all_to_all | solution.py:35
  12.6 0.8 dynamic-slice_bitcast_fusion.4
  13.4 6.9 %collective-permute-start.6 = (f32[1,128,128]{2,1,0:T(8,128)S(1)}, f32[1,128,128]{2,1,0:T(8,128)S(1)}, u32[]{:S(2)}, u32[]{:S(2)}) collective-permute-start(f32[1,128,128]{2,1,0:T(8,128)S(1)} %dynamic-slice_bitcast_fusion.4), channel_id=1, source_target_pairs={{0,2},{2,0},{1,3},{3,1},{4,6},{6,4},{5,7},{7,5},{8,10},{10,8},{9,1... | collective-permute-start | bytes 196616 | tf_op jit(solution)/shard_map/ppermute | solution.py:204
  20.3 0.2 all-to-all-done
  20.6 1.7 %collective-permute-start.5 = (f32[64,8,128]{2,1,0:T(8,128)S(1)}, f32[64,8,128]{2,1,0:T(8,128)S(1)}, u32[]{:S(2)}, u32[]{:S(2)}) collective-permute-start(f32[64,8,128]{2,1,0:T(8,128)S(1)} %bitcast.43), channel_id=1, source_target_pairs={{0,16},{1,17},{16,32},{17,33},{32,48},{33,49},{48,2},{49,3},{2,18}... | collective-permute-start | bytes 786440 | tf_op jit(solution)/shard_map/ppermute | solution.py:31
  22.3 3.0 %collective-permute-start.4 = (f32[64,8,128]{2,1,0:T(8,128)S(1)}, f32[64,8,128]{2,1,0:T(8,128)S(1)}, u32[]{:S(2)}, u32[]{:S(2)}) collective-permute-start(f32[64,8,128]{2,1,0:T(8,128)S(1)} %bitcast.44), channel_id=1, source_target_pairs={{0,34},{1,33},{16,50},{17,49},{32,0},{33,3},{48,16},{49,19},{2,32}... | collective-permute-start | bytes 786440 | tf_op jit(solution)/shard_map/ppermute | solution.py:31
  25.3 1.1 collective-permute-start.3
  26.5 0.9 dynamic-slice_bitcast_fusion
  27.4 5.0 %collective-permute-start.2 = (f32[16,128]{1,0:T(8,128)S(1)}, f32[16,128]{1,0:T(8,128)S(1)}, u32[]{:S(2)}, u32[]{:S(2)}) collective-permute-start(f32[16,128]{1,0:T(8,128)S(1)} %bitcast.49), channel_id=1, source_target_pairs={{0,2},{2,0},{1,3},{3,1},{4,6},{6,4},{5,7},{7,5},{8,10},{10,8},{9,1... | collective-permute-start | bytes 24584 | tf_op jit(solution)/shard_map/ppermute | solution.py:21
  32.4 0.7 dynamic-slice_bitcast_fusion.3
  33.1 5.9 %collective-permute-done.2 = f32[16,128]{1,0:T(8,128)S(1)} collective-permute-done((f32[16,128]{1,0:T(8,128)S(1)}, f32[16,128]{1,0:T(8,128)S(1)}, u32[]{:S(2)}, u32[]{:S(2)}) %collective-permute-start.2) | collective-permute-done | bytes 8224 | tf_op jit(solution)/shard_map/ppermute | solution.py:21
  39.0 0.4 collective-permute-done.4
  39.4 0.1 pad_maximum_fusion.table_ref
  39.4 1.5 shard_map.94
  41.0 1.3 copy-done
  42.2 0.6 copy-done.5
  42.9 6.1 %all-to-all-start.1 = ((f32[32,15,8,128]{3,2,1,0:T(8,128)}), f32[32,15,8,128]{3,2,1,0:T(8,128)S(1)}, u32[]{:S(2)}, u32[]{:S(2)}) async-start(f32[32,15,8,128]{3,2,1,0:T(8,128)} %copy-done), calls=%async_computation.1 | async-start | bytes 3932160 | tf_op jit(solution)/shard_map/all_to_all | solution.py:35
  49.0 0.3 collective-permute-start
  49.3 3.1 %collective-permute-start.8 = (f32[4,128,128]{2,1,0:T(8,128)}, f32[4,128,128]{2,1,0:T(8,128)S(1)}, u32[]{:S(2)}, u32[]{:S(2)}) collective-permute-start(f32[4,128,128]{2,1,0:T(8,128)} %get-tuple-element.24), channel_id=1, source_target_pairs={{0,3},{3,0},{1,2},{2,1},{4,7},{7,4},{5,6},{6,5},{8,11},{11,8},{9,1... | collective-permute-start | bytes 786440 | tf_op jit(solution)/shard_map/ppermute | solution.py:204
  52.4 2.4 %collective-permute-start.7 = (f32[3,128,128]{2,1,0:T(8,128)}, f32[3,128,128]{2,1,0:T(8,128)S(1)}, u32[]{:S(2)}, u32[]{:S(2)}) collective-permute-start(f32[3,128,128]{2,1,0:T(8,128)} %dynamic-slice_bitcast_fusion.3), channel_id=1, source_target_pairs={{0,2},{2,0},{1,3},{3,1},{4,6},{6,4},{5,7},{7,5},{8,10},{10,8},{9,1... | collective-permute-start | bytes 589832 | tf_op jit(solution)/shard_map/ppermute | solution.py:204
  54.8 0.9 constant_dynamic-slice_fusion.2.refs_5_
  55.8 12.4 %collective-permute-done.7.refs_3_ = f32[3,128,128]{2,1,0:T(8,128)S(1)} collective-permute-done((f32[3,128,128]{2,1,0:T(8,128)}, f32[3,128,128]{2,1,0:T(8,128)S(1)}, u32[]{:S(2)}, u32[]{:S(2)}) %collective-permute-start.7) | collective-permute-done | bytes 196640 | tf_op jit(solution)/shard_map/ppermute | solution.py:204
  68.2 7.7 %all-to-all-done.1 = f32[32,15,8,128]{3,2,1,0:T(8,128)S(1)} async-done(((f32[32,15,8,128]{3,2,1,0:T(8,128)}), f32[32,15,8,128]{3,2,1,0:T(8,128)S(1)}, u32[]{:S(2)}, u32[]{:S(2)}) %all-to-all-start.1) | async-done | bytes 1966112 | tf_op jit(solution)/shard_map/all_to_all | solution.py:35
  75.9 0.8 copy-done.6
  76.7 2.8 %shard_map.95 = (f32[128,256]{1,0:T(8,128)}, f32[16,2,17,8,128]{4,3,2,1,0:T(8,128)S(1)}, f32[128,256]{1,0:T(8,128)S(1)}, f32[8,128]{1,0:T(8,128)S(1)}) custom-call(f32[4,128,128]{2,1,0:T(8,128)S(1)} %get-tuple-element.39.refs_0_, f32[4,128,128]{2,1,0:T(8,128)S(1)} %collective-permute-done.refs_1_, f32[1,128,128]{2,1,0:T(8,128)S(1)} %copy-done.6, ...), custom_call_target="tpu_custom_call" | custom-call | flops 956301312 | bytes 6291456 | tf_op jit(solution)/shard_map/pallas_call | solution.py:258
  79.5 0.0 copy-start.3
  79.5 0.6 copy-done.3
  80.2 33.8 %all_to_all.20 = f32[32,17,8,128]{3,2,1,0:T(8,128)S(1)} all-to-all(f32[32,17,8,128]{3,2,1,0:T(8,128)S(1)} %bitcast.40), channel_id=1, replica_groups=mesh['x'=4,'zl'=4,'y'=4,'zh'=2,'c'=2] {'x','y','c'}, dimensions={0} | all-to-all | bytes 4456448 | tf_op jit(solution)/shard_map/all_to_all | solution.py:35
  114.0 2.3 %shard_map.96 = f32[4,67,8,128]{3,2,1,0:T(8,128)S(1)} custom-call(s32[16,128]{1,0:T(8,128)S(1)} %convert_element_type.12.near_ref, s32[16,128]{1,0:T(8,128)S(1)} %convert_element_type.13.far_ref, f32[16,2,17,8,128]{4,3,2,1,0:T(8,128)S(1)} %bitcast.38, f32[8,128]{1,0:T(8,128)S(1)} %get-tuple-element.29.bias_ref), custom_call_target="tpu_custom_call" | custom-call | bytes 4194304 | tf_op jit(solution)/shard_map/pallas_call | solution.py:281
  116.3 0.1 slice_bitcast_fusion.2
  116.3 6.9 %collective-permute-start.9 = (f32[67,8,128]{2,1,0:T(8,128)S(1)}, f32[67,8,128]{2,1,0:T(8,128)S(1)}, u32[]{:S(2)}, u32[]{:S(2)}) collective-permute-start(f32[67,8,128]{2,1,0:T(8,128)S(1)} %get-tuple-element.34), channel_id=1, source_target_pairs={{0,16},{1,17},{16,32},{17,33},{32,48},{33,49},{48,2},{49,3},{2,18}... | collective-permute-start | bytes 823304 | tf_op jit(solution)/shard_map/ppermute | solution.py:31
  123.2 1.5 collective-permute-start.10
  124.8 5.3 %collective-permute-done.9 = f32[67,8,128]{2,1,0:T(8,128)S(1)} collective-permute-done((f32[67,8,128]{2,1,0:T(8,128)S(1)}, f32[67,8,128]{2,1,0:T(8,128)S(1)}, u32[]{:S(2)}, u32[]{:S(2)}) %collective-permute-start.9) | collective-permute-done | bytes 274464 | tf_op jit(solution)/shard_map/ppermute | solution.py:31
  130.1 5.1 %collective-permute-done.11 = f32[67,8,128]{2,1,0:T(8,128)S(1)} collective-permute-done((f32[67,8,128]{2,1,0:T(8,128)S(1)}, f32[67,8,128]{2,1,0:T(8,128)S(1)}, u32[]{:S(2)}, u32[]{:S(2)}) %collective-permute-start.11) | collective-permute-done | bytes 274464 | tf_op jit(solution)/shard_map/ppermute | solution.py:31
  135.2 0.9 collective-permute-done.10
  136.1 0.1 fusion.2
  136.3 2.5 %collective-permute-start.12 = (f32[35,8,128]{2,1,0:T(8,128)S(1)}, f32[35,8,128]{2,1,0:T(8,128)S(1)}, u32[]{:S(2)}, u32[]{:S(2)}) collective-permute-start(f32[35,8,128]{2,1,0:T(8,128)S(1)} %pad_maximum_fusion.3), channel_id=1, source_target_pairs={{0,2},{2,0},{1,3},{3,1},{4,6},{6,4},{5,7},{7,5},{8,10},{10,8},{9,1... | collective-permute-start | bytes 430088 | tf_op jit(solution)/shard_map/ppermute | solution.py:21
  138.8 6.8 %collective-permute-done.12 = f32[35,8,128]{2,1,0:T(8,128)S(1)} collective-permute-done((f32[35,8,128]{2,1,0:T(8,128)S(1)}, f32[35,8,128]{2,1,0:T(8,128)S(1)}, u32[]{:S(2)}, u32[]{:S(2)}) %collective-permute-start.12) | collective-permute-done | bytes 143392 | tf_op jit(solution)/shard_map/ppermute | solution.py:21
  145.6 0.1 pad_maximum_fusion.1
  145.7 15.7 %all_to_all.21 = f32[32,4,8,128]{3,2,1,0:T(8,128)S(1)} all-to-all(f32[32,4,8,128]{3,2,1,0:T(8,128)S(1)} %pad_maximum_fusion.1), channel_id=1, replica_groups=mesh['x'=4,'zl'=4,'y'=4,'zh'=2,'c'=2] {'x','y','c'}, dimensions={0} | all-to-all | bytes 1048576 | tf_op jit(solution)/shard_map/all_to_all | solution.py:35
  161.4 0.8 shard_map.97
  (38 shorter events, 0.3 us)
Async XLA Ops:
  0.6 25.8 %copy-start.9 = (f32[256]{0:T(256)S(1)}, f32[256]{0:T(256)}, u32[]{:S(2)}) copy-start(f32[256]{0:T(256)} %param.10) | copy-start | bytes 3076
  1.6 4.1 %collective-permute-start.1 = (f32[1,16]{1,0:T(1,128)S(1)}, f32[1,16]{1,0:T(1,128)S(1)}, u32[]{:S(2)}, u32[]{:S(2)}) collective-permute-start(f32[1,16]{1,0:T(1,128)S(1)} %concatenate.39), channel_id=1, source_target_pairs={{0,1},{1,0},{2,3},{3,2},{4,5},{5,4},{6,7},{7,6},{8,9},{9,8},{10,11... | collective-permute-start | bytes 200 | tf_op jit(solution)/shard_map/ppermute | solution.py:21
  5.8 1.0 copy-start.1
  6.8 19.6 %copy-start.8 = (f32[256,256]{1,0:T(8,128)S(1)}, f32[256,256]{1,0:T(8,128)}, u32[]{:S(2)}) copy-start(f32[256,256]{1,0:T(8,128)} %param.9) | copy-start | bytes 786436
  6.8 19.7 %copy-start.7 = (f32[4,4,128,128]{3,2,1,0:T(8,128)S(1)}, f32[4,4,128,128]{3,2,1,0:T(8,128)}, u32[]{:S(2)}) copy-start(f32[4,4,128,128]{3,2,1,0:T(8,128)} %param.7) | copy-start | bytes 3145732
  7.6 13.0 %all-to-all-start = ((f32[16,5,8,128]{3,2,1,0:T(8,128)}), f32[16,5,8,128]{3,2,1,0:T(8,128)S(1)}, u32[]{:S(2)}, u32[]{:S(2)}) async-start(f32[16,5,8,128]{3,2,1,0:T(8,128)} %shard_map.93), calls=%async_computation | async-start | bytes 655360 | tf_op jit(solution)/shard_map/all_to_all | solution.py:35
  13.4 28.8 %collective-permute-start.6 = (f32[1,128,128]{2,1,0:T(8,128)S(1)}, f32[1,128,128]{2,1,0:T(8,128)S(1)}, u32[]{:S(2)}, u32[]{:S(2)}) collective-permute-start(f32[1,128,128]{2,1,0:T(8,128)S(1)} %dynamic-slice_bitcast_fusion.4), channel_id=1, source_target_pairs={{0,2},{2,0},{1,3},{3,1},{4,6},{6,4},{5,7},{7,5},{8,10},{10,8},{9,1... | collective-permute-start | bytes 196616 | tf_op jit(solution)/shard_map/ppermute | solution.py:204
  20.6 18.3 %collective-permute-start.5 = (f32[64,8,128]{2,1,0:T(8,128)S(1)}, f32[64,8,128]{2,1,0:T(8,128)S(1)}, u32[]{:S(2)}, u32[]{:S(2)}) collective-permute-start(f32[64,8,128]{2,1,0:T(8,128)S(1)} %bitcast.43), channel_id=1, source_target_pairs={{0,16},{1,17},{16,32},{17,33},{32,48},{33,49},{48,2},{49,3},{2,18}... | collective-permute-start | bytes 786440 | tf_op jit(solution)/shard_map/ppermute | solution.py:31
  22.3 17.0 %collective-permute-start.4 = (f32[64,8,128]{2,1,0:T(8,128)S(1)}, f32[64,8,128]{2,1,0:T(8,128)S(1)}, u32[]{:S(2)}, u32[]{:S(2)}) collective-permute-start(f32[64,8,128]{2,1,0:T(8,128)S(1)} %bitcast.44), channel_id=1, source_target_pairs={{0,34},{1,33},{16,50},{17,49},{32,0},{33,3},{48,16},{49,19},{2,32}... | collective-permute-start | bytes 786440 | tf_op jit(solution)/shard_map/ppermute | solution.py:31
  25.3 14.0 %collective-permute-start.3 = (f32[64,8,128]{2,1,0:T(8,128)S(1)}, f32[64,8,128]{2,1,0:T(8,128)S(1)}, u32[]{:S(2)}, u32[]{:S(2)}) collective-permute-start(f32[64,8,128]{2,1,0:T(8,128)S(1)} %bitcast.45), channel_id=1, source_target_pairs={{0,50},{1,51},{16,0},{17,1},{32,16},{33,17},{48,32},{49,33},{2,48}... | collective-permute-start | bytes 786440 | tf_op jit(solution)/shard_map/ppermute | solution.py:31
  27.4 11.6 %collective-permute-start.2 = (f32[16,128]{1,0:T(8,128)S(1)}, f32[16,128]{1,0:T(8,128)S(1)}, u32[]{:S(2)}, u32[]{:S(2)}) collective-permute-start(f32[16,128]{1,0:T(8,128)S(1)} %bitcast.49), channel_id=1, source_target_pairs={{0,2},{2,0},{1,3},{3,1},{4,6},{6,4},{5,7},{7,5},{8,10},{10,8},{9,1... | collective-permute-start | bytes 24584 | tf_op jit(solution)/shard_map/ppermute | solution.py:21
  40.9 1.3 copy-start
  42.2 33.6 %copy-start.2 = (f32[128,256]{1,0:T(8,128)S(1)}, f32[128,256]{1,0:T(8,128)}, u32[]{:S(2)}) copy-start(f32[128,256]{1,0:T(8,128)} %refs_7_.1) | copy-start | bytes 393220
  42.2 0.6 copy-start.5
  42.9 33.0 %all-to-all-start.1 = ((f32[32,15,8,128]{3,2,1,0:T(8,128)}), f32[32,15,8,128]{3,2,1,0:T(8,128)S(1)}, u32[]{:S(2)}, u32[]{:S(2)}) async-start(f32[32,15,8,128]{3,2,1,0:T(8,128)} %copy-done), calls=%async_computation.1 | async-start | bytes 3932160 | tf_op jit(solution)/shard_map/all_to_all | solution.py:35
  49.0 6.8 %collective-permute-start = (f32[4,128,128]{2,1,0:T(8,128)}, f32[4,128,128]{2,1,0:T(8,128)S(1)}, u32[]{:S(2)}, u32[]{:S(2)}) collective-permute-start(f32[4,128,128]{2,1,0:T(8,128)} %get-tuple-element.38), channel_id=1, source_target_pairs={{0,1},{1,0},{2,3},{3,2},{4,5},{5,4},{6,7},{7,6},{8,9},{9,8},{10,11... | collective-permute-start | bytes 786440 | tf_op jit(solution)/shard_map/ppermute | solution.py:204
  49.3 18.9 %collective-permute-start.8 = (f32[4,128,128]{2,1,0:T(8,128)}, f32[4,128,128]{2,1,0:T(8,128)S(1)}, u32[]{:S(2)}, u32[]{:S(2)}) collective-permute-start(f32[4,128,128]{2,1,0:T(8,128)} %get-tuple-element.24), channel_id=1, source_target_pairs={{0,3},{3,0},{1,2},{2,1},{4,7},{7,4},{5,6},{6,5},{8,11},{11,8},{9,1... | collective-permute-start | bytes 786440 | tf_op jit(solution)/shard_map/ppermute | solution.py:204
  52.4 15.7 %collective-permute-start.7 = (f32[3,128,128]{2,1,0:T(8,128)}, f32[3,128,128]{2,1,0:T(8,128)S(1)}, u32[]{:S(2)}, u32[]{:S(2)}) collective-permute-start(f32[3,128,128]{2,1,0:T(8,128)} %dynamic-slice_bitcast_fusion.3), channel_id=1, source_target_pairs={{0,2},{2,0},{1,3},{3,1},{4,6},{6,4},{5,7},{7,5},{8,10},{10,8},{9,1... | collective-permute-start | bytes 589832 | tf_op jit(solution)/shard_map/ppermute | solution.py:204
  75.9 0.8 copy-start.6
  79.5 0.7 copy-start.3
  116.3 13.7 %collective-permute-start.9 = (f32[67,8,128]{2,1,0:T(8,128)S(1)}, f32[67,8,128]{2,1,0:T(8,128)S(1)}, u32[]{:S(2)}, u32[]{:S(2)}) collective-permute-start(f32[67,8,128]{2,1,0:T(8,128)S(1)} %get-tuple-element.34), channel_id=1, source_target_pairs={{0,16},{1,17},{16,32},{17,33},{32,48},{33,49},{48,2},{49,3},{2,18}... | collective-permute-start | bytes 823304 | tf_op jit(solution)/shard_map/ppermute | solution.py:31
  123.2 11.9 %collective-permute-start.11 = (f32[67,8,128]{2,1,0:T(8,128)S(1)}, f32[67,8,128]{2,1,0:T(8,128)S(1)}, u32[]{:S(2)}, u32[]{:S(2)}) collective-permute-start(f32[67,8,128]{2,1,0:T(8,128)S(1)} %get-tuple-element.35), channel_id=1, source_target_pairs={{0,32},{1,35},{16,48},{17,51},{32,2},{33,1},{48,18},{49,17},{2,34}... | collective-permute-start | bytes 823304 | tf_op jit(solution)/shard_map/ppermute | solution.py:31
  123.2 12.8 %collective-permute-start.10 = (f32[67,8,128]{2,1,0:T(8,128)S(1)}, f32[67,8,128]{2,1,0:T(8,128)S(1)}, u32[]{:S(2)}, u32[]{:S(2)}) collective-permute-start(f32[67,8,128]{2,1,0:T(8,128)S(1)} %get-tuple-element.36), channel_id=1, source_target_pairs={{0,50},{1,51},{16,0},{17,1},{32,16},{33,17},{48,32},{49,33},{2,48}... | collective-permute-start | bytes 823304 | tf_op jit(solution)/shard_map/ppermute | solution.py:31
  136.2 25.2 %copy-start.4 = (f32[128,256]{1,0:T(8,128)S(1)}, f32[128,256]{1,0:T(8,128)}, u32[]{:S(2)}) copy-start(f32[128,256]{1,0:T(8,128)} %copy-done.3) | copy-start | bytes 393220
  136.3 9.3 %collective-permute-start.12 = (f32[35,8,128]{2,1,0:T(8,128)S(1)}, f32[35,8,128]{2,1,0:T(8,128)S(1)}, u32[]{:S(2)}, u32[]{:S(2)}) collective-permute-start(f32[35,8,128]{2,1,0:T(8,128)S(1)} %pad_maximum_fusion.3), channel_id=1, source_target_pairs={{0,2},{2,0},{1,3},{3,1},{4,6},{6,4},{5,7},{7,5},{8,10},{10,8},{9,1... | collective-permute-start | bytes 430088 | tf_op jit(solution)/shard_map/ppermute | solution.py:21
